TPU v7x, 1024 devices: a whole 4x8x16 slice. The times are simulated.
1024 devices in a mesh: exp: 64 (over y, x, core), attn: 16 (over z).
Axes of the slice: x: 4, y: 8, z: 16, core: 2. Of those that a mesh axis runs over, the one named last changes fastest.
Arguments:
- tokens: bfloat16 [8192, 2048], P('exp', 'attn'), may hold values from -6 to 6
- cotangent: bfloat16 [8192, 2048], P('exp', 'attn'), may hold values from -6 to 6
- expert_ids: int32 [8192, 2], P('exp'), may hold values from 0 to 63, all different within a row; in each aligned block of 128 rows (0 to 127, 128 to 255, ...) at most 6 rows name the same one
- route_weight: bfloat16 [8192, 2], P('exp'), may hold values from 0.099609375 to 1
- gate_weight: bfloat16 [64, 2048, 768], P('exp', 'attn'), may hold values from -0.125 to 0.125
- up_weight: bfloat16 [64, 2048, 768], P('exp', 'attn'), may hold values from -0.125 to 0.125
- down_weight: bfloat16 [64, 768, 2048], P('exp', None, 'attn'), may hold values from -0.21875 to 0.21875
Outputs:
- grad_tokens: bfloat16 [8192, 2048], P('exp', 'attn')
- grad_route: float32 [8192, 2], P('exp')
- grad_gate: float32 [64, 2048, 768], P('exp', 'attn')
- grad_up: float32 [64, 2048, 768], P('exp', 'attn')
- grad_down: float32 [64, 768, 2048], P('exp', None, 'attn')
Inputs may be any that keep to these rules, and one draw needn't show every extreme that they name: `expert_ids`: each row names 2 different experts. Within the 128 tokens of one index of exp (aligned blocks of rows), no expert is named by more than 6 choices, and in every draw some block names some expert exactly 6 times.
All inputs are finite; a program needn't handle non-finite values.
Results may differ from a plain program's by a relative error of at most 0.028.
Values may be sent and summed in bfloat16 or wider, within the bound.
No kernel may reach another device: no remote copies, remote signals or barrier semaphores. Data moves between devices by JAX's collectives and lax.ppermute only.
A program may use at most 32 MiB of HBM per device.

v0:
```python
import jax
import jax.numpy as jnp
from jax import lax
from jax.sharding import PartitionSpec as P


def swiglu_grads(summed, hidden):
    gate_part = summed[:, :hidden]
    up_part = summed[:, hidden : 2 * hidden]
    back_part = summed[:, 2 * hidden :]
    sigmoid_gate = jax.nn.sigmoid(gate_part)
    silu_gate = gate_part * sigmoid_gate
    activation = silu_gate * up_part
    grad_g = back_part * up_part * sigmoid_gate * (1.0 + gate_part * (1.0 - sigmoid_gate))
    grad_u = back_part * silu_gate
    return jnp.concatenate([activation, grad_g, grad_u], axis=1).astype(jnp.bfloat16)


def shards(tokens, cotangent, expert_ids, route_weight, gate_weight, up_weight, down_weight):
    tok_rows, width_share = tokens.shape
    per_token = expert_ids.shape[1]
    experts = lax.axis_size("exp")
    capacity = 3 * tok_rows * per_token // (2 * experts)
    hidden = gate_weight.shape[2]
    slot_total = experts * capacity
    routed = expert_ids.reshape(-1)
    one_hot = (routed[:, None] == jnp.arange(experts, dtype=jnp.int32)[None, :]).astype(jnp.int32)
    ranked = jnp.cumsum(one_hot, axis=0) - 1
    slot_pos = jnp.sum(ranked * one_hot, axis=1)
    target = routed * capacity + slot_pos
    feat_send = (
        jnp.zeros((slot_total, width_share), jnp.bfloat16)
        .at[target]
        .set(jnp.repeat(tokens, per_token, axis=0))
    )
    upstream_send = (
        jnp.zeros((slot_total, width_share), jnp.bfloat16)
        .at[target]
        .set(jnp.repeat(cotangent, per_token, axis=0))
    )
    weight_send = jnp.zeros((slot_total,), jnp.bfloat16).at[target].set(route_weight.reshape(-1))
    feat_recv, upstream_recv, weight_recv = (
        lax.all_to_all(
            feat_send.reshape(experts, capacity, width_share),
            "exp",
            split_axis=0,
            concat_axis=0,
            tiled=True,
        ),
        lax.all_to_all(
            upstream_send.reshape(experts, capacity, width_share),
            "exp",
            split_axis=0,
            concat_axis=0,
            tiled=True,
        ),
        lax.all_to_all(
            weight_send.reshape(experts, capacity), "exp", split_axis=0, concat_axis=0, tiled=True
        ),
    )
    feat_rows = feat_recv.reshape(slot_total, width_share)
    upstream_rows = upstream_recv.reshape(slot_total, width_share)
    weight_rows = weight_recv.reshape(slot_total)
    scaled_rows = (
        weight_rows[:, None].astype(jnp.float32) * upstream_rows.astype(jnp.float32)
    ).astype(jnp.bfloat16)
    joint_weight = jnp.concatenate([gate_weight[0], up_weight[0]], axis=1)
    down_share = down_weight[0]
    feat_block = feat_rows
    scaled_block = scaled_rows
    gate_up = jnp.dot(feat_block, joint_weight, preferred_element_type=jnp.float32)
    back_hidden = lax.dot_general(
        scaled_block, down_share, (((1,), (1,)), ((), ())), preferred_element_type=jnp.float32
    )
    summed = lax.psum(
        jnp.concatenate([gate_up, back_hidden], axis=1).astype(jnp.bfloat16), "attn"
    ).astype(jnp.float32)
    act_rows = swiglu_grads(summed, hidden)
    feat_block = feat_rows
    scaled_block = scaled_rows
    activation = act_rows[:, :hidden]
    grad_pair = act_rows[:, hidden:]
    grad_joint = lax.dot_general(
        feat_block, grad_pair, (((0,), (0,)), ((), ())), preferred_element_type=jnp.float32
    )
    grad_down_part = lax.dot_general(
        activation, scaled_block, (((0,), (0,)), ((), ())), preferred_element_type=jnp.float32
    )
    token_block = lax.dot_general(
        grad_pair, joint_weight, (((1,), (1,)), ((), ())), preferred_element_type=jnp.float32
    ).astype(jnp.bfloat16)
    out_block = jnp.dot(activation, down_share, preferred_element_type=jnp.float32)
    score_block = jnp.sum(upstream_rows.astype(jnp.float32) * out_block, axis=1).astype(
        jnp.bfloat16
    )
    totals = (grad_joint, grad_down_part, token_block, score_block)
    grad_joint, grad_down_share, token_rows, score_rows = totals
    token_back, score_back = (
        lax.all_to_all(
            token_rows.reshape(experts, capacity, width_share),
            "exp",
            split_axis=0,
            concat_axis=0,
            tiled=True,
        ),
        lax.all_to_all(
            score_rows.reshape(experts, capacity), "exp", split_axis=0, concat_axis=0, tiled=True
        ),
    )
    token_choice = token_back.reshape(slot_total, width_share)[target]
    grad_tokens = jnp.sum(
        token_choice.reshape(tok_rows, per_token, width_share).astype(jnp.float32), axis=1
    ).astype(jnp.bfloat16)
    score_choice = score_back.reshape(slot_total)[target].reshape(tok_rows, per_token)
    grad_route = lax.psum(score_choice.astype(jnp.float32), "attn")
    grad_gate = grad_joint[:, :hidden][None]
    grad_up = grad_joint[:, hidden:][None]
    return (grad_tokens, grad_route, grad_gate, grad_up, grad_down_share[None])


def solution(mesh):
    in_specs = (
        P("exp", "attn"),
        P("exp", "attn"),
        P("exp", None),
        P("exp", None),
        P("exp", "attn", None),
        P("exp", "attn", None),
        P("exp", None, "attn"),
    )
    out_specs = (
        P("exp", "attn"),
        P("exp", None),
        P("exp", "attn", None),
        P("exp", "attn", None),
        P("exp", None, "attn"),
    )
    return jax.shard_map(shards, mesh=mesh, in_specs=in_specs, out_specs=out_specs, check_vma=False)
```

profile of v0, /device:TPU:2, one launch (start us, length us, event | category | flops | bytes accessed | tf_op | source)
XLA Modules:
  0.0 315.6 jit_solution(9436918772450032873)
XLA Ops:
  7.2 0.8 copy.22
  8.3 0.7 broadcast_multiply_fusion
  10.1 0.8 copy.25
  11.2 2.2 scatter_custom_fusion.1
  13.3 0.8 all_to_all.25
  14.1 17.2 %all-to-all-start.1 = ((bf16[64,1,6]{2,1,0:T(2,128)(2,1)}), bf16[64,1,6]{2,1,0:T(2,128)(2,1)S(1)}, u32[]{:S(2)}, u32[]{:S(2)}) async-start(bf16[64,1,6]{2,1,0:T(2,128)(2,1)} %all_to_all.25), calls=%async_computation.1 | async-start | bytes 65536 | tf_op jit(solution)/shard_map/all_to_all | solution.py:57
  31.3 0.8 broadcast_in_dim.26
  32.1 1.2 scatter_custom_fusion.2
  33.3 0.7 reshape.139
  34.0 5.9 %all-to-all-done.1 = bf16[64,1,6]{2,1,0:T(2,128)(2,1)S(1)} async-done(((bf16[64,1,6]{2,1,0:T(2,128)(2,1)}), bf16[64,1,6]{2,1,0:T(2,128)(2,1)S(1)}, u32[]{:S(2)}, u32[]{:S(2)}) %all-to-all-start.1) | async-done | bytes 800 | tf_op jit(solution)/shard_map/all_to_all | solution.py:57
  39.9 5.5 %all-to-all-start.2 = ((bf16[64,6,128]{2,1,0:T(8,128)(2,1)}), bf16[64,6,128]{2,1,0:T(8,128)(2,1)S(1)}, u32[]{:S(2)}, u32[]{:S(2)}) async-start(bf16[64,6,128]{2,1,0:T(8,128)(2,1)} %reshape.139), calls=%async_computation.2 | async-start | bytes 262144 | tf_op jit(solution)/shard_map/all_to_all | solution.py:50
  45.5 1.2 scatter_custom_fusion
  46.8 0.7 reshape.135
  47.5 7.9 %all-to-all-done.2 = bf16[64,6,128]{2,1,0:T(8,128)(2,1)S(1)} async-done(((bf16[64,6,128]{2,1,0:T(8,128)(2,1)}), bf16[64,6,128]{2,1,0:T(8,128)(2,1)S(1)}, u32[]{:S(2)}, u32[]{:S(2)}) %all-to-all-start.2) | async-done | bytes 98336 | tf_op jit(solution)/shard_map/all_to_all | solution.py:50
  55.4 5.8 %all-to-all-start = ((bf16[64,6,128]{2,1,0:T(8,128)(2,1)}), bf16[64,6,128]{2,1,0:T(8,128)(2,1)S(1)}, u32[]{:S(2)}, u32[]{:S(2)}) async-start(bf16[64,6,128]{2,1,0:T(8,128)(2,1)} %reshape.135), calls=%async_computation | async-start | bytes 262144 | tf_op jit(solution)/shard_map/all_to_all | solution.py:43
  61.8 9.4 %all-to-all-done = bf16[64,6,128]{2,1,0:T(8,128)(2,1)S(1)} async-done(((bf16[64,6,128]{2,1,0:T(8,128)(2,1)}), bf16[64,6,128]{2,1,0:T(8,128)(2,1)S(1)}, u32[]{:S(2)}, u32[]{:S(2)}) %all-to-all-start) | async-done | bytes 98336 | tf_op jit(solution)/shard_map/all_to_all | solution.py:43
  71.7 1.3 pad_maximum_fusion
  73.5 145.2 %all-reduce.2.cloned.1.call-done = bf16[384,2304]{1,0:T(8,128)(2,1)} async-done(((bf16[384,2304]{1,0:T(8,128)(2,1)}), bf16[384,2304]{1,0:T(8,128)(2,1)}) %all-reduce.2.cloned.1.call-update) | async-done | bytes 1769488 | tf_op jit(solution)/shard_map/psum | solution.py:75
  218.7 1.7 convert_element_type.76
  220.4 0.7 multiply_convert_fusion
  221.4 0.8 convert_element_type.91
  222.2 10.3 %all-to-all-start.4 = ((bf16[64,1,6]{2,1,0:T(2,128)(2,1)}), bf16[64,1,6]{2,1,0:T(2,128)(2,1)S(1)}, u32[]{:S(2)}, u32[]{:S(2)}) async-start(bf16[64,1,6]{2,1,0:T(2,128)(2,1)} %convert_element_type.91), calls=%async_computation.4 | async-start | bytes 65536 | tf_op jit(solution)/shard_map/all_to_all | solution.py:106
  233.4 0.7 reshape.140
  234.0 7.0 %all-to-all-done.4 = bf16[64,1,6]{2,1,0:T(2,128)(2,1)S(1)} async-done(((bf16[64,1,6]{2,1,0:T(2,128)(2,1)}), bf16[64,1,6]{2,1,0:T(2,128)(2,1)S(1)}, u32[]{:S(2)}, u32[]{:S(2)}) %all-to-all-start.4) | async-done | bytes 800 | tf_op jit(solution)/shard_map/all_to_all | solution.py:106
  241.1 5.7 %all-to-all-start.3 = ((bf16[64,6,128]{2,1,0:T(8,128)(2,1)}), bf16[64,6,128]{2,1,0:T(8,128)(2,1)S(1)}, u32[]{:S(2)}, u32[]{:S(2)}) async-start(bf16[64,6,128]{2,1,0:T(8,128)(2,1)} %reshape.140), calls=%async_computation.3 | async-start | bytes 262144 | tf_op jit(solution)/shard_map/all_to_all | solution.py:99
  246.8 0.9 slice_bitcast_fusion
  247.7 1.2 convolution_bitcast_fusion
  249.1 1.9 gather_fusion.1
  251.2 55.2 %psum.15 = f32[128,2]{1,0:T(8,128)S(1)} all-reduce(f32[128,2]{1,0:T(8,128)S(1)} %reshape.146), channel_id=1, replica_groups=mesh['exp'=64,'attn'=16] {'attn'}, use_global_device_ids=true, to_apply=%region_9.10 | all-reduce | flops 256 | bytes 2048 | tf_op jit(solution)/shard_map/psum | solution.py:115
  306.4 0.6 copy.29
  307.1 0.9 gather_fusion
  307.9 0.8 reduce_sum.34
  (42 shorter events, 4.8 us)
Async XLA Ops:
  7.2 54.3 %copy-start = (bf16[1,768,128]{2,1,0:T(8,128)(2,1)S(1)}, bf16[1,768,128]{2,1,0:T(8,128)(2,1)}, u32[]{:S(2)}) copy-start(bf16[1,768,128]{2,1,0:T(8,128)(2,1)} %param.13) | copy-start | bytes 589828
  7.2 38.3 %copy-start.3 = (bf16[128,128]{1,0:T(8,128)(2,1)S(1)}, bf16[128,128]{1,0:T(8,128)(2,1)}, u32[]{:S(2)}) copy-start(bf16[128,128]{1,0:T(8,128)(2,1)} %param.7) | copy-start | bytes 98308
  14.1 25.8 %all-to-all-start.1 = ((bf16[64,1,6]{2,1,0:T(2,128)(2,1)}), bf16[64,1,6]{2,1,0:T(2,128)(2,1)S(1)}, u32[]{:S(2)}, u32[]{:S(2)}) async-start(bf16[64,1,6]{2,1,0:T(2,128)(2,1)} %all_to_all.25), calls=%async_computation.1 | async-start | bytes 65536 | tf_op jit(solution)/shard_map/all_to_all | solution.py:57
  39.9 15.5 %all-to-all-start.2 = ((bf16[64,6,128]{2,1,0:T(8,128)(2,1)}), bf16[64,6,128]{2,1,0:T(8,128)(2,1)S(1)}, u32[]{:S(2)}, u32[]{:S(2)}) async-start(bf16[64,6,128]{2,1,0:T(8,128)(2,1)} %reshape.139), calls=%async_computation.2 | async-start | bytes 262144 | tf_op jit(solution)/shard_map/all_to_all | solution.py:50
  45.5 25.8 %copy-start.1 = (bf16[1,128,768]{2,1,0:T(8,128)(2,1)S(1)}, bf16[1,128,768]{2,1,0:T(8,128)(2,1)}, u32[]{:S(2)}) copy-start(bf16[1,128,768]{2,1,0:T(8,128)(2,1)} %param.12) | copy-start | bytes 589828
  45.5 25.8 %copy-start.2 = (bf16[1,128,768]{2,1,0:T(8,128)(2,1)S(1)}, bf16[1,128,768]{2,1,0:T(8,128)(2,1)}, u32[]{:S(2)}) copy-start(bf16[1,128,768]{2,1,0:T(8,128)(2,1)} %param.11) | copy-start | bytes 589828
  55.4 15.8 %all-to-all-start = ((bf16[64,6,128]{2,1,0:T(8,128)(2,1)}), bf16[64,6,128]{2,1,0:T(8,128)(2,1)S(1)}, u32[]{:S(2)}, u32[]{:S(2)}) async-start(bf16[64,6,128]{2,1,0:T(8,128)(2,1)} %reshape.135), calls=%async_computation | async-start | bytes 262144 | tf_op jit(solution)/shard_map/all_to_all | solution.py:43
  61.3 157.4 %all-reduce.2.cloned.1.call-start = ((), (), s32[]{:S(2)}) async-start(), calls=%async_computation.5 | async-start | bytes 3538944 | tf_op jit(solution)/shard_map/psum | solution.py:75
  222.2 18.8 %all-to-all-start.4 = ((bf16[64,1,6]{2,1,0:T(2,128)(2,1)}), bf16[64,1,6]{2,1,0:T(2,128)(2,1)S(1)}, u32[]{:S(2)}, u32[]{:S(2)}) async-start(bf16[64,1,6]{2,1,0:T(2,128)(2,1)} %convert_element_type.91), calls=%async_computation.4 | async-start | bytes 65536 | tf_op jit(solution)/shard_map/all_to_all | solution.py:106
  241.1 66.0 %all-to-all-start.3 = ((bf16[64,6,128]{2,1,0:T(8,128)(2,1)}), bf16[64,6,128]{2,1,0:T(8,128)(2,1)S(1)}, u32[]{:S(2)}, u32[]{:S(2)}) async-start(bf16[64,6,128]{2,1,0:T(8,128)(2,1)} %reshape.140), calls=%async_computation.3 | async-start | bytes 262144 | tf_op jit(solution)/shard_map/all_to_all | solution.py:99
Sparse Core Ops, SparseCore 0:
  73.2 145.4 all-reduce.1
where the time goes:
time: 316 us
  waiting for transfers between devices  176 us (56%)
  blocking collectives  55.2 us (17%)
  starting transfers between devices  44.5 us (14%)
  local copies, waits for them, and re-layouts  16.6 us (5%)
  between operations  14.3 us (5%)
  other arithmetic  6.3 us (2%)
  matrix products  3.16 us (1%)
    psum x1, waiting for transfers between devices, shards(): lax.psum(jnp.concatenate([gate_up, back_hidden], axis=1).astype(jnp.bfloa...  145 us
    psum x1, blocking collectives, shards(): grad_route = lax.psum(score_choice.astype(jnp.float32), 'attn')  55.2 us
    all_to_all x1, starting transfers between devices, shards(): lax.all_to_all(weight_send.reshape(experts, capacity), 'exp', split_axis=...  17.2 us
    all_to_all x1, starting transfers between devices, shards(): lax.all_to_all(score_rows.reshape(experts, capacity), 'exp', split_axis=0...  10.3 us
    all_to_all x1, waiting for transfers between devices, shards(): lax.all_to_all(feat_send.reshape(experts, capacity, width_share), 'exp',...  9.4 us
    all_to_all x1, waiting for transfers between devices, shards(): lax.all_to_all(upstream_send.reshape(experts, capacity, width_share), 'ex...  7.94 us
    all_to_all x1, waiting for transfers between devices, shards(): lax.all_to_all(score_rows.reshape(experts, capacity), 'exp', split_axis=0...  7.01 us
  transfers between devices with their start and end apart: 6, of which 5 were waited for; matrix products, arithmetic and copies ran while one was open for 4% of the time, Pallas kernels for 0%

commit v1 on v0

v1 whole, which is shorter than its diff:
```python
import functools

import jax
import jax.numpy as jnp
from jax import lax
from jax.experimental import pallas as pl
from jax.experimental.pallas import tpu as pltpu
from jax.sharding import PartitionSpec as P

F32 = jnp.float32
BF16 = jnp.bfloat16
PAD = 8


def iota(shape, axis):
    return lax.broadcasted_iota(jnp.int32, shape, axis)


def one_hot(mask):
    return jnp.where(mask, 1.0, 0.0).astype(BF16)


def mm(a, b, ca, cb):
    return lax.dot_general(a, b, (((ca,), (cb,)), ((), ())), preferred_element_type=F32)


def pack_kernel(ids_ref, weight_ref, tok_ref, cot_ref, send_ref, rank_ref):
    top, tok = ids_ref.shape
    rows = send_ref.shape[0]
    width = tok_ref.shape[1]
    ids = ids_ref[...]
    weight = weight_ref[...].astype(F32)
    row, col = iota((tok, tok), 0), iota((tok, tok), 1)
    columns = [
        jnp.sum(jnp.where(row == col, ids[j : j + 1, :], 0), axis=1, keepdims=True)
        for j in range(top)
    ]
    ranks, hots, scaled = [], [], []
    slot = iota((rows, tok), 0)
    for j in range(top):
        same = [jnp.where((columns[i] == ids[j : j + 1, :]) & (row < col), 1, 0) for i in range(top)]
        rank = jnp.sum(functools.reduce(jnp.add, same), axis=0, keepdims=True)
        ranks.append(rank)
        hit = slot == ids[j : j + 1, :] * PAD + rank
        hots.append(jnp.where(hit, 1.0, 0.0))
        scaled.append(jnp.where(hit, weight[j : j + 1, :], 0.0))
    rank_ref[...] = jnp.concatenate(ranks, axis=0)
    plain = functools.reduce(jnp.add, hots).astype(BF16)
    heavy = functools.reduce(jnp.add, scaled).astype(BF16)
    send_ref[:, :width] = mm(plain, tok_ref[...], 1, 0).astype(BF16)
    send_ref[:, width:] = mm(heavy, cot_ref[...], 1, 0).astype(BF16)


def partial_kernel(cap, recv_ref, gate_ref, up_ref, down_ref, rows_ref, part_ref):
    step = pl.program_id(0)
    slots, padded = rows_ref.shape[0], recv_ref.shape[0]
    width = gate_ref.shape[0]

    @pl.when(step == 0)
    def _():
        s, r = iota((slots, padded), 0), iota((slots, padded), 1)
        keep = one_hot(((r >> 3) * cap + (r & 7) == s) & ((r & 7) < cap))
        rows_ref[...] = mm(keep, recv_ref[...], 1, 0).astype(BF16)
        part_ref[...] = mm(rows_ref[:, :width], gate_ref[...], 1, 0).astype(BF16)

    @pl.when(step == 1)
    def _():
        part_ref[...] = mm(rows_ref[:, :width], up_ref[...], 1, 0).astype(BF16)

    @pl.when(step == 2)
    def _():
        part_ref[...] = mm(rows_ref[:, width:], down_ref[...], 1, 1).astype(BF16)


def sum_kernel(parts, part_ref, out_ref):
    n = part_ref.shape[0] // parts
    total = part_ref[0:n, :].astype(F32)
    for i in range(1, parts):
        total = total + part_ref[i * n : (i + 1) * n, :].astype(F32)
    total = total.astype(BF16)
    for i in range(parts):
        out_ref[i * n : (i + 1) * n, :] = total


def grad_kernel(
    cap,
    rows_ref,
    gate_sum_ref,
    up_sum_ref,
    back_sum_ref,
    gate_ref,
    up_ref,
    down_ref,
    grad_gate_ref,
    grad_up_ref,
    grad_down_ref,
    send_ref,
    term_ref,
    score_ref,
):
    step = pl.program_id(0)
    slots = rows_ref.shape[0]
    width = gate_ref.shape[0]
    gate = gate_sum_ref[...].astype(F32)
    up = up_sum_ref[...].astype(F32)
    back = back_sum_ref[...].astype(F32)
    sig = jax.nn.sigmoid(gate)
    silu = gate * sig
    act_wide = silu * up
    act = act_wide.astype(BF16)
    grad_g = (back * up * sig * (1.0 + gate * (1.0 - sig))).astype(BF16)
    grad_u = (back * silu).astype(BF16)
    feat, scaled = rows_ref[:, :width], rows_ref[:, width:]
    grad_gate_ref[...] = mm(feat, grad_g, 0, 0)
    grad_up_ref[...] = mm(feat, grad_u, 0, 0)
    grad_down_ref[...] = mm(act, scaled, 0, 0)
    term = mm(grad_g, gate_ref[...], 1, 1) + mm(grad_u, up_ref[...], 1, 1)
    score = jnp.sum(act.astype(F32) * back, axis=1, keepdims=True)

    @pl.when(step == 0)
    def _():
        term_ref[...] = term
        score_ref[...] = jnp.broadcast_to(score, score_ref.shape)

    @pl.when(step > 0)
    def _():
        term_ref[...] += term
        score_ref[...] += jnp.broadcast_to(score, score_ref.shape)

    @pl.when(step == pl.num_programs(0) - 1)
    def _():
        padded = send_ref.shape[0]
        r, s = iota((padded, slots), 0), iota((padded, slots), 1)
        spread = one_hot(((r >> 3) * cap + (r & 7) == s) & ((r & 7) < cap))
        base = (r >> 3) * cap
        block = one_hot(((r & 7) == cap) & (s >= base) & (s < base + cap))
        s2, lane = iota((slots, width), 0), iota((slots, width), 1)
        own = jnp.where(lax.rem(s2, cap) == lane, score_ref[...], 0.0).astype(BF16)
        send_ref[...] = (
            mm(spread, term_ref[...].astype(BF16), 1, 0) + mm(block, own, 1, 0)
        ).astype(BF16)


def merge_kernel(cap, ids_ref, rank_ref, weight_ref, recv_ref, tok_ref, route_ref):
    top, tok = ids_ref.shape
    rows, width = recv_ref.shape
    recv = recv_ref[...]
    slot = iota((rows, tok), 0)
    sub = iota((width, tok), 0)
    hots, scores = [], []
    for j in range(top):
        ids, rank = ids_ref[j : j + 1, :], rank_ref[j : j + 1, :]
        hots.append(jnp.where(slot == ids * PAD + rank, 1.0, 0.0))
        line = mm(recv, one_hot(slot == ids * PAD + cap), 0, 0)
        scores.append(jnp.sum(jnp.where(sub == rank, line, 0.0), axis=0, keepdims=True))
    tok_ref[...] = mm(functools.reduce(jnp.add, hots).astype(BF16), recv, 0, 0).astype(BF16)
    route_ref[...] = jnp.concatenate(scores, axis=0) / weight_ref[...].astype(F32)


def full(shape):
    return pl.BlockSpec(shape, lambda k: (0,) * len(shape))


def exchange(rows, axis):
    n = lax.axis_size(axis)
    blocks = rows.reshape(n, rows.shape[0] // n, rows.shape[1])
    blocks = lax.all_to_all(blocks, axis, split_axis=0, concat_axis=0, tiled=True)
    return blocks.reshape(rows.shape)


def shards(tokens, cotangent, expert_ids, route_weight, gate_weight, up_weight, down_weight):
    tok, width = tokens.shape
    top = expert_ids.shape[1]
    experts, parts = lax.axis_size("exp"), lax.axis_size("attn")
    cap = 3 * tok * top // (2 * experts)
    hidden = gate_weight.shape[2]
    slots, padded = experts * cap, experts * PAD
    ids, weight = expert_ids.T, route_weight.T
    gate_w, up_w, down_w = gate_weight[0], up_weight[0], down_weight[0]

    send, rank = pl.pallas_call(
        pack_kernel,
        out_shape=(
            jax.ShapeDtypeStruct((padded, 2 * width), BF16),
            jax.ShapeDtypeStruct((top, tok), jnp.int32),
        ),
        name="pack",
    )(ids, weight, tokens, cotangent)
    recv = exchange(send, "exp")
    rows, part = pl.pallas_call(
        functools.partial(partial_kernel, cap),
        grid=(3,),
        out_shape=(
            jax.ShapeDtypeStruct((slots, 2 * width), BF16),
            jax.ShapeDtypeStruct((slots, 3 * hidden), BF16),
        ),
        in_specs=[
            full((padded, 2 * width)),
            full((width, hidden)),
            full((width, hidden)),
            full((hidden, width)),
        ],
        out_specs=(
            full((slots, 2 * width)),
            pl.BlockSpec((slots, hidden), lambda k: (0, k)),
        ),
        name="partial",
    )(recv, gate_w, up_w, down_w)
    summed = pl.pallas_call(
        functools.partial(sum_kernel, parts),
        out_shape=jax.ShapeDtypeStruct((slots, 3 * hidden), BF16),
        name="sums",
    )(exchange(part, "attn"))
    summed = exchange(summed, "attn")
    n = 3
    piece = hidden // n
    grad_gate, grad_up, grad_down, back = pl.pallas_call(
        functools.partial(grad_kernel, cap),
        grid=(n,),
        out_shape=(
            jax.ShapeDtypeStruct((width, hidden), F32),
            jax.ShapeDtypeStruct((width, hidden), F32),
            jax.ShapeDtypeStruct((hidden, width), F32),
            jax.ShapeDtypeStruct((padded, width), BF16),
        ),
        in_specs=[
            full((slots, 2 * width)),
            pl.BlockSpec((slots, piece), lambda k: (0, k)),
            pl.BlockSpec((slots, piece), lambda k: (0, n + k)),
            pl.BlockSpec((slots, piece), lambda k: (0, 2 * n + k)),
            pl.BlockSpec((width, piece), lambda k: (0, k)),
            pl.BlockSpec((width, piece), lambda k: (0, k)),
            pl.BlockSpec((piece, width), lambda k: (k, 0)),
        ],
        out_specs=(
            pl.BlockSpec((width, piece), lambda k: (0, k)),
            pl.BlockSpec((width, piece), lambda k: (0, k)),
            pl.BlockSpec((piece, width), lambda k: (k, 0)),
            full((padded, width)),
        ),
        scratch_shapes=[pltpu.VMEM((slots, width), F32), pltpu.VMEM((slots, width), F32)],
        name="grads",
    )(rows, summed, summed, summed, gate_w, up_w, down_w)
    grad_tokens, grad_route = pl.pallas_call(
        functools.partial(merge_kernel, cap),
        out_shape=(
            jax.ShapeDtypeStruct((tok, width), BF16),
            jax.ShapeDtypeStruct((top, tok), F32),
        ),
        name="merge",
    )(ids, rank, weight, exchange(back, "exp"))
    return grad_tokens, grad_route.T, grad_gate[None], grad_up[None], grad_down[None]


def solution(mesh):
    in_specs = (
        P("exp", "attn"),
        P("exp", "attn"),
        P("exp", None),
        P("exp", None),
        P("exp", "attn", None),
        P("exp", "attn", None),
        P("exp", None, "attn"),
    )
    out_specs = (
        P("exp", "attn"),
        P("exp", None),
        P("exp", "attn", None),
        P("exp", "attn", None),
        P("exp", None, "attn"),
    )
    return jax.shard_map(shards, mesh=mesh, in_specs=in_specs, out_specs=out_specs, check_vma=False)
```

time: 316 us -> 250 us (0.79)
  the two profiles are of different devices: /device:TPU:2 before, /device:TPU:1 now
where the time goes in v1:
time: 250 us
  blocking collectives  233 us (93%)
  Pallas kernels  15.9 us (6%)
    all_to_all x4, blocking collectives, exchange(): lax.all_to_all(blocks, axis, split_axis=0, concat_axis=0, tiled=True)  233 us
    pallas_call x1, Pallas kernels, shards(): pl.pallas_call(functools.partial(grad_kernel, cap), grid=(n,), out_shape=...  5.21 us

profile of v1, /device:TPU:1, one launch (start us, length us, event | category | flops | bytes accessed | tf_op | source)
XLA Modules:
  0.0 249.7 jit_solution(4068403369049827611)
XLA Ops:
  0.6 1.9 pack.1
  2.5 32.1 %all_to_all.20 = bf16[64,8,256]{2,1,0:T(8,128)(2,1)} all-to-all(bf16[64,8,256]{2,1,0:T(8,128)(2,1)} %bitcast.31), channel_id=1, replica_groups=mesh['exp'=64,'attn'=16] {'exp'}, dimensions={0} | all-to-all | bytes 524288 | tf_op jit(solution)/shard_map/all_to_all | solution.py:167
  34.6 4.0 %partial.1 = (bf16[384,256]{1,0:T(8,128)(2,1)}, bf16[384,2304]{1,0:T(8,128)(2,1)}) custom-call(bf16[512,256]{1,0:T(8,128)(2,1)} %bitcast.23, bf16[128,768]{1,0:T(8,128)(2,1)} %bitcast.24, bf16[128,768]{1,0:T(8,128)(2,1)} %bitcast.26, bf16[768,128]{1,0:T(8,128)(2,1)} %bitcast.28), custom_call_target="tpu_custom_call" | custom-call | tf_op jit(solution)/shard_map/partial/pallas_call | solution.py:190
  38.6 91.3 %all_to_all.21 = bf16[16,24,2304]{2,1,0:T(8,128)(2,1)} all-to-all(bf16[16,24,2304]{2,1,0:T(8,128)(2,1)} %bitcast.22), channel_id=1, replica_groups=mesh['exp'=64,'attn'=16] {'attn'}, dimensions={0} | all-to-all | bytes 3538944 | tf_op jit(solution)/shard_map/all_to_all | solution.py:167
  129.9 2.9 %sums.1 = bf16[384,2304]{1,0:T(8,128)(2,1)} custom-call(bf16[384,2304]{1,0:T(8,128)(2,1)} %bitcast.20), custom_call_target="tpu_custom_call" | custom-call | tf_op jit(solution)/shard_map/sums/pallas_call | solution.py:209
  132.9 88.5 %all_to_all.22 = bf16[16,24,2304]{2,1,0:T(8,128)(2,1)} all-to-all(bf16[16,24,2304]{2,1,0:T(8,128)(2,1)} %bitcast.21), channel_id=1, replica_groups=mesh['exp'=64,'attn'=16] {'attn'}, dimensions={0} | all-to-all | bytes 3538944 | tf_op jit(solution)/shard_map/all_to_all | solution.py:167
  221.3 5.2 %grads.1 = (f32[128,768]{1,0:T(8,128)}, f32[128,768]{1,0:T(8,128)}, f32[768,128]{1,0:T(8,128)}, bf16[512,128]{1,0:T(8,128)(2,1)}) custom-call(bf16[384,256]{1,0:T(8,128)(2,1)} %get-tuple-element.17.rows_ref, bf16[384,2304]{1,0:T(8,128)(2,1)} %bitcast.17, bf16[384,2304]{1,0:T(8,128)(2,1)} %bitcast.18, bf16[384,2304]{1,0:T(8,128)(2,1)} %bitcast.19, ...), custom_call_target="tpu_custom_call" | custom-call | tf_op jit(solution)/shard_map/grads/pallas_call | solution.py:217
  226.6 21.2 %all_to_all.23 = bf16[64,8,128]{2,1,0:T(8,128)(2,1)} all-to-all(bf16[64,8,128]{2,1,0:T(8,128)(2,1)} %bitcast.32), channel_id=1, replica_groups=mesh['exp'=64,'attn'=16] {'exp'}, dimensions={0} | all-to-all | bytes 262144 | tf_op jit(solution)/shard_map/all_to_all | solution.py:167
  247.8 1.9 merge.1

commit v2 on v1

v2 whole, which is shorter than its diff:
```python
import functools
import math

import jax
import jax.numpy as jnp
from jax import lax
from jax.experimental import pallas as pl
from jax.sharding import PartitionSpec as P

F32 = jnp.float32
BF16 = jnp.bfloat16
PAD = 8


def iota(shape, axis):
    return lax.broadcasted_iota(jnp.int32, shape, axis)


def one_hot(mask):
    return jnp.where(mask, 1.0, 0.0).astype(BF16)


def mm(a, b, ca, cb):
    return lax.dot_general(a, b, (((ca,), (cb,)), ((), ())), preferred_element_type=F32)


def pack_kernel(ids_ref, weight_ref, tok_ref, cot_ref, send_ref, rank_ref):
    top, tok = ids_ref.shape
    rows = send_ref.shape[0]
    width = tok_ref.shape[1]
    ids = ids_ref[...]
    weight = weight_ref[...].astype(F32)
    row, col = iota((tok, tok), 0), iota((tok, tok), 1)
    columns = [
        jnp.sum(jnp.where(row == col, ids[j : j + 1, :], 0), axis=1, keepdims=True)
        for j in range(top)
    ]
    ranks, hots, scaled = [], [], []
    slot = iota((rows, tok), 0)
    for j in range(top):
        same = [jnp.where((columns[i] == ids[j : j + 1, :]) & (row < col), 1, 0) for i in range(top)]
        rank = jnp.sum(functools.reduce(jnp.add, same), axis=0, keepdims=True)
        ranks.append(rank)
        hit = slot == ids[j : j + 1, :] * PAD + rank
        hots.append(jnp.where(hit, 1.0, 0.0))
        scaled.append(jnp.where(hit, weight[j : j + 1, :], 0.0))
    rank_ref[...] = jnp.concatenate(ranks, axis=0)
    plain = functools.reduce(jnp.add, hots).astype(BF16)
    heavy = functools.reduce(jnp.add, scaled).astype(BF16)
    send_ref[:, :width] = mm(plain, tok_ref[...], 1, 0).astype(BF16)
    send_ref[:, width:] = mm(heavy, cot_ref[...], 1, 0).astype(BF16)


def spread_kernel(cap, local, recv_ref, gate_ref, up_ref, down_ref, out_ref):
    padded = recv_ref.shape[0]
    width, hidden = gate_ref.shape
    slots = padded // PAD * cap
    piece = hidden // local
    block = out_ref.shape[0] // local
    s, r = iota((slots, padded), 0), iota((slots, padded), 1)
    keep = one_hot(((r >> 3) * cap + (r & 7) == s) & ((r & 7) < cap))
    rows = mm(keep, recv_ref[...], 1, 0).astype(BF16)
    eye = one_hot(iota((width, width), 0) == iota((width, width), 1))
    turned = [mm(ref[...], eye, 0, 0).astype(BF16) for ref in (gate_ref, up_ref)]
    for p in range(local):
        at = p * block
        out_ref[at : at + slots, :] = rows[:, :width]
        out_ref[at + slots : at + 2 * slots, :] = rows[:, width:]
        at += 2 * slots
        for m in range(2):
            out_ref[at : at + piece, :] = turned[m][p * piece : (p + 1) * piece, :]
            at += piece
        out_ref[at : at + piece, :] = down_ref[p * piece : (p + 1) * piece, :]


def partial_kernel(slots, local, strided, held_ref, part_ref):
    block = held_ref.shape[0] // local
    piece = (block - 2 * slots) // 3
    chunk = piece // strided
    for m in range(3):
        total = None
        for f in range(local):
            at = f * block
            rows = held_ref[at : at + slots, :] if m < 2 else held_ref[at + slots : at + 2 * slots, :]
            at += 2 * slots + m * piece
            term = mm(held_ref[at : at + piece, :], rows, 1, 1)
            total = term if total is None else total + term
        total = total.astype(BF16)
        for q in range(strided):
            to = (q * 3 + m) * chunk
            part_ref[to : to + chunk, :] = total[q * chunk : (q + 1) * chunk, :]


def act_kernel(strided, part_ref, out_ref):
    n = part_ref.shape[0] // strided
    chunk = n // 3
    total = part_ref[0:n, :].astype(F32)
    for q in range(1, strided):
        total = total + part_ref[q * n : (q + 1) * n, :].astype(F32)
    gate, up, back = (total[m * chunk : (m + 1) * chunk, :] for m in range(3))
    sig = jax.nn.sigmoid(gate)
    silu = gate * sig
    act = (silu * up).astype(BF16)
    grad_g = (back * up * sig * (1.0 + gate * (1.0 - sig))).astype(BF16)
    grad_u = (back * silu).astype(BF16)
    score = jnp.sum(act.astype(F32) * back, axis=0, keepdims=True)
    score = jnp.where(iota((PAD, score.shape[1]), 0) == 0, score, 0.0).astype(BF16)
    m = out_ref.shape[0] // strided
    for q in range(strided):
        at = q * m
        out_ref[at : at + chunk, :] = act
        out_ref[at + chunk : at + 2 * chunk, :] = grad_g
        out_ref[at + 2 * chunk : at + n, :] = grad_u
        out_ref[at + n : at + m, :] = score


def grad_kernel(local, strided, held_ref, acts_ref, out_ref):
    slots = acts_ref.shape[1]
    width = held_ref.shape[1]
    block = held_ref.shape[0] // local
    piece = (block - 2 * slots) // 3
    m = acts_ref.shape[0] // strided
    chunk = (m - PAD) // 3
    act, grad_g, grad_u = (
        jnp.concatenate(
            [acts_ref[q * m + k * chunk : q * m + (k + 1) * chunk, :] for q in range(strided)], axis=0
        )
        for k in range(3)
    )
    score = acts_ref[3 * chunk : 3 * chunk + PAD, :].astype(F32)
    for q in range(1, strided):
        score = score + acts_ref[q * m + 3 * chunk : (q + 1) * m, :].astype(F32)
    lines = slots // width
    score = jnp.concatenate(
        [score[0:1, k * width : (k + 1) * width] for k in range(lines)]
        + [jnp.zeros((PAD - lines, width), F32)],
        axis=0,
    ).astype(BF16)
    out = out_ref.shape[0] // local
    for f in range(local):
        at = f * block
        feat, scaled = held_ref[at : at + slots, :], held_ref[at + slots : at + 2 * slots, :]
        at += 2 * slots
        gate_w, up_w = held_ref[at : at + piece, :], held_ref[at + piece : at + 2 * piece, :]
        to = f * out
        out_ref[to : to + slots, :] = (mm(grad_g, gate_w, 0, 0) + mm(grad_u, up_w, 0, 0)).astype(BF16)
        out_ref[to + slots : to + slots + PAD, :] = score
        to += slots + PAD
        out_ref[to : to + piece, :] = mm(grad_g, feat, 1, 0).astype(BF16)
        out_ref[to + piece : to + 2 * piece, :] = mm(grad_u, feat, 1, 0).astype(BF16)
        out_ref[to + 2 * piece : to + 3 * piece, :] = mm(act, scaled, 1, 0).astype(BF16)


def back_kernel(cap, slots, local, got_ref, send_ref):
    padded, width = send_ref.shape
    block = got_ref.shape[0] // local
    term = got_ref[0 : slots + PAD, :].astype(F32)
    for f in range(1, local):
        term = term + got_ref[f * block : f * block + slots + PAD, :].astype(F32)
    lines = slots // width
    score = jnp.concatenate([term[slots + k : slots + k + 1, :] for k in range(lines)], axis=1)
    term = term[:slots, :].astype(BF16)
    r, s = iota((padded, slots), 0), iota((padded, slots), 1)
    spread = one_hot(((r >> 3) * cap + (r & 7) == s) & ((r & 7) < cap))
    base = (r >> 3) * cap
    mine = ((r & 7) == cap) & (s >= base) & (s < base + cap)
    scores = jnp.where(mine, score, 0.0).astype(BF16)
    lane = one_hot(lax.rem(iota((slots, width), 0), cap) == iota((slots, width), 1))
    send_ref[...] = (mm(spread, term, 1, 0) + mm(scores, lane, 1, 0)).astype(BF16)


def out_kernel(skip, local, got_ref, grad_gate_ref, grad_up_ref, grad_down_ref):
    block = got_ref.shape[0] // local
    width = got_ref.shape[1]
    piece = (block - skip) // 3
    eye = one_hot(iota((width, width), 0) == iota((width, width), 1))
    gate, up, down = (
        jnp.concatenate(
            [got_ref[f * block + skip + m * piece : f * block + skip + (m + 1) * piece, :] for f in range(local)],
            axis=0,
        )
        for m in range(3)
    )
    grad_gate_ref[...] = mm(eye, gate, 1, 1)
    grad_up_ref[...] = mm(eye, up, 1, 1)
    grad_down_ref[...] = down.astype(F32)


def merge_kernel(cap, ids_ref, rank_ref, weight_ref, recv_ref, tok_ref, route_ref):
    top, tok = ids_ref.shape
    rows, width = recv_ref.shape
    recv = recv_ref[...]
    slot = iota((rows, tok), 0)
    sub = iota((width, tok), 0)
    hots, scores = [], []
    for j in range(top):
        ids, rank = ids_ref[j : j + 1, :], rank_ref[j : j + 1, :]
        hots.append(jnp.where(slot == ids * PAD + rank, 1.0, 0.0))
        line = mm(recv, one_hot(slot == ids * PAD + cap), 0, 0)
        scores.append(jnp.sum(jnp.where(sub == rank, line, 0.0), axis=0, keepdims=True))
    tok_ref[...] = mm(functools.reduce(jnp.add, hots).astype(BF16), recv, 0, 0).astype(BF16)
    route_ref[...] = jnp.concatenate(scores, axis=0) / weight_ref[...].astype(F32)


def exchange(rows, axis, groups=None):
    n = lax.axis_size(axis) if groups is None else len(groups[0])
    blocks = rows.reshape(n, rows.shape[0] // n, rows.shape[1])
    blocks = lax.all_to_all(
        blocks, axis, split_axis=0, concat_axis=0, tiled=True, axis_index_groups=groups
    )
    return blocks.reshape(rows.shape)


def shape_of(*dims, dtype=BF16):
    return jax.ShapeDtypeStruct(dims, dtype)


def shards(tokens, cotangent, expert_ids, route_weight, gate_weight, up_weight, down_weight):
    tok, width = tokens.shape
    top = expert_ids.shape[1]
    experts, parts = lax.axis_size("exp"), lax.axis_size("attn")
    cap = 3 * tok * top // (2 * experts)
    hidden = gate_weight.shape[2]
    slots, padded = experts * cap, experts * PAD
    local = math.isqrt(parts)
    strided = parts // local
    piece = hidden // local
    near = [[q * local + r for r in range(local)] for q in range(strided)]
    far = [[q * local + r for q in range(strided)] for r in range(local)]
    ids, weight = expert_ids.T, route_weight.T
    gate_w, up_w, down_w = gate_weight[0], up_weight[0], down_weight[0]

    send, rank = pl.pallas_call(
        pack_kernel,
        out_shape=(shape_of(padded, 2 * width), shape_of(top, tok, dtype=jnp.int32)),
        name="pack",
    )(ids, weight, tokens, cotangent)
    recv = exchange(send, "exp")
    held = pl.pallas_call(
        functools.partial(spread_kernel, cap, local),
        out_shape=shape_of(local * (2 * slots + 3 * piece), width),
        name="spread",
    )(recv, gate_w, up_w, down_w)
    held = exchange(held, "attn", near)
    part = pl.pallas_call(
        functools.partial(partial_kernel, slots, local, strided),
        out_shape=shape_of(3 * piece, slots),
        name="partial",
    )(held)
    part = exchange(part, "attn", far)
    acts = pl.pallas_call(
        functools.partial(act_kernel, strided),
        out_shape=shape_of(3 * piece + strided * PAD, slots),
        name="acts",
    )(part)
    acts = exchange(acts, "attn", far)
    got = pl.pallas_call(
        functools.partial(grad_kernel, local, strided),
        out_shape=shape_of(local * (slots + PAD + 3 * piece), width),
        name="grads",
    )(held, acts)
    got = exchange(got, "attn", near)
    back = pl.pallas_call(
        functools.partial(back_kernel, cap, slots, local),
        out_shape=shape_of(padded, width),
        name="back",
    )(got)
    back = exchange(back, "exp")
    grad_gate, grad_up, grad_down = pl.pallas_call(
        functools.partial(out_kernel, slots + PAD, local),
        out_shape=(
            shape_of(width, hidden, dtype=F32),
            shape_of(width, hidden, dtype=F32),
            shape_of(hidden, width, dtype=F32),
        ),
        name="out",
    )(got)
    grad_tokens, grad_route = pl.pallas_call(
        functools.partial(merge_kernel, cap),
        out_shape=(shape_of(tok, width), shape_of(top, tok, dtype=F32)),
        name="merge",
    )(ids, rank, weight, back)
    return grad_tokens, grad_route.T, grad_gate[None], grad_up[None], grad_down[None]


def solution(mesh):
    in_specs = (
        P("exp", "attn"),
        P("exp", "attn"),
        P("exp", None),
        P("exp", None),
        P("exp", "attn", None),
        P("exp", "attn", None),
        P("exp", None, "attn"),
    )
    out_specs = (
        P("exp", "attn"),
        P("exp", None),
        P("exp", "attn", None),
        P("exp", "attn", None),
        P("exp", None, "attn"),
    )
    return jax.shard_map(shards, mesh=mesh, in_specs=in_specs, out_specs=out_specs, check_vma=False)
```

time: 250 us -> 205 us (0.82)
  blocking collectives: 233 us -> 167 us
  waiting for transfers between devices: 0 us -> 8.65 us
  starting transfers between devices: 0 us -> 7.59 us
  Pallas kernels: 15.9 us -> 19.4 us
    all_to_all x4 -> x5, blocking collectives: 233 us -> 167 us  [exchange(): lax.all_to_all(blocks, axis, split_axis=0, concat_axis=0, tiled=True, axi...]
    all_to_all x0 -> x1, waiting for transfers between devices: none -> 8.65 us  [exchange(): lax.all_to_all(blocks, axis, split_axis=0, concat_axis=0, tiled=True, axi...]
    all_to_all x0 -> x1, starting transfers between devices: none -> 7.59 us  [exchange(): lax.all_to_all(blocks, axis, split_axis=0, concat_axis=0, tiled=True, axi...]
    pallas_call x5 -> x8, Pallas kernels: 15.9 us -> 19.4 us  [the longest x1 3.44 us: shards(): pl.pallas_call(functools.partial(grad_kernel, local, strided), out_shape=...]
  transfers between devices with their start and end apart: 0 -> 1, of which waited for: 0 -> 1; matrix products, arithmetic and copies ran while one was open for 0% -> 0% of each run, Pallas kernels for 0% -> 1%
where the time goes in v2:
time: 205 us; the launch traced here: 204 us
  blocking collectives  167 us (81%)
  Pallas kernels  19.4 us (9%)
  waiting for transfers between devices  8.65 us (4%)
  starting transfers between devices  7.59 us (4%)
    all_to_all x5, blocking collectives, exchange(): lax.all_to_all(blocks, axis, split_axis=0, concat_axis=0, tiled=True, axi...  167 us
    all_to_all x1, waiting for transfers between devices, exchange(): lax.all_to_all(blocks, axis, split_axis=0, concat_axis=0, tiled=True, axi...  8.65 us
    all_to_all x1, starting transfers between devices, exchange(): lax.all_to_all(blocks, axis, split_axis=0, concat_axis=0, tiled=True, axi...  7.59 us
  transfers between devices with their start and end apart: 1, of which 1 were waited for; matrix products, arithmetic and copies ran while one was open for 0% of the time, Pallas kernels for 1%

profile of v2, /device:TPU:1, one launch (start us, length us, event | category | flops | bytes accessed | tf_op | source)
XLA Modules:
  0.0 203.7 jit_solution(7739558086078349538)
XLA Ops:
  0.6 1.9 pack.1
  2.5 32.1 %all_to_all.30 = bf16[64,8,256]{2,1,0:T(8,128)(2,1)} all-to-all(bf16[64,8,256]{2,1,0:T(8,128)(2,1)} %bitcast.34), channel_id=1, replica_groups=mesh['exp'=64,'attn'=16] {'exp'}, dimensions={0} | all-to-all | bytes 524288 | tf_op jit(solution)/shard_map/all_to_all | solution.py:208
  34.6 2.7 %spread.1 = bf16[5376,128]{1,0:T(8,128)(2,1)} custom-call(bf16[512,256]{1,0:T(8,128)(2,1)} %bitcast.31, bf16[128,768]{1,0:T(8,128)(2,1)} %bitcast.35, bf16[128,768]{1,0:T(8,128)(2,1)} %bitcast.36, bf16[768,128]{1,0:T(8,128)(2,1)} %bitcast.37), custom_call_target="tpu_custom_call" | custom-call | tf_op jit(solution)/shard_map/spread/pallas_call | solution.py:239
  37.3 36.7 %all_to_all.31 = bf16[4,1344,128]{2,1,0:T(8,128)(2,1)} all-to-all(bf16[4,1344,128]{2,1,0:T(8,128)(2,1)} %bitcast.25), channel_id=1, replica_groups={{0,1,2,3},{4,5,6,7},{8,9,10,11},{12,13,14,15},{16,17,18,19},{20,21,22,2..., dimensions={0} | all-to-all | bytes 2752512 | tf_op jit(solution)/shard_map/all_to_all | solution.py:208
  73.9 2.8 %partial.1 = bf16[576,384]{1,0:T(8,128)(2,1)} custom-call(bf16[5376,128]{1,0:T(8,128)(2,1)} %bitcast.21), custom_call_target="tpu_custom_call" | custom-call | tf_op jit(solution)/shard_map/partial/pallas_call | solution.py:245
  76.7 34.9 %all_to_all.32 = bf16[4,144,384]{2,1,0:T(8,128)(2,1)} all-to-all(bf16[4,144,384]{2,1,0:T(8,128)(2,1)} %bitcast.29), channel_id=1, replica_groups={{0,4,8,12},{1,5,9,13},{2,6,10,14},{3,7,11,15},{16,20,24,28},{17,21,25,2..., dimensions={0} | all-to-all | bytes 884736 | tf_op jit(solution)/shard_map/all_to_all | solution.py:208
  111.6 1.9 acts.1
  113.5 32.5 %all_to_all.33 = bf16[4,152,384]{2,1,0:T(8,128)(2,1)} all-to-all(bf16[4,152,384]{2,1,0:T(8,128)(2,1)} %bitcast.27), channel_id=1, replica_groups={{0,4,8,12},{1,5,9,13},{2,6,10,14},{3,7,11,15},{16,20,24,28},{17,21,25,2..., dimensions={0} | all-to-all | bytes 933888 | tf_op jit(solution)/shard_map/all_to_all | solution.py:208
  145.9 3.4 %grads.1 = bf16[3872,128]{1,0:T(8,128)(2,1)} custom-call(bf16[5376,128]{1,0:T(8,128)(2,1)} %bitcast.22, bf16[608,384]{1,0:T(8,128)(2,1)} %bitcast.28), custom_call_target="tpu_custom_call" | custom-call | tf_op jit(solution)/shard_map/grads/pallas_call | solution.py:257
  149.4 30.7 %all_to_all.34 = bf16[4,968,128]{2,1,0:T(8,128)(2,1)} all-to-all(bf16[4,968,128]{2,1,0:T(8,128)(2,1)} %bitcast.26), channel_id=1, replica_groups={{0,1,2,3},{4,5,6,7},{8,9,10,11},{12,13,14,15},{16,17,18,19},{20,21,22,2..., dimensions={0} | all-to-all | bytes 1982464 | tf_op jit(solution)/shard_map/all_to_all | solution.py:208
  180.1 2.4 %back.1 = bf16[512,128]{1,0:T(8,128)(2,1)} custom-call(bf16[3872,128]{1,0:T(8,128)(2,1)} %bitcast.23), custom_call_target="tpu_custom_call" | custom-call | tf_op jit(solution)/shard_map/back/pallas_call | solution.py:263
  182.5 7.6 %all-to-all-start.5 = ((bf16[64,8,128]{2,1,0:T(8,128)(2,1)}), bf16[64,8,128]{2,1,0:T(8,128)(2,1)S(1)}, u32[]{:S(2)}, u32[]{:S(2)}) async-start(bf16[64,8,128]{2,1,0:T(8,128)(2,1)} %bitcast.32), calls=%async_computation.5 | async-start | bytes 262144 | tf_op jit(solution)/shard_map/all_to_all | solution.py:208
  190.1 2.4 %out.1 = (f32[128,768]{1,0:T(8,128)}, f32[128,768]{1,0:T(8,128)}, f32[768,128]{1,0:T(8,128)}) custom-call(bf16[3872,128]{1,0:T(8,128)(2,1)} %bitcast.24), custom_call_target="tpu_custom_call" | custom-call | tf_op jit(solution)/shard_map/out/pallas_call | solution.py:269
  192.5 8.7 %all-to-all-done.5 = bf16[64,8,128]{2,1,0:T(8,128)(2,1)S(1)} async-done(((bf16[64,8,128]{2,1,0:T(8,128)(2,1)}), bf16[64,8,128]{2,1,0:T(8,128)(2,1)S(1)}, u32[]{:S(2)}, u32[]{:S(2)}) %all-to-all-start.5) | async-done | bytes 131104 | tf_op jit(solution)/shard_map/all_to_all | solution.py:208
  201.2 0.0 copy-start
  201.2 0.6 copy-done
  201.8 1.9 merge.1
Async XLA Ops:
  182.5 18.7 %all-to-all-start.5 = ((bf16[64,8,128]{2,1,0:T(8,128)(2,1)}), bf16[64,8,128]{2,1,0:T(8,128)(2,1)S(1)}, u32[]{:S(2)}, u32[]{:S(2)}) async-start(bf16[64,8,128]{2,1,0:T(8,128)(2,1)} %bitcast.32), calls=%async_computation.5 | async-start | bytes 262144 | tf_op jit(solution)/shard_map/all_to_all | solution.py:208
  201.2 0.6 copy-start

commit v3 on v2

--- a/solution.py
+++ b/solution.py
@@ -5,10 +5,12 @@
 import jax.numpy as jnp
 from jax import lax
 from jax.experimental import pallas as pl
+from jax.experimental.pallas import tpu as pltpu
 from jax.sharding import PartitionSpec as P
 
 F32 = jnp.float32
 BF16 = jnp.bfloat16
+VMEM = 67043328
 PAD = 8
 
 
@@ -24,7 +26,8 @@
     return lax.dot_general(a, b, (((ca,), (cb,)), ((), ())), preferred_element_type=F32)
 
 
-def pack_kernel(ids_ref, weight_ref, tok_ref, cot_ref, send_ref, rank_ref):
+def pack_kernel(ready, ids_ref, weight_ref, tok_ref, cot_ref, send_ref, rank_ref):
+    ready()
     top, tok = ids_ref.shape
     rows = send_ref.shape[0]
     width = tok_ref.shape[1]
@@ -51,7 +54,7 @@
     send_ref[:, width:] = mm(heavy, cot_ref[...], 1, 0).astype(BF16)
 
 
-def spread_kernel(cap, local, recv_ref, gate_ref, up_ref, down_ref, out_ref):
+def spread_kernel(cap, local, ready, recv_ref, gate_ref, up_ref, down_ref, out_ref):
     padded = recv_ref.shape[0]
     width, hidden = gate_ref.shape
     slots = padded // PAD * cap
@@ -61,6 +64,7 @@
     keep = one_hot(((r >> 3) * cap + (r & 7) == s) & ((r & 7) < cap))
     rows = mm(keep, recv_ref[...], 1, 0).astype(BF16)
     eye = one_hot(iota((width, width), 0) == iota((width, width), 1))
+    ready()
     turned = [mm(ref[...], eye, 0, 0).astype(BF16) for ref in (gate_ref, up_ref)]
     for p in range(local):
         at = p * block
@@ -204,11 +208,57 @@
 
 def exchange(rows, axis, groups=None):
     n = lax.axis_size(axis) if groups is None else len(groups[0])
+    axis = axis if groups is None else ("exp", "attn")
     blocks = rows.reshape(n, rows.shape[0] // n, rows.shape[1])
     blocks = lax.all_to_all(
         blocks, axis, split_axis=0, concat_axis=0, tiled=True, axis_index_groups=groups
     )
     return blocks.reshape(rows.shape)
+
+
+def device_groups(experts, parts, local):
+    strided, near, far = parts // local, [], []
+    for e in range(experts):
+        shift = e % 2 * (local // 2)
+        place = [
+            [
+                e * parts + (q * local + (r ^ (local // 2 if 2 * q >= strided else 0)) + shift) % parts
+                for r in range(local)
+            ]
+            for q in range(strided)
+        ]
+        near += place
+        far += [list(column) for column in zip(*place)]
+    return near, far
+
+
+def call(kernel, room=48 * 2**20, **options):
+    params = pltpu.CompilerParams(vmem_limit_bytes=VMEM - room)
+    return pl.pallas_call(kernel, compiler_params=params, **options)
+
+
+def call_fetching(kernel, plain, fetched, **options):
+    def body(*refs):
+        n, m = len(plain), len(fetched)
+        sources, held, sem = refs[n : n + m], refs[-1 - m : -1], refs[-1]
+        copies = [pltpu.make_async_copy(sources[i], held[i], sem.at[i]) for i in range(m)]
+        for copy in copies:
+            copy.start()
+
+        def ready():
+            for copy in copies:
+                copy.wait()
+
+        kernel(ready, *refs[:n], *held, *refs[n + m : -1 - m])
+
+    return call(
+        body,
+        in_specs=[pl.BlockSpec(memory_space=pltpu.VMEM)] * len(plain)
+        + [pl.BlockSpec(memory_space=pltpu.HBM)] * len(fetched),
+        scratch_shapes=[pltpu.VMEM(x.shape, x.dtype) for x in fetched]
+        + [pltpu.SemaphoreType.DMA((len(fetched),))],
+        **options,
+    )(*plain, *fetched)
 
 
 def shape_of(*dims, dtype=BF16):
@@ -225,48 +275,53 @@
     local = math.isqrt(parts)
     strided = parts // local
     piece = hidden // local
-    near = [[q * local + r for r in range(local)] for q in range(strided)]
-    far = [[q * local + r for q in range(strided)] for r in range(local)]
+    near, far = device_groups(experts, parts, local)
     ids, weight = expert_ids.T, route_weight.T
     gate_w, up_w, down_w = gate_weight[0], up_weight[0], down_weight[0]
 
-    send, rank = pl.pallas_call(
+    send, rank = call_fetching(
         pack_kernel,
+        (),
+        (ids, weight, tokens, cotangent),
         out_shape=(shape_of(padded, 2 * width), shape_of(top, tok, dtype=jnp.int32)),
         name="pack",
-    )(ids, weight, tokens, cotangent)
+        room=0,
+    )
     recv = exchange(send, "exp")
-    held = pl.pallas_call(
+    held = call_fetching(
         functools.partial(spread_kernel, cap, local),
+        (recv,),
+        (gate_w, up_w, down_w),
         out_shape=shape_of(local * (2 * slots + 3 * piece), width),
         name="spread",
-    )(recv, gate_w, up_w, down_w)
+        room=2 * local * (2 * slots + 3 * piece) * width + 2 * padded * 2 * width + 2**16,
+    )
     held = exchange(held, "attn", near)
-    part = pl.pallas_call(
+    part = call(
         functools.partial(partial_kernel, slots, local, strided),
         out_shape=shape_of(3 * piece, slots),
         name="partial",
     )(held)
     part = exchange(part, "attn", far)
-    acts = pl.pallas_call(
+    acts = call(
         functools.partial(act_kernel, strided),
         out_shape=shape_of(3 * piece + strided * PAD, slots),
         name="acts",
     )(part)
     acts = exchange(acts, "attn", far)
-    got = pl.pallas_call(
+    got = call(
         functools.partial(grad_kernel, local, strided),
         out_shape=shape_of(local * (slots + PAD + 3 * piece), width),
         name="grads",
     )(held, acts)
     got = exchange(got, "attn", near)
-    back = pl.pallas_call(
+    back = call(
         functools.partial(back_kernel, cap, slots, local),
         out_shape=shape_of(padded, width),
         name="back",
     )(got)
     back = exchange(back, "exp")
-    grad_gate, grad_up, grad_down = pl.pallas_call(
+    grad_gate, grad_up, grad_down = call(
         functools.partial(out_kernel, slots + PAD, local),
         out_shape=(
             shape_of(width, hidden, dtype=F32),
@@ -275,7 +330,7 @@
         ),
         name="out",
     )(got)
-    grad_tokens, grad_route = pl.pallas_call(
+    grad_tokens, grad_route = call(
         functools.partial(merge_kernel, cap),
         out_shape=(shape_of(tok, width), shape_of(top, tok, dtype=F32)),
         name="merge",

time: 205 us -> 172 us (0.84)
  blocking collectives: 167 us -> 144 us
  Pallas kernels: 19.4 us -> 10.7 us
    all_to_all x5, blocking collectives: 167 us -> 144 us  [exchange(): lax.all_to_all(blocks, axis, split_axis=0, concat_axis=0, tiled=True, axi...]
    pallas_call x8, Pallas kernels: 19.4 us -> 10.7 us  [the longest x2 5.51 us: call_fetching(): call(body, in_specs=[pl.BlockSpec(memory_space=pltpu.VMEM)] * len(plain)...]
where the time goes in v3:
time: 172 us; the launch traced here: 171 us
  blocking collectives  144 us (84%)
  Pallas kernels  10.7 us (6%)
  waiting for transfers between devices  9.85 us (6%)
  starting transfers between devices  5.99 us (3%)
    all_to_all x5, blocking collectives, exchange(): lax.all_to_all(blocks, axis, split_axis=0, concat_axis=0, tiled=True, axi...  144 us
    all_to_all x1, waiting for transfers between devices, exchange(): lax.all_to_all(blocks, axis, split_axis=0, concat_axis=0, tiled=True, axi...  9.85 us
    all_to_all x1, starting transfers between devices, exchange(): lax.all_to_all(blocks, axis, split_axis=0, concat_axis=0, tiled=True, axi...  5.99 us
    pallas_call x2, Pallas kernels, call_fetching(): call(body, in_specs=[pl.BlockSpec(memory_space=pltpu.VMEM)] * len(plain)...  5.51 us
  transfers between devices with their start and end apart: 1, of which 1 were waited for; matrix products, arithmetic and copies ran while one was open for 0% of the time, Pallas kernels for 1%

profile of v3, /device:TPU:1, one launch (start us, length us, event | category | flops | bytes accessed | tf_op | source)
XLA Modules:
  0.0 171.0 jit_solution(12674805640553271353)
XLA Ops:
  0.6 1.9 %pack.1 = (bf16[512,256]{1,0:T(8,128)(2,1)}, s32[2,128]{1,0:T(2,128)}) custom-call(s32[2,128]{1,0:T(2,128)} %bitcast.31, bf16[2,128]{1,0:T(2,128)(2,1)} %bitcast.33, bf16[128,128]{1,0:T(8,128)(2,1)} %refs_2_.1, bf16[128,128]{1,0:T(8,128)(2,1)} %refs_3_.1), custom_call_target="tpu_custom_call" | custom-call | tf_op jit(solution)/shard_map/pack/pallas_call | solution.py:254
  2.6 32.1 %all_to_all.30 = bf16[64,8,256]{2,1,0:T(8,128)(2,1)} all-to-all(bf16[64,8,256]{2,1,0:T(8,128)(2,1)} %bitcast.37), channel_id=1, replica_groups=mesh['exp'=64,'attn'=16] {'exp'}, dimensions={0} | all-to-all | bytes 524288 | tf_op jit(solution)/shard_map/all_to_all | solution.py:213
  34.6 3.6 %spread.1 = bf16[5376,128]{1,0:T(8,128)(2,1)} custom-call(bf16[512,256]{1,0:T(8,128)(2,1)} %bitcast.36, bf16[128,768]{1,0:T(8,128)(2,1)} %bitcast.38, bf16[128,768]{1,0:T(8,128)(2,1)} %bitcast.39, bf16[768,128]{1,0:T(8,128)(2,1)} %bitcast.40), custom_call_target="tpu_custom_call" | custom-call | tf_op jit(solution)/shard_map/spread/pallas_call | solution.py:254
  38.2 36.0 %all_to_all.31 = bf16[4,1344,128]{2,1,0:T(8,128)(2,1)S(1)} all-to-all(bf16[4,1344,128]{2,1,0:T(8,128)(2,1)} %bitcast.35), channel_id=1, replica_groups={{0,1,2,3},{4,5,6,7},{10,11,8,9},{14,15,12,13},{18,19,20,21},{22,23,24,2..., dimensions={0} | all-to-all | bytes 2752512 | tf_op jit(solution)/shard_map/all_to_all | solution.py:213
  74.2 0.7 partial.1
  74.9 24.6 %all_to_all.32 = bf16[4,144,384]{2,1,0:T(8,128)(2,1)S(1)} all-to-all(bf16[4,144,384]{2,1,0:T(8,128)(2,1)S(1)} %bitcast.28), channel_id=1, replica_groups={{0,4,10,14},{1,5,11,15},{2,6,8,12},{3,7,9,13},{18,22,28,16},{19,23,29,1..., dimensions={0} | all-to-all | bytes 884736 | tf_op jit(solution)/shard_map/all_to_all | solution.py:213
  99.5 0.1 acts.1
  99.6 15.3 %all_to_all.33 = bf16[4,152,384]{2,1,0:T(8,128)(2,1)S(1)} all-to-all(bf16[4,152,384]{2,1,0:T(8,128)(2,1)S(1)} %bitcast.26), channel_id=1, replica_groups={{0,4,10,14},{1,5,11,15},{2,6,8,12},{3,7,9,13},{18,22,28,16},{19,23,29,1..., dimensions={0} | all-to-all | bytes 933888 | tf_op jit(solution)/shard_map/all_to_all | solution.py:213
  114.9 1.1 grads.1
  116.0 35.7 %all_to_all.34 = bf16[4,968,128]{2,1,0:T(8,128)(2,1)S(1)} all-to-all(bf16[4,968,128]{2,1,0:T(8,128)(2,1)S(1)} %bitcast.25), channel_id=1, replica_groups={{0,1,2,3},{4,5,6,7},{10,11,8,9},{14,15,12,13},{18,19,20,21},{22,23,24,2..., dimensions={0} | all-to-all | bytes 1982464 | tf_op jit(solution)/shard_map/all_to_all | solution.py:213
  151.7 0.0 copy-start
  151.7 0.0 copy-start.1
  151.7 0.0 copy-start.2
  151.7 1.2 back.1
  152.9 6.0 %all-to-all-start.5 = ((bf16[64,8,128]{2,1,0:T(8,128)(2,1)}), bf16[64,8,128]{2,1,0:T(8,128)(2,1)S(1)}, u32[]{:S(2)}, u32[]{:S(2)}) async-start(bf16[64,8,128]{2,1,0:T(8,128)(2,1)} %bitcast.15), calls=%async_computation.5 | async-start | bytes 262144 | tf_op jit(solution)/shard_map/all_to_all | solution.py:213
  158.9 1.2 out.1
  160.1 9.9 %all-to-all-done.5 = bf16[64,8,128]{2,1,0:T(8,128)(2,1)S(1)} async-done(((bf16[64,8,128]{2,1,0:T(8,128)(2,1)}), bf16[64,8,128]{2,1,0:T(8,128)(2,1)S(1)}, u32[]{:S(2)}, u32[]{:S(2)}) %all-to-all-start.5) | async-done | bytes 131104 | tf_op jit(solution)/shard_map/all_to_all | solution.py:213
  170.0 0.0 copy-done
  170.0 0.0 copy-done.1
  170.0 0.0 copy-done.2
  170.0 0.9 merge.1
Async XLA Ops:
  151.7 18.3 %copy-start = (s32[128,2]{0,1:T(2,128)S(1)}, s32[128,2]{0,1:T(2,128)}, u32[]{:S(2)}) copy-start(s32[128,2]{0,1:T(2,128)} %param.9) | copy-start | bytes 3076
  151.7 18.3 %copy-start.1 = (bf16[128,2]{0,1:T(2,128)(2,1)S(1)}, bf16[128,2]{0,1:T(2,128)(2,1)}, u32[]{:S(2)}) copy-start(bf16[128,2]{0,1:T(2,128)(2,1)} %param.10) | copy-start | bytes 1540
  151.7 18.3 %copy-start.2 = (s32[2,128]{1,0:T(2,128)S(1)}, s32[2,128]{1,0:T(2,128)}, u32[]{:S(2)}) copy-start(s32[2,128]{1,0:T(2,128)} %get-tuple-element.12.rank_ref) | copy-start | bytes 3076
  152.9 17.1 %all-to-all-start.5 = ((bf16[64,8,128]{2,1,0:T(8,128)(2,1)}), bf16[64,8,128]{2,1,0:T(8,128)(2,1)S(1)}, u32[]{:S(2)}, u32[]{:S(2)}) async-start(bf16[64,8,128]{2,1,0:T(8,128)(2,1)} %bitcast.15), calls=%async_computation.5 | async-start | bytes 262144 | tf_op jit(solution)/shard_map/all_to_all | solution.py:213

commit v4 on v3

--- a/solution.py
+++ b/solution.py
@@ -7,6 +7,7 @@
 from jax.experimental import pallas as pl
 from jax.experimental.pallas import tpu as pltpu
 from jax.sharding import PartitionSpec as P
+
 
 F32 = jnp.float32
 BF16 = jnp.bfloat16
@@ -54,40 +55,49 @@
     send_ref[:, width:] = mm(heavy, cot_ref[...], 1, 0).astype(BF16)
 
 
-def spread_kernel(cap, local, ready, recv_ref, gate_ref, up_ref, down_ref, out_ref):
+def turn_kernel(local, ready, near_ref, gate_ref, up_ref, down_ref, *chunk_refs):
+    *chunk_refs, held_ref = chunk_refs
+    width, hidden = gate_ref.shape
+    piece = hidden // local
+    eye = one_hot(iota((width, width), 0) == iota((width, width), 1))
+    ready()
+    for m, ref in enumerate((gate_ref, up_ref)):
+        held_ref[m * hidden : (m + 1) * hidden, :] = mm(ref[...], eye, 0, 0).astype(BF16)
+    held_ref[2 * hidden : 3 * hidden, :] = down_ref[...]
+    for k, chunk_ref in enumerate(chunk_refs):
+        peer = near_ref[0] ^ k
+        for m in range(3):
+            at = pl.multiple_of(m * hidden + peer * piece, piece)
+            chunk_ref[m * piece : (m + 1) * piece, :] = held_ref[pl.ds(at, piece), :]
+
+
+def spread_kernel(cap, local, recv_ref, out_ref):
     padded = recv_ref.shape[0]
-    width, hidden = gate_ref.shape
+    width = out_ref.shape[1]
     slots = padded // PAD * cap
-    piece = hidden // local
-    block = out_ref.shape[0] // local
     s, r = iota((slots, padded), 0), iota((slots, padded), 1)
     keep = one_hot(((r >> 3) * cap + (r & 7) == s) & ((r & 7) < cap))
     rows = mm(keep, recv_ref[...], 1, 0).astype(BF16)
-    eye = one_hot(iota((width, width), 0) == iota((width, width), 1))
-    ready()
-    turned = [mm(ref[...], eye, 0, 0).astype(BF16) for ref in (gate_ref, up_ref)]
     for p in range(local):
-        at = p * block
+        at = p * 2 * slots
         out_ref[at : at + slots, :] = rows[:, :width]
         out_ref[at + slots : at + 2 * slots, :] = rows[:, width:]
-        at += 2 * slots
-        for m in range(2):
-            out_ref[at : at + piece, :] = turned[m][p * piece : (p + 1) * piece, :]
-            at += piece
-        out_ref[at : at + piece, :] = down_ref[p * piece : (p + 1) * piece, :]
-
-
-def partial_kernel(slots, local, strided, held_ref, part_ref):
-    block = held_ref.shape[0] // local
-    piece = (block - 2 * slots) // 3
+
+
+def rows_of(held_ref, near_ref, k, slots, scaled):
+    at = pl.multiple_of((near_ref[0] ^ k) * (2 * slots) + slots * scaled, 16)
+    return held_ref[pl.ds(at, slots), :]
+
+
+def partial_kernel(slots, strided, near_ref, held_ref, *refs):
+    *weight_refs, part_ref = refs
+    piece = weight_refs[0].shape[0] // 3
     chunk = piece // strided
     for m in range(3):
         total = None
-        for f in range(local):
-            at = f * block
-            rows = held_ref[at : at + slots, :] if m < 2 else held_ref[at + slots : at + 2 * slots, :]
-            at += 2 * slots + m * piece
-            term = mm(held_ref[at : at + piece, :], rows, 1, 1)
+        for k, weight_ref in enumerate(weight_refs):
+            rows = rows_of(held_ref, near_ref, k, slots, m // 2)
+            term = mm(weight_ref[m * piece : (m + 1) * piece, :], rows, 1, 1)
             total = term if total is None else total + term
         total = total.astype(BF16)
         for q in range(strided):
@@ -118,41 +128,50 @@
         out_ref[at + n : at + m, :] = score
 
 
-def grad_kernel(local, strided, held_ref, acts_ref, out_ref):
-    slots = acts_ref.shape[1]
-    width = held_ref.shape[1]
-    block = held_ref.shape[0] // local
-    piece = (block - 2 * slots) // 3
+def acts_of(acts_ref, strided):
     m = acts_ref.shape[0] // strided
     chunk = (m - PAD) // 3
-    act, grad_g, grad_u = (
+    return [
         jnp.concatenate(
             [acts_ref[q * m + k * chunk : q * m + (k + 1) * chunk, :] for q in range(strided)], axis=0
         )
         for k in range(3)
-    )
-    score = acts_ref[3 * chunk : 3 * chunk + PAD, :].astype(F32)
+    ]
+
+
+def term_kernel(strided, near_ref, acts_ref, *refs):
+    *weight_refs, out_ref = refs
+    slots = acts_ref.shape[1]
+    width = out_ref.shape[1]
+    piece = weight_refs[0].shape[0] // 3
+    m = acts_ref.shape[0] // strided
+    _, grad_g, grad_u = acts_of(acts_ref, strided)
+    score = acts_ref[m - PAD : m, :].astype(F32)
     for q in range(1, strided):
-        score = score + acts_ref[q * m + 3 * chunk : (q + 1) * m, :].astype(F32)
+        score = score + acts_ref[(q + 1) * m - PAD : (q + 1) * m, :].astype(F32)
     lines = slots // width
     score = jnp.concatenate(
         [score[0:1, k * width : (k + 1) * width] for k in range(lines)]
         + [jnp.zeros((PAD - lines, width), F32)],
         axis=0,
     ).astype(BF16)
-    out = out_ref.shape[0] // local
-    for f in range(local):
-        at = f * block
-        feat, scaled = held_ref[at : at + slots, :], held_ref[at + slots : at + 2 * slots, :]
-        at += 2 * slots
-        gate_w, up_w = held_ref[at : at + piece, :], held_ref[at + piece : at + 2 * piece, :]
-        to = f * out
-        out_ref[to : to + slots, :] = (mm(grad_g, gate_w, 0, 0) + mm(grad_u, up_w, 0, 0)).astype(BF16)
-        out_ref[to + slots : to + slots + PAD, :] = score
-        to += slots + PAD
-        out_ref[to : to + piece, :] = mm(grad_g, feat, 1, 0).astype(BF16)
-        out_ref[to + piece : to + 2 * piece, :] = mm(grad_u, feat, 1, 0).astype(BF16)
-        out_ref[to + 2 * piece : to + 3 * piece, :] = mm(act, scaled, 1, 0).astype(BF16)
+    for k, weight_ref in enumerate(weight_refs):
+        gate_w, up_w = weight_ref[0:piece, :], weight_ref[piece : 2 * piece, :]
+        to = pl.multiple_of((near_ref[0] ^ k) * (slots + PAD), PAD)
+        out_ref[pl.ds(to, slots), :] = (mm(grad_g, gate_w, 0, 0) + mm(grad_u, up_w, 0, 0)).astype(BF16)
+        out_ref[pl.ds(to + slots, PAD), :] = score
+
+
+def grad_kernel(strided, near_ref, held_ref, acts_ref, back_ref, *out_refs):
+    slots = acts_ref.shape[1]
+    piece = out_refs[0].shape[0] // 3
+    act, grad_g, grad_u = acts_of(acts_ref, strided)
+    for k, out_ref in enumerate(out_refs):
+        feat = rows_of(held_ref, near_ref, k, slots, 0)
+        scaled = rows_of(held_ref, near_ref, k, slots, 1)
+        out_ref[0:piece, :] = mm(grad_g, feat, 1, 0).astype(BF16)
+        out_ref[piece : 2 * piece, :] = mm(grad_u, feat, 1, 0).astype(BF16)
+        out_ref[2 * piece : 3 * piece, :] = mm(act, scaled, 1, 0).astype(BF16)
 
 
 def back_kernel(cap, slots, local, got_ref, send_ref):
@@ -173,21 +192,18 @@
     send_ref[...] = (mm(spread, term, 1, 0) + mm(scores, lane, 1, 0)).astype(BF16)
 
 
-def out_kernel(skip, local, got_ref, grad_gate_ref, grad_up_ref, grad_down_ref):
-    block = got_ref.shape[0] // local
-    width = got_ref.shape[1]
-    piece = (block - skip) // 3
+def out_kernel(near_ref, *refs):
+    *got_refs, grad_gate_ref, grad_up_ref, grad_down_ref, held_ref = refs
+    piece, width = got_refs[0].shape[0] // 3, got_refs[0].shape[1]
+    hidden = piece * len(got_refs)
+    for k, got_ref in enumerate(got_refs):
+        for m in range(3):
+            at = pl.multiple_of(m * hidden + (near_ref[0] ^ k) * piece, piece)
+            held_ref[pl.ds(at, piece), :] = got_ref[m * piece : (m + 1) * piece, :]
     eye = one_hot(iota((width, width), 0) == iota((width, width), 1))
-    gate, up, down = (
-        jnp.concatenate(
-            [got_ref[f * block + skip + m * piece : f * block + skip + (m + 1) * piece, :] for f in range(local)],
-            axis=0,
-        )
-        for m in range(3)
-    )
-    grad_gate_ref[...] = mm(eye, gate, 1, 1)
-    grad_up_ref[...] = mm(eye, up, 1, 1)
-    grad_down_ref[...] = down.astype(F32)
+    grad_gate_ref[...] = mm(eye, held_ref[0:hidden, :], 1, 1)
+    grad_up_ref[...] = mm(eye, held_ref[hidden : 2 * hidden, :], 1, 1)
+    grad_down_ref[...] = held_ref[2 * hidden :, :].astype(F32)
 
 
 def merge_kernel(cap, ids_ref, rank_ref, weight_ref, recv_ref, tok_ref, route_ref):
@@ -232,15 +248,31 @@
     return near, far
 
 
-def call(kernel, room=48 * 2**20, **options):
+def near_number(parts, local):
+    strided = parts // local
+    at = (lax.axis_index("attn") + parts - lax.axis_index("exp") % 2 * (local // 2)) % parts
+    return at % local ^ jnp.where(2 * (at // local) >= strided, local // 2, 0)
+
+
+def swap(chunks, near):
+    out = [chunks[0]]
+    for k in range(1, len(chunks)):
+        pairs = [(group[r], group[r ^ k]) for group in near for r in range(len(group))]
+        out.append(lax.ppermute(chunks[k], ("exp", "attn"), pairs))
+    return out
+
+
+def call(kernel, operands, room=48 * 2**20, **options):
     params = pltpu.CompilerParams(vmem_limit_bytes=VMEM - room)
-    return pl.pallas_call(kernel, compiler_params=params, **options)
-
-
-def call_fetching(kernel, plain, fetched, **options):
+    specs = [pl.BlockSpec(memory_space=pltpu.SMEM if x.shape == (1,) else pltpu.VMEM) for x in operands]
+    return pl.pallas_call(kernel, in_specs=specs, compiler_params=params, **options)(*operands)
+
+
+def call_fetching(kernel, plain, fetched, scratch=(), **options):
     def body(*refs):
         n, m = len(plain), len(fetched)
-        sources, held, sem = refs[n : n + m], refs[-1 - m : -1], refs[-1]
+        sources, sem = refs[n : n + m], refs[-1]
+        held = refs[len(refs) - 1 - m : -1]
         copies = [pltpu.make_async_copy(sources[i], held[i], sem.at[i]) for i in range(m)]
         for copy in copies:
             copy.start()
@@ -249,14 +281,16 @@
             for copy in copies:
                 copy.wait()
 
-        kernel(ready, *refs[:n], *held, *refs[n + m : -1 - m])
-
-    return call(
+        kernel(ready, *refs[:n], *held, *refs[n + m : len(refs) - 1 - m])
+
+    space = [pltpu.SMEM if x.shape == (1,) else pltpu.VMEM for x in plain] + [pltpu.HBM] * len(fetched)
+    return pl.pallas_call(
         body,
-        in_specs=[pl.BlockSpec(memory_space=pltpu.VMEM)] * len(plain)
-        + [pl.BlockSpec(memory_space=pltpu.HBM)] * len(fetched),
-        scratch_shapes=[pltpu.VMEM(x.shape, x.dtype) for x in fetched]
+        in_specs=[pl.BlockSpec(memory_space=x) for x in space],
+        scratch_shapes=list(scratch)
+        + [pltpu.VMEM(x.shape, x.dtype) for x in fetched]
         + [pltpu.SemaphoreType.DMA((len(fetched),))],
+        compiler_params=pltpu.CompilerParams(vmem_limit_bytes=VMEM),
         **options,
     )(*plain, *fetched)
 
@@ -276,6 +310,7 @@
     strided = parts // local
     piece = hidden // local
     near, far = device_groups(experts, parts, local)
+    me = near_number(parts, local).reshape(1)
     ids, weight = expert_ids.T, route_weight.T
     gate_w, up_w, down_w = gate_weight[0], up_weight[0], down_weight[0]
 
@@ -285,56 +320,74 @@
         (ids, weight, tokens, cotangent),
         out_shape=(shape_of(padded, 2 * width), shape_of(top, tok, dtype=jnp.int32)),
         name="pack",
-        room=0,
     )
     recv = exchange(send, "exp")
-    held = call_fetching(
+    chunks = call_fetching(
+        functools.partial(turn_kernel, local),
+        (me,),
+        (gate_w, up_w, down_w),
+        scratch=[pltpu.VMEM((3 * hidden, width), BF16)],
+        out_shape=(shape_of(3 * piece, width),) * local,
+        name="turn",
+    )
+    chunks = swap(chunks, near)
+    held = call(
         functools.partial(spread_kernel, cap, local),
         (recv,),
-        (gate_w, up_w, down_w),
-        out_shape=shape_of(local * (2 * slots + 3 * piece), width),
+        out_shape=shape_of(local * 2 * slots, width),
         name="spread",
-        room=2 * local * (2 * slots + 3 * piece) * width + 2 * padded * 2 * width + 2**16,
     )
     held = exchange(held, "attn", near)
     part = call(
-        functools.partial(partial_kernel, slots, local, strided),
+        functools.partial(partial_kernel, slots, strided),
+        (me, held, *chunks),
         out_shape=shape_of(3 * piece, slots),
         name="partial",
-    )(held)
+    )
     part = exchange(part, "attn", far)
     acts = call(
         functools.partial(act_kernel, strided),
+        (part,),
         out_shape=shape_of(3 * piece + strided * PAD, slots),
         name="acts",
-    )(part)
+    )
     acts = exchange(acts, "attn", far)
-    got = call(
-        functools.partial(grad_kernel, local, strided),
-        out_shape=shape_of(local * (slots + PAD + 3 * piece), width),
-        name="grads",
-    )(held, acts)
-    got = exchange(got, "attn", near)
+    terms = call(
+        functools.partial(term_kernel, strided),
+        (me, acts, *chunks),
+        out_shape=shape_of(local * (slots + PAD), width),
+        name="terms",
+    )
     back = call(
         functools.partial(back_kernel, cap, slots, local),
+        (exchange(terms, "attn", near),),
         out_shape=shape_of(padded, width),
         name="back",
-    )(got)
-    back = exchange(back, "exp")
+    )
+    got = call(
+        functools.partial(grad_kernel, strided),
+        (me, held, acts, back),
+        out_shape=(shape_of(3 * piece, width),) * local,
+        name="grads",
+    )
+    got = swap(got, near)
     grad_gate, grad_up, grad_down = call(
-        functools.partial(out_kernel, slots + PAD, local),
+        out_kernel,
+        (me, *got),
         out_shape=(
             shape_of(width, hidden, dtype=F32),
             shape_of(width, hidden, dtype=F32),
             shape_of(hidden, width, dtype=F32),
         ),
+        scratch_shapes=[pltpu.VMEM((3 * hidden, width), BF16)],
         name="out",
-    )(got)
+    )
     grad_tokens, grad_route = call(
         functools.partial(merge_kernel, cap),
+        (ids, rank, weight, exchange(back, "exp")),
         out_shape=(shape_of(tok, width), shape_of(top, tok, dtype=F32)),
         name="merge",
-    )(ids, rank, weight, back)
+    )
     return grad_tokens, grad_route.T, grad_gate[None], grad_up[None], grad_down[None]
 
 

time: 172 us -> 171 us (level)
  blocking collectives: 144 us -> 102 us
  starting transfers between devices: 5.99 us -> 35.8 us
  waiting for transfers between devices: 9.85 us -> 16.9 us
  Pallas kernels: 10.7 us -> 13.1 us
    all_to_all x5 -> x4, blocking collectives: 144 us -> 102 us  [exchange(): lax.all_to_all(blocks, axis, split_axis=0, concat_axis=0, tiled=True, axi...]
    ppermute x0 -> x6, starting transfers between devices: none -> 19.5 us  [swap(): out.append(lax.ppermute(chunks[k], ('exp', 'attn'), pairs))]
    ppermute x0 -> x6, waiting for transfers between devices: none -> 16.9 us  [swap(): out.append(lax.ppermute(chunks[k], ('exp', 'attn'), pairs))]
    all_to_all x1 -> x2, starting transfers between devices: 5.99 us -> 16.3 us  [exchange(): lax.all_to_all(blocks, axis, split_axis=0, concat_axis=0, tiled=True, axi...]
    all_to_all x1 -> x2, waiting for transfers between devices: 9.85 us -> 0.01 us  [exchange(): lax.all_to_all(blocks, axis, split_axis=0, concat_axis=0, tiled=True, axi...]
    pallas_call x8 -> x10, Pallas kernels: 10.7 us -> 13.1 us  [the longest x8 8.87 us: call(): pl.pallas_call(kernel, in_specs=specs, compiler_params=params, **options)]
  transfers between devices with their start and end apart: 1 -> 8, of which waited for: 1 -> 4; matrix products, arithmetic and copies ran while one was open for 0% -> 0% of each run, Pallas kernels for 1% -> 3%
where the time goes in v4:
time: 171 us; the launch traced here: 170 us
  blocking collectives  102 us (60%)
  starting transfers between devices  35.8 us (21%)
  waiting for transfers between devices  16.9 us (10%)
  Pallas kernels  13.1 us (8%)
    all_to_all x4, blocking collectives, exchange(): lax.all_to_all(blocks, axis, split_axis=0, concat_axis=0, tiled=True, axi...  102 us
    ppermute x6, starting transfers between devices, swap(): out.append(lax.ppermute(chunks[k], ('exp', 'attn'), pairs))  19.5 us
    ppermute x6, waiting for transfers between devices, swap(): out.append(lax.ppermute(chunks[k], ('exp', 'attn'), pairs))  16.9 us
    all_to_all x2, starting transfers between devices, exchange(): lax.all_to_all(blocks, axis, split_axis=0, concat_axis=0, tiled=True, axi...  16.3 us
    pallas_call x8, Pallas kernels, call(): pl.pallas_call(kernel, in_specs=specs, compiler_params=params, **options)  8.87 us
    pallas_call x2, Pallas kernels, call_fetching(): pl.pallas_call(body, in_specs=[pl.BlockSpec(memory_space=x) for x in spac...  4.19 us
  transfers between devices with their start and end apart: 8, of which 4 were waited for; matrix products, arithmetic and copies ran while one was open for 0% of the time, Pallas kernels for 3%

profile of v4, /device:TPU:1, one launch (start us, length us, event | category | flops | bytes accessed | tf_op | source)
XLA Modules:
  0.0 169.9 jit_solution(8490341792051625270)
XLA Ops:
  0.6 1.9 %pack.1 = (bf16[512,256]{1,0:T(8,128)(2,1)}, s32[2,128]{1,0:T(2,128)}) custom-call(s32[2,128]{1,0:T(2,128)} %bitcast.31, bf16[2,128]{1,0:T(2,128)(2,1)} %bitcast.33, bf16[128,128]{1,0:T(8,128)(2,1)} %refs_2_.1, bf16[128,128]{1,0:T(8,128)(2,1)} %refs_3_.1), custom_call_target="tpu_custom_call" | custom-call | tf_op jit(solution)/shard_map/pack/pallas_call | solution.py:287
  2.6 31.4 %all_to_all.30 = bf16[64,8,256]{2,1,0:T(8,128)(2,1)S(1)} all-to-all(bf16[64,8,256]{2,1,0:T(8,128)(2,1)} %bitcast.35), channel_id=1, replica_groups=mesh['exp'=64,'attn'=16] {'exp'}, dimensions={0} | all-to-all | bytes 524288 | tf_op jit(solution)/shard_map/all_to_all | solution.py:229
  33.9 1.2 spread.1
  35.1 10.6 %all-to-all-start.1 = ((bf16[4,768,128]{2,1,0:T(8,128)(2,1)}), bf16[4,768,128]{2,1,0:T(8,128)(2,1)}, u32[]{:S(2)}, u32[]{:S(2)}) async-start(bf16[4,768,128]{2,1,0:T(8,128)(2,1)} %bitcast.5), calls=%async_computation.1 | async-start | bytes 1572864 | tf_op jit(solution)/shard_map/all_to_all | solution.py:229
  45.7 2.3 %turn.1 = (bf16[576,128]{1,0:T(8,128)(2,1)}, bf16[576,128]{1,0:T(8,128)(2,1)}, bf16[576,128]{1,0:T(8,128)(2,1)}, bf16[576,128]{1,0:T(8,128)(2,1)}) custom-call(s32[1]{0:T(128)} %bitcast.2.refs_0_.near_ref, bf16[128,768]{1,0:T(8,128)(2,1)} %bitcast.36, bf16[128,768]{1,0:T(8,128)(2,1)} %bitcast.37, bf16[768,128]{1,0:T(8,128)(2,1)} %bitcast.38), custom_call_target="tpu_custom_call" | custom-call | tf_op jit(solution)/shard_map/turn/pallas_call | solution.py:287
  48.0 3.4 %collective-permute-start = (bf16[576,128]{1,0:T(8,128)(2,1)}, bf16[576,128]{1,0:T(8,128)(2,1)S(1)}, u32[]{:S(2)}, u32[]{:S(2)}) collective-permute-start(bf16[576,128]{1,0:T(8,128)(2,1)} %get-tuple-element.23), channel_id=1, source_target_pairs={{0,1},{1,0},{2,3},{3,2},{4,5},{5,4},{6,7},{7,6},{10,11},{11,10},{8... | collective-permute-start | bytes 442376 | tf_op jit(solution)/shard_map/ppermute | solution.py:261
  51.4 4.6 %collective-permute-start.1 = (bf16[576,128]{1,0:T(8,128)(2,1)}, bf16[576,128]{1,0:T(8,128)(2,1)S(1)}, u32[]{:S(2)}, u32[]{:S(2)}) collective-permute-start(bf16[576,128]{1,0:T(8,128)(2,1)} %get-tuple-element.24), channel_id=1, source_target_pairs={{0,2},{1,3},{2,0},{3,1},{4,6},{5,7},{6,4},{7,5},{10,8},{11,9},{8,1... | collective-permute-start | bytes 442376 | tf_op jit(solution)/shard_map/ppermute | solution.py:261
  56.0 1.9 %collective-permute-start.2 = (bf16[576,128]{1,0:T(8,128)(2,1)}, bf16[576,128]{1,0:T(8,128)(2,1)S(1)}, u32[]{:S(2)}, u32[]{:S(2)}) collective-permute-start(bf16[576,128]{1,0:T(8,128)(2,1)} %get-tuple-element.25), channel_id=1, source_target_pairs={{0,3},{1,2},{2,1},{3,0},{4,7},{5,6},{6,5},{7,4},{10,9},{11,8},{8,1... | collective-permute-start | bytes 442376 | tf_op jit(solution)/shard_map/ppermute | solution.py:261
  57.9 3.0 %collective-permute-done.refs_1_ = bf16[576,128]{1,0:T(8,128)(2,1)S(1)} collective-permute-done((bf16[576,128]{1,0:T(8,128)(2,1)}, bf16[576,128]{1,0:T(8,128)(2,1)S(1)}, u32[]{:S(2)}, u32[]{:S(2)}) %collective-permute-start) | collective-permute-done | bytes 147488 | tf_op jit(solution)/shard_map/ppermute | solution.py:261
  60.9 8.2 %collective-permute-done.1.refs_2_ = bf16[576,128]{1,0:T(8,128)(2,1)S(1)} collective-permute-done((bf16[576,128]{1,0:T(8,128)(2,1)}, bf16[576,128]{1,0:T(8,128)(2,1)S(1)}, u32[]{:S(2)}, u32[]{:S(2)}) %collective-permute-start.1) | collective-permute-done | bytes 147488 | tf_op jit(solution)/shard_map/ppermute | solution.py:261
  69.2 0.0 collective-permute-done.2.refs_3_
  69.2 0.0 all-to-all-done.1
  69.2 0.9 copy-done
  70.1 1.8 %partial.1 = bf16[576,384]{1,0:T(8,128)(2,1)S(1)} custom-call(s32[1]{0:T(128)} %bitcast.2.refs_0_.near_ref, bf16[3072,128]{1,0:T(8,128)(2,1)} %bitcast.6.held_ref, bf16[576,128]{1,0:T(8,128)(2,1)S(1)} %copy-done, bf16[576,128]{1,0:T(8,128)(2,1)S(1)} %collective-permute-done.refs_1_, bf16[576,128]{1,0:T(8,128)(2,1)S(1)} %collective-permute-done.1.refs_2_, ...), custom_call_target="tpu_custom_call" | custom-call | tf_op jit(solution)/shard_map/partial/pallas_call | solution.py:268
  71.9 29.3 %all_to_all.31 = bf16[4,144,384]{2,1,0:T(8,128)(2,1)S(1)} all-to-all(bf16[4,144,384]{2,1,0:T(8,128)(2,1)S(1)} %bitcast.26), channel_id=1, replica_groups={{0,4,10,14},{1,5,11,15},{2,6,8,12},{3,7,9,13},{18,22,28,16},{19,23,29,1..., dimensions={0} | all-to-all | bytes 884736 | tf_op jit(solution)/shard_map/all_to_all | solution.py:229
  101.2 0.1 acts.1
  101.3 0.0 copy-start.1
  101.3 24.1 %all_to_all.32 = bf16[4,152,384]{2,1,0:T(8,128)(2,1)S(1)} all-to-all(bf16[4,152,384]{2,1,0:T(8,128)(2,1)S(1)} %bitcast.24), channel_id=1, replica_groups={{0,4,10,14},{1,5,11,15},{2,6,8,12},{3,7,9,13},{18,22,28,16},{19,23,29,1..., dimensions={0} | all-to-all | bytes 933888 | tf_op jit(solution)/shard_map/all_to_all | solution.py:229
  125.4 0.6 terms.1
  126.0 17.0 %all_to_all.33 = bf16[4,392,128]{2,1,0:T(8,128)(2,1)S(1)} all-to-all(bf16[4,392,128]{2,1,0:T(8,128)(2,1)S(1)} %bitcast.27), channel_id=1, replica_groups={{0,1,2,3},{4,5,6,7},{10,11,8,9},{14,15,12,13},{18,19,20,21},{22,23,24,2..., dimensions={0} | all-to-all | bytes 802816 | tf_op jit(solution)/shard_map/all_to_all | solution.py:229
  143.0 1.2 back.1.back_ref
  144.2 5.7 %all-to-all-start.5 = ((bf16[64,8,128]{2,1,0:T(8,128)(2,1)}), bf16[64,8,128]{2,1,0:T(8,128)(2,1)S(1)}, u32[]{:S(2)}, u32[]{:S(2)}) async-start(bf16[64,8,128]{2,1,0:T(8,128)(2,1)} %bitcast.16), calls=%async_computation.5 | async-start | bytes 262144 | tf_op jit(solution)/shard_map/all_to_all | solution.py:229
  149.9 1.8 %grads.1 = (bf16[576,128]{1,0:T(8,128)(2,1)S(1)}, bf16[576,128]{1,0:T(8,128)(2,1)S(1)}, bf16[576,128]{1,0:T(8,128)(2,1)S(1)}, bf16[576,128]{1,0:T(8,128)(2,1)S(1)}) custom-call(s32[1]{0:T(128)} %bitcast.2.refs_0_.near_ref, bf16[3072,128]{1,0:T(8,128)(2,1)} %bitcast.6.held_ref, bf16[608,384]{1,0:T(8,128)(2,1)S(1)} %bitcast.23, bf16[512,128]{1,0:T(8,128)(2,1)} %back.1.back_ref), custom_call_target="tpu_custom_call" | custom-call | tf_op jit(solution)/shard_map/grads/pallas_call | solution.py:268
  151.7 2.2 %collective-permute-start.3 = (bf16[576,128]{1,0:T(8,128)(2,1)S(1)}, bf16[576,128]{1,0:T(8,128)(2,1)S(1)}, u32[]{:S(2)}, u32[]{:S(2)}) collective-permute-start(bf16[576,128]{1,0:T(8,128)(2,1)S(1)} %get-tuple-element.29), channel_id=1, source_target_pairs={{0,1},{1,0},{2,3},{3,2},{4,5},{5,4},{6,7},{7,6},{10,11},{11,10},{8... | collective-permute-start | bytes 442376 | tf_op jit(solution)/shard_map/ppermute | solution.py:261
  154.0 1.9 %collective-permute-start.4 = (bf16[576,128]{1,0:T(8,128)(2,1)S(1)}, bf16[576,128]{1,0:T(8,128)(2,1)S(1)}, u32[]{:S(2)}, u32[]{:S(2)}) collective-permute-start(bf16[576,128]{1,0:T(8,128)(2,1)S(1)} %get-tuple-element.30), channel_id=1, source_target_pairs={{0,2},{1,3},{2,0},{3,1},{4,6},{5,7},{6,4},{7,5},{10,8},{11,9},{8,1... | collective-permute-start | bytes 442376 | tf_op jit(solution)/shard_map/ppermute | solution.py:261
  155.9 5.4 %collective-permute-start.5 = (bf16[576,128]{1,0:T(8,128)(2,1)S(1)}, bf16[576,128]{1,0:T(8,128)(2,1)S(1)}, u32[]{:S(2)}, u32[]{:S(2)}) collective-permute-start(bf16[576,128]{1,0:T(8,128)(2,1)S(1)} %get-tuple-element.31), channel_id=1, source_target_pairs={{0,3},{1,2},{2,1},{3,0},{4,7},{5,6},{6,5},{7,4},{10,9},{11,8},{8,1... | collective-permute-start | bytes 442376 | tf_op jit(solution)/shard_map/ppermute | solution.py:261
  161.3 0.0 collective-permute-done.3.refs_1_
  161.3 2.2 %collective-permute-done.4.refs_2_ = bf16[576,128]{1,0:T(8,128)(2,1)S(1)} collective-permute-done((bf16[576,128]{1,0:T(8,128)(2,1)S(1)}, bf16[576,128]{1,0:T(8,128)(2,1)S(1)}, u32[]{:S(2)}, u32[]{:S(2)}) %collective-permute-start.4) | collective-permute-done | bytes 147488 | tf_op jit(solution)/shard_map/ppermute | solution.py:261
  163.6 3.4 %collective-permute-done.5.refs_3_ = bf16[576,128]{1,0:T(8,128)(2,1)S(1)} collective-permute-done((bf16[576,128]{1,0:T(8,128)(2,1)S(1)}, bf16[576,128]{1,0:T(8,128)(2,1)S(1)}, u32[]{:S(2)}, u32[]{:S(2)}) %collective-permute-start.5) | collective-permute-done | bytes 147488 | tf_op jit(solution)/shard_map/ppermute | solution.py:261
  166.9 1.3 out.1
  168.2 0.7 copy-done.2
  168.9 0.9 merge.1
  (8 shorter events, 0.0 us)
Async XLA Ops:
  35.1 34.1 %all-to-all-start.1 = ((bf16[4,768,128]{2,1,0:T(8,128)(2,1)}), bf16[4,768,128]{2,1,0:T(8,128)(2,1)}, u32[]{:S(2)}, u32[]{:S(2)}) async-start(bf16[4,768,128]{2,1,0:T(8,128)(2,1)} %bitcast.5), calls=%async_computation.1 | async-start | bytes 1572864 | tf_op jit(solution)/shard_map/all_to_all | solution.py:229
  48.0 12.9 %collective-permute-start = (bf16[576,128]{1,0:T(8,128)(2,1)}, bf16[576,128]{1,0:T(8,128)(2,1)S(1)}, u32[]{:S(2)}, u32[]{:S(2)}) collective-permute-start(bf16[576,128]{1,0:T(8,128)(2,1)} %get-tuple-element.23), channel_id=1, source_target_pairs={{0,1},{1,0},{2,3},{3,2},{4,5},{5,4},{6,7},{7,6},{10,11},{11,10},{8... | collective-permute-start | bytes 442376 | tf_op jit(solution)/shard_map/ppermute | solution.py:261
  51.4 17.8 %collective-permute-start.1 = (bf16[576,128]{1,0:T(8,128)(2,1)}, bf16[576,128]{1,0:T(8,128)(2,1)S(1)}, u32[]{:S(2)}, u32[]{:S(2)}) collective-permute-start(bf16[576,128]{1,0:T(8,128)(2,1)} %get-tuple-element.24), channel_id=1, source_target_pairs={{0,2},{1,3},{2,0},{3,1},{4,6},{5,7},{6,4},{7,5},{10,8},{11,9},{8,1... | collective-permute-start | bytes 442376 | tf_op jit(solution)/shard_map/ppermute | solution.py:261
  56.0 13.2 %collective-permute-start.2 = (bf16[576,128]{1,0:T(8,128)(2,1)}, bf16[576,128]{1,0:T(8,128)(2,1)S(1)}, u32[]{:S(2)}, u32[]{:S(2)}) collective-permute-start(bf16[576,128]{1,0:T(8,128)(2,1)} %get-tuple-element.25), channel_id=1, source_target_pairs={{0,3},{1,2},{2,1},{3,0},{4,7},{5,6},{6,5},{7,4},{10,9},{11,8},{8,1... | collective-permute-start | bytes 442376 | tf_op jit(solution)/shard_map/ppermute | solution.py:261
  69.2 0.9 copy-start
  101.3 24.1 %copy-start.1 = (bf16[576,128]{1,0:T(8,128)(2,1)S(1)}, bf16[576,128]{1,0:T(8,128)(2,1)}, u32[]{:S(2)}) copy-start(bf16[576,128]{1,0:T(8,128)(2,1)} %get-tuple-element.22.refs_0_) | copy-start | bytes 442372
  144.2 24.0 %all-to-all-start.5 = ((bf16[64,8,128]{2,1,0:T(8,128)(2,1)}), bf16[64,8,128]{2,1,0:T(8,128)(2,1)S(1)}, u32[]{:S(2)}, u32[]{:S(2)}) async-start(bf16[64,8,128]{2,1,0:T(8,128)(2,1)} %bitcast.16), calls=%async_computation.5 | async-start | bytes 262144 | tf_op jit(solution)/shard_map/all_to_all | solution.py:229
  151.7 9.6 %collective-permute-start.3 = (bf16[576,128]{1,0:T(8,128)(2,1)S(1)}, bf16[576,128]{1,0:T(8,128)(2,1)S(1)}, u32[]{:S(2)}, u32[]{:S(2)}) collective-permute-start(bf16[576,128]{1,0:T(8,128)(2,1)S(1)} %get-tuple-element.29), channel_id=1, source_target_pairs={{0,1},{1,0},{2,3},{3,2},{4,5},{5,4},{6,7},{7,6},{10,11},{11,10},{8... | collective-permute-start | bytes 442376 | tf_op jit(solution)/shard_map/ppermute | solution.py:261
  154.0 9.6 %collective-permute-start.4 = (bf16[576,128]{1,0:T(8,128)(2,1)S(1)}, bf16[576,128]{1,0:T(8,128)(2,1)S(1)}, u32[]{:S(2)}, u32[]{:S(2)}) collective-permute-start(bf16[576,128]{1,0:T(8,128)(2,1)S(1)} %get-tuple-element.30), channel_id=1, source_target_pairs={{0,2},{1,3},{2,0},{3,1},{4,6},{5,7},{6,4},{7,5},{10,8},{11,9},{8,1... | collective-permute-start | bytes 442376 | tf_op jit(solution)/shard_map/ppermute | solution.py:261
  155.9 11.1 %collective-permute-start.5 = (bf16[576,128]{1,0:T(8,128)(2,1)S(1)}, bf16[576,128]{1,0:T(8,128)(2,1)S(1)}, u32[]{:S(2)}, u32[]{:S(2)}) collective-permute-start(bf16[576,128]{1,0:T(8,128)(2,1)S(1)} %get-tuple-element.31), channel_id=1, source_target_pairs={{0,3},{1,2},{2,1},{3,0},{4,7},{5,6},{6,5},{7,4},{10,9},{11,8},{8,1... | collective-permute-start | bytes 442376 | tf_op jit(solution)/shard_map/ppermute | solution.py:261
  166.9 1.3 copy-start.4
  168.2 0.7 copy-start.2
  168.2 0.7 copy-start.3

commit v5 on v4

--- a/solution.py
+++ b/solution.py
@@ -27,7 +27,7 @@
     return lax.dot_general(a, b, (((ca,), (cb,)), ((), ())), preferred_element_type=F32)
 
 
-def pack_kernel(ready, ids_ref, weight_ref, tok_ref, cot_ref, send_ref, rank_ref):
+def pack_kernel(ready, ids_ref, weight_ref, tok_ref, cot_ref, send_ref, table_ref):
     ready()
     top, tok = ids_ref.shape
     rows = send_ref.shape[0]
@@ -48,7 +48,9 @@
         hit = slot == ids[j : j + 1, :] * PAD + rank
         hots.append(jnp.where(hit, 1.0, 0.0))
         scaled.append(jnp.where(hit, weight[j : j + 1, :], 0.0))
-    rank_ref[...] = jnp.concatenate(ranks, axis=0)
+    firsts = [ids[j : j + 1, :] * PAD for j in range(top)]
+    table = jnp.concatenate(firsts + ranks, axis=0).astype(F32)
+    table_ref[...] = jnp.concatenate([table, 1.0 / weight], axis=0)
     plain = functools.reduce(jnp.add, hots).astype(BF16)
     heavy = functools.reduce(jnp.add, scaled).astype(BF16)
     send_ref[:, :width] = mm(plain, tok_ref[...], 1, 0).astype(BF16)
@@ -162,7 +164,7 @@
         out_ref[pl.ds(to + slots, PAD), :] = score
 
 
-def grad_kernel(strided, near_ref, held_ref, acts_ref, back_ref, *out_refs):
+def grad_kernel(strided, near_ref, held_ref, acts_ref, *out_refs):
     slots = acts_ref.shape[1]
     piece = out_refs[0].shape[0] // 3
     act, grad_g, grad_u = acts_of(acts_ref, strided)
@@ -206,20 +208,21 @@
     grad_down_ref[...] = held_ref[2 * hidden :, :].astype(F32)
 
 
-def merge_kernel(cap, ids_ref, rank_ref, weight_ref, recv_ref, tok_ref, route_ref):
-    top, tok = ids_ref.shape
+def merge_kernel(cap, table_ref, recv_ref, tok_ref, route_ref):
+    top, tok = route_ref.shape
     rows, width = recv_ref.shape
     recv = recv_ref[...]
     slot = iota((rows, tok), 0)
     sub = iota((width, tok), 0)
+    first, rank = (table_ref[i * top : (i + 1) * top, :].astype(jnp.int32) for i in range(2))
     hots, scores = [], []
     for j in range(top):
-        ids, rank = ids_ref[j : j + 1, :], rank_ref[j : j + 1, :]
-        hots.append(jnp.where(slot == ids * PAD + rank, 1.0, 0.0))
-        line = mm(recv, one_hot(slot == ids * PAD + cap), 0, 0)
-        scores.append(jnp.sum(jnp.where(sub == rank, line, 0.0), axis=0, keepdims=True))
+        at, own = first[j : j + 1, :], rank[j : j + 1, :]
+        hots.append(jnp.where(slot == at + own, 1.0, 0.0))
+        line = mm(recv, one_hot(slot == at + cap), 0, 0)
+        scores.append(jnp.sum(jnp.where(sub == own, line, 0.0), axis=0, keepdims=True))
     tok_ref[...] = mm(functools.reduce(jnp.add, hots).astype(BF16), recv, 0, 0).astype(BF16)
-    route_ref[...] = jnp.concatenate(scores, axis=0) / weight_ref[...].astype(F32)
+    route_ref[...] = jnp.concatenate(scores, axis=0) * table_ref[2 * top : 3 * top, :]
 
 
 def exchange(rows, axis, groups=None):
@@ -314,11 +317,11 @@
     ids, weight = expert_ids.T, route_weight.T
     gate_w, up_w, down_w = gate_weight[0], up_weight[0], down_weight[0]
 
-    send, rank = call_fetching(
+    send, table = call_fetching(
         pack_kernel,
         (),
         (ids, weight, tokens, cotangent),
-        out_shape=(shape_of(padded, 2 * width), shape_of(top, tok, dtype=jnp.int32)),
+        out_shape=(shape_of(padded, 2 * width), shape_of(3 * top, tok, dtype=F32)),
         name="pack",
     )
     recv = exchange(send, "exp")
@@ -358,19 +361,20 @@
         out_shape=shape_of(local * (slots + PAD), width),
         name="terms",
     )
+    terms = exchange(terms, "attn", near)
+    got = call(
+        functools.partial(grad_kernel, strided),
+        (me, held, acts),
+        out_shape=(shape_of(3 * piece, width),) * local,
+        name="grads",
+    )
+    got = swap(got, near)
     back = call(
         functools.partial(back_kernel, cap, slots, local),
-        (exchange(terms, "attn", near),),
+        (terms,),
         out_shape=shape_of(padded, width),
         name="back",
     )
-    got = call(
-        functools.partial(grad_kernel, strided),
-        (me, held, acts, back),
-        out_shape=(shape_of(3 * piece, width),) * local,
-        name="grads",
-    )
-    got = swap(got, near)
     grad_gate, grad_up, grad_down = call(
         out_kernel,
         (me, *got),
@@ -384,7 +388,7 @@
     )
     grad_tokens, grad_route = call(
         functools.partial(merge_kernel, cap),
-        (ids, rank, weight, exchange(back, "exp")),
+        (table, exchange(back, "exp")),
         out_shape=(shape_of(tok, width), shape_of(top, tok, dtype=F32)),
         name="merge",
     )

time: 171 us -> 170 us (level)
  no operation moved by 1% of the time
where the time goes in v5:
time: 170 us; the launch traced here: 169 us
  blocking collectives  102 us (60%)
  starting transfers between devices  35.9 us (21%)
  waiting for transfers between devices  16.9 us (10%)
  Pallas kernels  13.1 us (8%)
    all_to_all x4, blocking collectives, exchange(): lax.all_to_all(blocks, axis, split_axis=0, concat_axis=0, tiled=True, axi...  102 us
    ppermute x6, starting transfers between devices, swap(): out.append(lax.ppermute(chunks[k], ('exp', 'attn'), pairs))  19.5 us
    ppermute x6, waiting for transfers between devices, swap(): out.append(lax.ppermute(chunks[k], ('exp', 'attn'), pairs))  16.9 us
    all_to_all x2, starting transfers between devices, exchange(): lax.all_to_all(blocks, axis, split_axis=0, concat_axis=0, tiled=True, axi...  16.4 us
    pallas_call x8, Pallas kernels, call(): pl.pallas_call(kernel, in_specs=specs, compiler_params=params, **options)  8.88 us
    pallas_call x2, Pallas kernels, call_fetching(): pl.pallas_call(body, in_specs=[pl.BlockSpec(memory_space=x) for x in spac...  4.18 us
  transfers between devices with their start and end apart: 8, of which 4 were waited for; matrix products, arithmetic and copies ran while one was open for 0% of the time, Pallas kernels for 3%

profile of v5, /device:TPU:1, one launch (start us, length us, event | category | flops | bytes accessed | tf_op | source)
XLA Modules:
  0.0 169.3 jit_solution(3311346152099798322)
XLA Ops:
  0.6 1.9 %pack.1 = (bf16[512,256]{1,0:T(8,128)(2,1)}, f32[6,128]{1,0:T(8,128)}) custom-call(s32[2,128]{1,0:T(2,128)} %bitcast.35, bf16[2,128]{1,0:T(2,128)(2,1)} %bitcast.36, bf16[128,128]{1,0:T(8,128)(2,1)} %refs_2_.1, bf16[128,128]{1,0:T(8,128)(2,1)} %refs_3_.1), custom_call_target="tpu_custom_call" | custom-call | tf_op jit(solution)/shard_map/pack/pallas_call | solution.py:290
  2.6 31.4 %all_to_all.30 = bf16[64,8,256]{2,1,0:T(8,128)(2,1)S(1)} all-to-all(bf16[64,8,256]{2,1,0:T(8,128)(2,1)} %bitcast.31), channel_id=1, replica_groups=mesh['exp'=64,'attn'=16] {'exp'}, dimensions={0} | all-to-all | bytes 524288 | tf_op jit(solution)/shard_map/all_to_all | solution.py:232
  33.9 1.2 spread.1
  35.1 10.6 %all-to-all-start.1 = ((bf16[4,768,128]{2,1,0:T(8,128)(2,1)}), bf16[4,768,128]{2,1,0:T(8,128)(2,1)}, u32[]{:S(2)}, u32[]{:S(2)}) async-start(bf16[4,768,128]{2,1,0:T(8,128)(2,1)} %bitcast.5), calls=%async_computation.1 | async-start | bytes 1572864 | tf_op jit(solution)/shard_map/all_to_all | solution.py:232
  45.7 2.3 %turn.1 = (bf16[576,128]{1,0:T(8,128)(2,1)}, bf16[576,128]{1,0:T(8,128)(2,1)}, bf16[576,128]{1,0:T(8,128)(2,1)}, bf16[576,128]{1,0:T(8,128)(2,1)}) custom-call(s32[1]{0:T(128)} %bitcast.2.refs_0_.near_ref, bf16[128,768]{1,0:T(8,128)(2,1)} %bitcast.32, bf16[128,768]{1,0:T(8,128)(2,1)} %bitcast.33, bf16[768,128]{1,0:T(8,128)(2,1)} %bitcast.34), custom_call_target="tpu_custom_call" | custom-call | tf_op jit(solution)/shard_map/turn/pallas_call | solution.py:290
  48.0 3.4 %collective-permute-start = (bf16[576,128]{1,0:T(8,128)(2,1)}, bf16[576,128]{1,0:T(8,128)(2,1)S(1)}, u32[]{:S(2)}, u32[]{:S(2)}) collective-permute-start(bf16[576,128]{1,0:T(8,128)(2,1)} %get-tuple-element.23), channel_id=1, source_target_pairs={{0,1},{1,0},{2,3},{3,2},{4,5},{5,4},{6,7},{7,6},{10,11},{11,10},{8... | collective-permute-start | bytes 442376 | tf_op jit(solution)/shard_map/ppermute | solution.py:264
  51.4 4.6 %collective-permute-start.1 = (bf16[576,128]{1,0:T(8,128)(2,1)}, bf16[576,128]{1,0:T(8,128)(2,1)S(1)}, u32[]{:S(2)}, u32[]{:S(2)}) collective-permute-start(bf16[576,128]{1,0:T(8,128)(2,1)} %get-tuple-element.24), channel_id=1, source_target_pairs={{0,2},{1,3},{2,0},{3,1},{4,6},{5,7},{6,4},{7,5},{10,8},{11,9},{8,1... | collective-permute-start | bytes 442376 | tf_op jit(solution)/shard_map/ppermute | solution.py:264
  56.0 1.9 %collective-permute-start.2 = (bf16[576,128]{1,0:T(8,128)(2,1)}, bf16[576,128]{1,0:T(8,128)(2,1)S(1)}, u32[]{:S(2)}, u32[]{:S(2)}) collective-permute-start(bf16[576,128]{1,0:T(8,128)(2,1)} %get-tuple-element.25), channel_id=1, source_target_pairs={{0,3},{1,2},{2,1},{3,0},{4,7},{5,6},{6,5},{7,4},{10,9},{11,8},{8,1... | collective-permute-start | bytes 442376 | tf_op jit(solution)/shard_map/ppermute | solution.py:264
  57.9 3.0 %collective-permute-done.refs_1_ = bf16[576,128]{1,0:T(8,128)(2,1)S(1)} collective-permute-done((bf16[576,128]{1,0:T(8,128)(2,1)}, bf16[576,128]{1,0:T(8,128)(2,1)S(1)}, u32[]{:S(2)}, u32[]{:S(2)}) %collective-permute-start) | collective-permute-done | bytes 147488 | tf_op jit(solution)/shard_map/ppermute | solution.py:264
  61.0 8.2 %collective-permute-done.1.refs_2_ = bf16[576,128]{1,0:T(8,128)(2,1)S(1)} collective-permute-done((bf16[576,128]{1,0:T(8,128)(2,1)}, bf16[576,128]{1,0:T(8,128)(2,1)S(1)}, u32[]{:S(2)}, u32[]{:S(2)}) %collective-permute-start.1) | collective-permute-done | bytes 147488 | tf_op jit(solution)/shard_map/ppermute | solution.py:264
  69.2 0.0 collective-permute-done.2.refs_3_
  69.2 0.0 all-to-all-done.1
  69.2 0.9 copy-done
  70.1 1.8 %partial.1 = bf16[576,384]{1,0:T(8,128)(2,1)S(1)} custom-call(s32[1]{0:T(128)} %bitcast.2.refs_0_.near_ref, bf16[3072,128]{1,0:T(8,128)(2,1)} %bitcast.6.held_ref, bf16[576,128]{1,0:T(8,128)(2,1)S(1)} %copy-done, bf16[576,128]{1,0:T(8,128)(2,1)S(1)} %collective-permute-done.refs_1_, bf16[576,128]{1,0:T(8,128)(2,1)S(1)} %collective-permute-done.1.refs_2_, ...), custom_call_target="tpu_custom_call" | custom-call | tf_op jit(solution)/shard_map/partial/pallas_call | solution.py:271
  71.9 29.3 %all_to_all.31 = bf16[4,144,384]{2,1,0:T(8,128)(2,1)S(1)} all-to-all(bf16[4,144,384]{2,1,0:T(8,128)(2,1)S(1)} %bitcast.26), channel_id=1, replica_groups={{0,4,10,14},{1,5,11,15},{2,6,8,12},{3,7,9,13},{18,22,28,16},{19,23,29,1..., dimensions={0} | all-to-all | bytes 884736 | tf_op jit(solution)/shard_map/all_to_all | solution.py:232
  101.2 0.1 acts.1
  101.3 0.0 copy-start.1
  101.3 24.1 %all_to_all.32 = bf16[4,152,384]{2,1,0:T(8,128)(2,1)S(1)} all-to-all(bf16[4,152,384]{2,1,0:T(8,128)(2,1)S(1)} %bitcast.24), channel_id=1, replica_groups={{0,4,10,14},{1,5,11,15},{2,6,8,12},{3,7,9,13},{18,22,28,16},{19,23,29,1..., dimensions={0} | all-to-all | bytes 933888 | tf_op jit(solution)/shard_map/all_to_all | solution.py:232
  125.4 0.6 terms.1
  126.0 17.0 %all_to_all.33 = bf16[4,392,128]{2,1,0:T(8,128)(2,1)S(1)} all-to-all(bf16[4,392,128]{2,1,0:T(8,128)(2,1)S(1)} %bitcast.27), channel_id=1, replica_groups={{0,1,2,3},{4,5,6,7},{10,11,8,9},{14,15,12,13},{18,19,20,21},{22,23,24,2..., dimensions={0} | all-to-all | bytes 802816 | tf_op jit(solution)/shard_map/all_to_all | solution.py:232
  143.0 1.2 back.1
  144.2 5.8 %all-to-all-start.5 = ((bf16[64,8,128]{2,1,0:T(8,128)(2,1)}), bf16[64,8,128]{2,1,0:T(8,128)(2,1)S(1)}, u32[]{:S(2)}, u32[]{:S(2)}) async-start(bf16[64,8,128]{2,1,0:T(8,128)(2,1)} %bitcast.16), calls=%async_computation.5 | async-start | bytes 262144 | tf_op jit(solution)/shard_map/all_to_all | solution.py:232
  150.0 1.8 %grads.1 = (bf16[576,128]{1,0:T(8,128)(2,1)S(1)}, bf16[576,128]{1,0:T(8,128)(2,1)S(1)}, bf16[576,128]{1,0:T(8,128)(2,1)S(1)}, bf16[576,128]{1,0:T(8,128)(2,1)S(1)}) custom-call(s32[1]{0:T(128)} %bitcast.2.refs_0_.near_ref, bf16[3072,128]{1,0:T(8,128)(2,1)} %bitcast.6.held_ref, bf16[608,384]{1,0:T(8,128)(2,1)S(1)} %bitcast.23), custom_call_target="tpu_custom_call" | custom-call | tf_op jit(solution)/shard_map/grads/pallas_call | solution.py:271
  151.8 2.2 %collective-permute-start.3 = (bf16[576,128]{1,0:T(8,128)(2,1)S(1)}, bf16[576,128]{1,0:T(8,128)(2,1)S(1)}, u32[]{:S(2)}, u32[]{:S(2)}) collective-permute-start(bf16[576,128]{1,0:T(8,128)(2,1)S(1)} %get-tuple-element.29), channel_id=1, source_target_pairs={{0,1},{1,0},{2,3},{3,2},{4,5},{5,4},{6,7},{7,6},{10,11},{11,10},{8... | collective-permute-start | bytes 442376 | tf_op jit(solution)/shard_map/ppermute | solution.py:264
  154.0 1.9 %collective-permute-start.4 = (bf16[576,128]{1,0:T(8,128)(2,1)S(1)}, bf16[576,128]{1,0:T(8,128)(2,1)S(1)}, u32[]{:S(2)}, u32[]{:S(2)}) collective-permute-start(bf16[576,128]{1,0:T(8,128)(2,1)S(1)} %get-tuple-element.30), channel_id=1, source_target_pairs={{0,2},{1,3},{2,0},{3,1},{4,6},{5,7},{6,4},{7,5},{10,8},{11,9},{8,1... | collective-permute-start | bytes 442376 | tf_op jit(solution)/shard_map/ppermute | solution.py:264
  156.0 5.4 %collective-permute-start.5 = (bf16[576,128]{1,0:T(8,128)(2,1)S(1)}, bf16[576,128]{1,0:T(8,128)(2,1)S(1)}, u32[]{:S(2)}, u32[]{:S(2)}) collective-permute-start(bf16[576,128]{1,0:T(8,128)(2,1)S(1)} %get-tuple-element.31), channel_id=1, source_target_pairs={{0,3},{1,2},{2,1},{3,0},{4,7},{5,6},{6,5},{7,4},{10,9},{11,8},{8,1... | collective-permute-start | bytes 442376 | tf_op jit(solution)/shard_map/ppermute | solution.py:264
  161.4 0.0 collective-permute-done.3.refs_1_
  161.4 2.2 %collective-permute-done.4.refs_2_ = bf16[576,128]{1,0:T(8,128)(2,1)S(1)} collective-permute-done((bf16[576,128]{1,0:T(8,128)(2,1)S(1)}, bf16[576,128]{1,0:T(8,128)(2,1)S(1)}, u32[]{:S(2)}, u32[]{:S(2)}) %collective-permute-start.4) | collective-permute-done | bytes 147488 | tf_op jit(solution)/shard_map/ppermute | solution.py:264
  163.6 3.4 %collective-permute-done.5.refs_3_ = bf16[576,128]{1,0:T(8,128)(2,1)S(1)} collective-permute-done((bf16[576,128]{1,0:T(8,128)(2,1)S(1)}, bf16[576,128]{1,0:T(8,128)(2,1)S(1)}, u32[]{:S(2)}, u32[]{:S(2)}) %collective-permute-start.5) | collective-permute-done | bytes 147488 | tf_op jit(solution)/shard_map/ppermute | solution.py:264
  167.0 1.3 out.1
  168.3 0.0 all-to-all-done.5
  168.3 0.9 merge.1
  (4 shorter events, 0.0 us)
Async XLA Ops:
  35.1 34.1 %all-to-all-start.1 = ((bf16[4,768,128]{2,1,0:T(8,128)(2,1)}), bf16[4,768,128]{2,1,0:T(8,128)(2,1)}, u32[]{:S(2)}, u32[]{:S(2)}) async-start(bf16[4,768,128]{2,1,0:T(8,128)(2,1)} %bitcast.5), calls=%async_computation.1 | async-start | bytes 1572864 | tf_op jit(solution)/shard_map/all_to_all | solution.py:232
  48.0 12.9 %collective-permute-start = (bf16[576,128]{1,0:T(8,128)(2,1)}, bf16[576,128]{1,0:T(8,128)(2,1)S(1)}, u32[]{:S(2)}, u32[]{:S(2)}) collective-permute-start(bf16[576,128]{1,0:T(8,128)(2,1)} %get-tuple-element.23), channel_id=1, source_target_pairs={{0,1},{1,0},{2,3},{3,2},{4,5},{5,4},{6,7},{7,6},{10,11},{11,10},{8... | collective-permute-start | bytes 442376 | tf_op jit(solution)/shard_map/ppermute | solution.py:264
  51.4 17.8 %collective-permute-start.1 = (bf16[576,128]{1,0:T(8,128)(2,1)}, bf16[576,128]{1,0:T(8,128)(2,1)S(1)}, u32[]{:S(2)}, u32[]{:S(2)}) collective-permute-start(bf16[576,128]{1,0:T(8,128)(2,1)} %get-tuple-element.24), channel_id=1, source_target_pairs={{0,2},{1,3},{2,0},{3,1},{4,6},{5,7},{6,4},{7,5},{10,8},{11,9},{8,1... | collective-permute-start | bytes 442376 | tf_op jit(solution)/shard_map/ppermute | solution.py:264
  56.0 13.2 %collective-permute-start.2 = (bf16[576,128]{1,0:T(8,128)(2,1)}, bf16[576,128]{1,0:T(8,128)(2,1)S(1)}, u32[]{:S(2)}, u32[]{:S(2)}) collective-permute-start(bf16[576,128]{1,0:T(8,128)(2,1)} %get-tuple-element.25), channel_id=1, source_target_pairs={{0,3},{1,2},{2,1},{3,0},{4,7},{5,6},{6,5},{7,4},{10,9},{11,8},{8,1... | collective-permute-start | bytes 442376 | tf_op jit(solution)/shard_map/ppermute | solution.py:264
  69.2 0.9 copy-start
  101.3 24.1 %copy-start.1 = (bf16[576,128]{1,0:T(8,128)(2,1)S(1)}, bf16[576,128]{1,0:T(8,128)(2,1)}, u32[]{:S(2)}) copy-start(bf16[576,128]{1,0:T(8,128)(2,1)} %get-tuple-element.22.refs_0_) | copy-start | bytes 442372
  144.2 24.1 %all-to-all-start.5 = ((bf16[64,8,128]{2,1,0:T(8,128)(2,1)}), bf16[64,8,128]{2,1,0:T(8,128)(2,1)S(1)}, u32[]{:S(2)}, u32[]{:S(2)}) async-start(bf16[64,8,128]{2,1,0:T(8,128)(2,1)} %bitcast.16), calls=%async_computation.5 | async-start | bytes 262144 | tf_op jit(solution)/shard_map/all_to_all | solution.py:232
  151.8 9.6 %collective-permute-start.3 = (bf16[576,128]{1,0:T(8,128)(2,1)S(1)}, bf16[576,128]{1,0:T(8,128)(2,1)S(1)}, u32[]{:S(2)}, u32[]{:S(2)}) collective-permute-start(bf16[576,128]{1,0:T(8,128)(2,1)S(1)} %get-tuple-element.29), channel_id=1, source_target_pairs={{0,1},{1,0},{2,3},{3,2},{4,5},{5,4},{6,7},{7,6},{10,11},{11,10},{8... | collective-permute-start | bytes 442376 | tf_op jit(solution)/shard_map/ppermute | solution.py:264
  154.0 9.6 %collective-permute-start.4 = (bf16[576,128]{1,0:T(8,128)(2,1)S(1)}, bf16[576,128]{1,0:T(8,128)(2,1)S(1)}, u32[]{:S(2)}, u32[]{:S(2)}) collective-permute-start(bf16[576,128]{1,0:T(8,128)(2,1)S(1)} %get-tuple-element.30), channel_id=1, source_target_pairs={{0,2},{1,3},{2,0},{3,1},{4,6},{5,7},{6,4},{7,5},{10,8},{11,9},{8,1... | collective-permute-start | bytes 442376 | tf_op jit(solution)/shard_map/ppermute | solution.py:264
  156.0 11.1 %collective-permute-start.5 = (bf16[576,128]{1,0:T(8,128)(2,1)S(1)}, bf16[576,128]{1,0:T(8,128)(2,1)S(1)}, u32[]{:S(2)}, u32[]{:S(2)}) collective-permute-start(bf16[576,128]{1,0:T(8,128)(2,1)S(1)} %get-tuple-element.31), channel_id=1, source_target_pairs={{0,3},{1,2},{2,1},{3,0},{4,7},{5,6},{6,5},{7,4},{10,9},{11,8},{8,1... | collective-permute-start | bytes 442376 | tf_op jit(solution)/shard_map/ppermute | solution.py:264
  167.0 1.3 copy-start.2

commit v6 on v5

--- a/solution.py
+++ b/solution.py
@@ -67,53 +67,66 @@
         held_ref[m * hidden : (m + 1) * hidden, :] = mm(ref[...], eye, 0, 0).astype(BF16)
     held_ref[2 * hidden : 3 * hidden, :] = down_ref[...]
     for k, chunk_ref in enumerate(chunk_refs):
-        peer = near_ref[0] ^ k
+        peer = (near_ref[0] & 15) ^ k
         for m in range(3):
             at = pl.multiple_of(m * hidden + peer * piece, piece)
             chunk_ref[m * piece : (m + 1) * piece, :] = held_ref[pl.ds(at, piece), :]
 
 
-def spread_kernel(cap, local, recv_ref, out_ref):
+def spread_kernel(cap, local, recv_ref, out_ref, scaled_ref):
     padded = recv_ref.shape[0]
-    width = out_ref.shape[1]
-    slots = padded // PAD * cap
+    slots, width = scaled_ref.shape
     s, r = iota((slots, padded), 0), iota((slots, padded), 1)
     keep = one_hot(((r >> 3) * cap + (r & 7) == s) & ((r & 7) < cap))
     rows = mm(keep, recv_ref[...], 1, 0).astype(BF16)
     for p in range(local):
-        at = p * 2 * slots
-        out_ref[at : at + slots, :] = rows[:, :width]
-        out_ref[at + slots : at + 2 * slots, :] = rows[:, width:]
-
-
-def rows_of(held_ref, near_ref, k, slots, scaled):
-    at = pl.multiple_of((near_ref[0] ^ k) * (2 * slots) + slots * scaled, 16)
-    return held_ref[pl.ds(at, slots), :]
-
-
-def partial_kernel(slots, strided, near_ref, held_ref, *refs):
+        out_ref[p * slots : (p + 1) * slots, :] = rows[:, :width]
+    scaled_ref[...] = rows[:, width:]
+
+
+def rows_of(held_ref, me_ref, k, slots):
+    return held_ref[pl.ds(pl.multiple_of(((me_ref[0] & 15) ^ k) * slots, 16), slots), :]
+
+
+def partial_kernel(slots, strided, me_ref, held_ref, *refs):
     *weight_refs, part_ref = refs
     piece = weight_refs[0].shape[0] // 3
     chunk = piece // strided
-    for m in range(3):
+    for m in range(2):
         total = None
         for k, weight_ref in enumerate(weight_refs):
-            rows = rows_of(held_ref, near_ref, k, slots, m // 2)
+            rows = rows_of(held_ref, me_ref, k, slots)
             term = mm(weight_ref[m * piece : (m + 1) * piece, :], rows, 1, 1)
             total = term if total is None else total + term
         total = total.astype(BF16)
         for q in range(strided):
-            to = (q * 3 + m) * chunk
+            to = (q * 2 + m) * chunk
             part_ref[to : to + chunk, :] = total[q * chunk : (q + 1) * chunk, :]
 
 
-def act_kernel(strided, part_ref, out_ref):
+def upstream_kernel(n, me_ref, *refs):
+    scaled_refs, weight_refs, chunk_refs, held_ref = refs[:n], refs[n : 2 * n], refs[2 * n : -1], refs[-1]
+    piece = weight_refs[0].shape[0] // 3
+    chunk = chunk_refs[0].shape[0]
+    total = None
+    for scaled_ref, weight_ref in zip(scaled_refs, weight_refs):
+        term = mm(weight_ref[2 * piece :, :], scaled_ref[...], 1, 1)
+        total = term if total is None else total + term
+    held_ref[...] = total.astype(BF16)
+    for k, chunk_ref in enumerate(chunk_refs):
+        at = pl.multiple_of(((me_ref[0] >> 4) ^ k) * chunk, 16)
+        chunk_ref[...] = held_ref[pl.ds(at, chunk), :]
+
+
+def act_kernel(strided, part_ref, *refs):
+    *back_refs, out_ref, act_ref = refs
     n = part_ref.shape[0] // strided
-    chunk = n // 3
+    chunk = n // 2
     total = part_ref[0:n, :].astype(F32)
     for q in range(1, strided):
         total = total + part_ref[q * n : (q + 1) * n, :].astype(F32)
-    gate, up, back = (total[m * chunk : (m + 1) * chunk, :] for m in range(3))
+    gate, up = total[:chunk, :], total[chunk:, :]
+    back = functools.reduce(jnp.add, [ref[...].astype(F32) for ref in back_refs])
     sig = jax.nn.sigmoid(gate)
     silu = gate * sig
     act = (silu * up).astype(BF16)
@@ -121,36 +134,36 @@
     grad_u = (back * silu).astype(BF16)
     score = jnp.sum(act.astype(F32) * back, axis=0, keepdims=True)
     score = jnp.where(iota((PAD, score.shape[1]), 0) == 0, score, 0.0).astype(BF16)
+    act_ref[...] = act
     m = out_ref.shape[0] // strided
     for q in range(strided):
         at = q * m
-        out_ref[at : at + chunk, :] = act
-        out_ref[at + chunk : at + 2 * chunk, :] = grad_g
-        out_ref[at + 2 * chunk : at + n, :] = grad_u
+        out_ref[at : at + chunk, :] = grad_g
+        out_ref[at + chunk : at + n, :] = grad_u
         out_ref[at + n : at + m, :] = score
 
 
-def acts_of(acts_ref, strided):
-    m = acts_ref.shape[0] // strided
-    chunk = (m - PAD) // 3
+def pair_of(pair_ref, strided):
+    m = pair_ref.shape[0] // strided
+    chunk = (m - PAD) // 2
     return [
         jnp.concatenate(
-            [acts_ref[q * m + k * chunk : q * m + (k + 1) * chunk, :] for q in range(strided)], axis=0
+            [pair_ref[q * m + k * chunk : q * m + (k + 1) * chunk, :] for q in range(strided)], axis=0
         )
-        for k in range(3)
+        for k in range(2)
     ]
 
 
-def term_kernel(strided, near_ref, acts_ref, *refs):
+def term_kernel(strided, me_ref, pair_ref, *refs):
     *weight_refs, out_ref = refs
-    slots = acts_ref.shape[1]
+    slots = pair_ref.shape[1]
     width = out_ref.shape[1]
     piece = weight_refs[0].shape[0] // 3
-    m = acts_ref.shape[0] // strided
-    _, grad_g, grad_u = acts_of(acts_ref, strided)
-    score = acts_ref[m - PAD : m, :].astype(F32)
+    m = pair_ref.shape[0] // strided
+    grad_g, grad_u = pair_of(pair_ref, strided)
+    score = pair_ref[m - PAD : m, :].astype(F32)
     for q in range(1, strided):
-        score = score + acts_ref[(q + 1) * m - PAD : (q + 1) * m, :].astype(F32)
+        score = score + pair_ref[(q + 1) * m - PAD : (q + 1) * m, :].astype(F32)
     lines = slots // width
     score = jnp.concatenate(
         [score[0:1, k * width : (k + 1) * width] for k in range(lines)]
@@ -159,21 +172,25 @@
     ).astype(BF16)
     for k, weight_ref in enumerate(weight_refs):
         gate_w, up_w = weight_ref[0:piece, :], weight_ref[piece : 2 * piece, :]
-        to = pl.multiple_of((near_ref[0] ^ k) * (slots + PAD), PAD)
+        to = pl.multiple_of(((me_ref[0] & 15) ^ k) * (slots + PAD), PAD)
         out_ref[pl.ds(to, slots), :] = (mm(grad_g, gate_w, 0, 0) + mm(grad_u, up_w, 0, 0)).astype(BF16)
         out_ref[pl.ds(to + slots, PAD), :] = score
 
 
-def grad_kernel(strided, near_ref, held_ref, acts_ref, *out_refs):
-    slots = acts_ref.shape[1]
+def grad_kernel(strided, local, me_ref, held_ref, pair_ref, *refs):
+    act_refs, scaled_refs = refs[:strided], refs[strided : strided + local]
+    out_refs, act_ref = refs[strided + local : -1], refs[-1]
+    slots = pair_ref.shape[1]
     piece = out_refs[0].shape[0] // 3
-    act, grad_g, grad_u = acts_of(acts_ref, strided)
+    chunk = piece // strided
+    grad_g, grad_u = pair_of(pair_ref, strided)
+    for k, ref in enumerate(act_refs):
+        act_ref[pl.ds(pl.multiple_of(((me_ref[0] >> 4) ^ k) * chunk, 16), chunk), :] = ref[...]
     for k, out_ref in enumerate(out_refs):
-        feat = rows_of(held_ref, near_ref, k, slots, 0)
-        scaled = rows_of(held_ref, near_ref, k, slots, 1)
+        feat = rows_of(held_ref, me_ref, k, slots)
         out_ref[0:piece, :] = mm(grad_g, feat, 1, 0).astype(BF16)
         out_ref[piece : 2 * piece, :] = mm(grad_u, feat, 1, 0).astype(BF16)
-        out_ref[2 * piece : 3 * piece, :] = mm(act, scaled, 1, 0).astype(BF16)
+        out_ref[2 * piece : 3 * piece, :] = mm(act_ref[...], scaled_refs[k][...], 1, 0).astype(BF16)
 
 
 def back_kernel(cap, slots, local, got_ref, send_ref):
@@ -200,7 +217,7 @@
     hidden = piece * len(got_refs)
     for k, got_ref in enumerate(got_refs):
         for m in range(3):
-            at = pl.multiple_of(m * hidden + (near_ref[0] ^ k) * piece, piece)
+            at = pl.multiple_of(m * hidden + ((near_ref[0] & 15) ^ k) * piece, piece)
             held_ref[pl.ds(at, piece), :] = got_ref[m * piece : (m + 1) * piece, :]
     eye = one_hot(iota((width, width), 0) == iota((width, width), 1))
     grad_gate_ref[...] = mm(eye, held_ref[0:hidden, :], 1, 1)
@@ -251,23 +268,24 @@
     return near, far
 
 
-def near_number(parts, local):
+def numbers(parts, local):
     strided = parts // local
     at = (lax.axis_index("attn") + parts - lax.axis_index("exp") % 2 * (local // 2)) % parts
-    return at % local ^ jnp.where(2 * (at // local) >= strided, local // 2, 0)
-
-
-def swap(chunks, near):
+    near = at % local ^ jnp.where(2 * (at // local) >= strided, local // 2, 0)
+    return (at // local * 16 + near).reshape(1)
+
+
+def swap(chunks, groups):
     out = [chunks[0]]
     for k in range(1, len(chunks)):
-        pairs = [(group[r], group[r ^ k]) for group in near for r in range(len(group))]
+        pairs = [(group[r], group[r ^ k]) for group in groups for r in range(len(group))]
         out.append(lax.ppermute(chunks[k], ("exp", "attn"), pairs))
     return out
 
 
 def call(kernel, operands, room=48 * 2**20, **options):
     params = pltpu.CompilerParams(vmem_limit_bytes=VMEM - room)
-    specs = [pl.BlockSpec(memory_space=pltpu.SMEM if x.shape == (1,) else pltpu.VMEM) for x in operands]
+    specs = [pl.BlockSpec(memory_space=pltpu.SMEM if x.ndim == 1 else pltpu.VMEM) for x in operands]
     return pl.pallas_call(kernel, in_specs=specs, compiler_params=params, **options)(*operands)
 
 
@@ -286,7 +304,7 @@
 
         kernel(ready, *refs[:n], *held, *refs[n + m : len(refs) - 1 - m])
 
-    space = [pltpu.SMEM if x.shape == (1,) else pltpu.VMEM for x in plain] + [pltpu.HBM] * len(fetched)
+    space = [pltpu.SMEM if x.ndim == 1 else pltpu.VMEM for x in plain] + [pltpu.HBM] * len(fetched)
     return pl.pallas_call(
         body,
         in_specs=[pl.BlockSpec(memory_space=x) for x in space],
@@ -313,7 +331,7 @@
     strided = parts // local
     piece = hidden // local
     near, far = device_groups(experts, parts, local)
-    me = near_number(parts, local).reshape(1)
+    me = numbers(parts, local)
     ids, weight = expert_ids.T, route_weight.T
     gate_w, up_w, down_w = gate_weight[0], up_weight[0], down_weight[0]
 
@@ -334,38 +352,50 @@
         name="turn",
     )
     chunks = swap(chunks, near)
-    held = call(
+    chunk = piece // strided
+    held, scaled = call(
         functools.partial(spread_kernel, cap, local),
         (recv,),
-        out_shape=shape_of(local * 2 * slots, width),
+        out_shape=(shape_of(local * slots, width), shape_of(slots, width)),
         name="spread",
     )
     held = exchange(held, "attn", near)
+    scaled = swap([scaled] * local, near)
     part = call(
         functools.partial(partial_kernel, slots, strided),
         (me, held, *chunks),
-        out_shape=shape_of(3 * piece, slots),
+        out_shape=shape_of(2 * piece, slots),
         name="partial",
     )
     part = exchange(part, "attn", far)
-    acts = call(
+    backs = call(
+        functools.partial(upstream_kernel, local),
+        (me, *scaled, *chunks),
+        out_shape=(shape_of(chunk, slots),) * strided,
+        scratch_shapes=[pltpu.VMEM((piece, slots), BF16)],
+        name="upstream",
+    )
+    backs = swap(backs, far)
+    pair, act = call(
         functools.partial(act_kernel, strided),
-        (part,),
-        out_shape=shape_of(3 * piece + strided * PAD, slots),
+        (part, *backs),
+        out_shape=(shape_of(2 * piece + strided * PAD, slots), shape_of(chunk, slots)),
         name="acts",
     )
-    acts = exchange(acts, "attn", far)
+    pair = exchange(pair, "attn", far)
+    act = swap([act] * strided, far)
     terms = call(
         functools.partial(term_kernel, strided),
-        (me, acts, *chunks),
+        (me, pair, *chunks),
         out_shape=shape_of(local * (slots + PAD), width),
         name="terms",
     )
     terms = exchange(terms, "attn", near)
     got = call(
-        functools.partial(grad_kernel, strided),
-        (me, held, acts),
+        functools.partial(grad_kernel, strided, local),
+        (me, held, pair, *act, *scaled),
         out_shape=(shape_of(3 * piece, width),) * local,
+        scratch_shapes=[pltpu.VMEM((piece, slots), BF16)],
         name="grads",
     )
     got = swap(got, near)

time: 170 us -> 205 us (1.21); the launches traced: 169 us -> 202 us
  starting transfers between devices: 35.9 us -> 80.2 us
  blocking collectives: 102 us -> 73.8 us
  waiting for transfers between devices: 16.9 us -> 31.6 us
    ppermute x6 -> x15, starting transfers between devices: 19.5 us -> 58.2 us  [swap(): out.append(lax.ppermute(chunks[k], ('exp', 'attn'), pairs))]
    all_to_all x4 -> x3, blocking collectives: 102 us -> 73.8 us  [exchange(): lax.all_to_all(blocks, axis, split_axis=0, concat_axis=0, tiled=True, axi...]
    ppermute x6 -> x15, waiting for transfers between devices: 16.9 us -> 31.6 us  [swap(): out.append(lax.ppermute(chunks[k], ('exp', 'attn'), pairs))]
    all_to_all x2 -> x3, starting transfers between devices: 16.4 us -> 22 us  [exchange(): lax.all_to_all(blocks, axis, split_axis=0, concat_axis=0, tiled=True, axi...]
    pallas_call x8 -> x9, Pallas kernels: 8.88 us -> 9.35 us  [call(): pl.pallas_call(kernel, in_specs=specs, compiler_params=params, **options)]
  transfers between devices with their start and end apart: 8 -> 18, of which waited for: 4 -> 9; matrix products, arithmetic and copies ran while one was open for 0% -> 0% of each run, Pallas kernels for 3% -> 3%
where the time goes in v6:
time: 205 us; the launch traced here: 202 us
  starting transfers between devices  80.2 us (39%)
  blocking collectives  73.8 us (36%)
  waiting for transfers between devices  31.6 us (15%)
  Pallas kernels  13.5 us (7%)
    all_to_all x3, blocking collectives, exchange(): lax.all_to_all(blocks, axis, split_axis=0, concat_axis=0, tiled=True, axi...  73.8 us
    ppermute x15, starting transfers between devices, swap(): out.append(lax.ppermute(chunks[k], ('exp', 'attn'), pairs))  58.2 us
    ppermute x15, waiting for transfers between devices, swap(): out.append(lax.ppermute(chunks[k], ('exp', 'attn'), pairs))  31.6 us
    all_to_all x3, starting transfers between devices, exchange(): lax.all_to_all(blocks, axis, split_axis=0, concat_axis=0, tiled=True, axi...  22 us
    pallas_call x9, Pallas kernels, call(): pl.pallas_call(kernel, in_specs=specs, compiler_params=params, **options)  9.35 us
    pallas_call x2, Pallas kernels, call_fetching(): pl.pallas_call(body, in_specs=[pl.BlockSpec(memory_space=x) for x in spac...  4.17 us
  transfers between devices with their start and end apart: 18, of which 9 were waited for; matrix products, arithmetic and copies ran while one was open for 0% of the time, Pallas kernels for 3%

profile of v6, /device:TPU:1, one launch (start us, length us, event | category | flops | bytes accessed | tf_op | source)
XLA Modules:
  0.0 201.5 jit_solution(17226099491639743723)
XLA Ops:
  0.6 1.9 pack.1
  2.6 31.4 %all_to_all.30 = bf16[64,8,256]{2,1,0:T(8,128)(2,1)S(1)} all-to-all(bf16[64,8,256]{2,1,0:T(8,128)(2,1)} %bitcast.30), channel_id=1, replica_groups=mesh['exp'=64,'attn'=16] {'exp'}, dimensions={0} | all-to-all | bytes 524288 | tf_op jit(solution)/shard_map/all_to_all | solution.py:249
  35.6 10.6 %all-to-all-start.1 = ((bf16[4,384,128]{2,1,0:T(8,128)(2,1)}), bf16[4,384,128]{2,1,0:T(8,128)(2,1)}, u32[]{:S(2)}, u32[]{:S(2)}) async-start(bf16[4,384,128]{2,1,0:T(8,128)(2,1)} %bitcast.5), calls=%async_computation.1 | async-start | bytes 786432 | tf_op jit(solution)/shard_map/all_to_all | solution.py:249
  46.2 2.2 %turn.1 = (bf16[576,128]{1,0:T(8,128)(2,1)}, bf16[576,128]{1,0:T(8,128)(2,1)}, bf16[576,128]{1,0:T(8,128)(2,1)}, bf16[576,128]{1,0:T(8,128)(2,1)}) custom-call(s32[1]{0:T(128)} %bitcast.2.refs_0_.me_ref.near_ref, bf16[128,768]{1,0:T(8,128)(2,1)} %bitcast.31, bf16[128,768]{1,0:T(8,128)(2,1)} %bitcast.32, bf16[768,128]{1,0:T(8,128)(2,1)} %bitcast.33), custom_call_target="tpu_custom_call" | custom-call | tf_op jit(solution)/shard_map/turn/pallas_call | solution.py:308
  48.5 3.4 %collective-permute-start = (bf16[576,128]{1,0:T(8,128)(2,1)}, bf16[576,128]{1,0:T(8,128)(2,1)S(1)}, u32[]{:S(2)}, u32[]{:S(2)}) collective-permute-start(bf16[576,128]{1,0:T(8,128)(2,1)} %get-tuple-element.32), channel_id=1, source_target_pairs={{0,1},{1,0},{2,3},{3,2},{4,5},{5,4},{6,7},{7,6},{10,11},{11,10},{8... | collective-permute-start | bytes 442376 | tf_op jit(solution)/shard_map/ppermute | solution.py:282
  51.8 4.5 %collective-permute-start.1 = (bf16[576,128]{1,0:T(8,128)(2,1)}, bf16[576,128]{1,0:T(8,128)(2,1)S(1)}, u32[]{:S(2)}, u32[]{:S(2)}) collective-permute-start(bf16[576,128]{1,0:T(8,128)(2,1)} %get-tuple-element.33), channel_id=1, source_target_pairs={{0,2},{1,3},{2,0},{3,1},{4,6},{5,7},{6,4},{7,5},{10,8},{11,9},{8,1... | collective-permute-start | bytes 442376 | tf_op jit(solution)/shard_map/ppermute | solution.py:282
  56.4 1.9 collective-permute-start.2
  58.3 5.0 %collective-permute-done.1.refs_2_.refs_6_ = bf16[576,128]{1,0:T(8,128)(2,1)S(1)} collective-permute-done((bf16[576,128]{1,0:T(8,128)(2,1)}, bf16[576,128]{1,0:T(8,128)(2,1)S(1)}, u32[]{:S(2)}, u32[]{:S(2)}) %collective-permute-start.1) | collective-permute-done | bytes 147488 | tf_op jit(solution)/shard_map/ppermute | solution.py:282
  63.4 3.1 %collective-permute-done.2.refs_3_.refs_7_ = bf16[576,128]{1,0:T(8,128)(2,1)S(1)} collective-permute-done((bf16[576,128]{1,0:T(8,128)(2,1)}, bf16[576,128]{1,0:T(8,128)(2,1)S(1)}, u32[]{:S(2)}, u32[]{:S(2)}) %collective-permute-start.2) | collective-permute-done | bytes 147488 | tf_op jit(solution)/shard_map/ppermute | solution.py:282
  67.3 2.2 %partial.1 = bf16[384,384]{1,0:T(8,128)(2,1)} custom-call(s32[1]{0:T(128)} %bitcast.2.refs_0_.me_ref.near_ref, bf16[1536,128]{1,0:T(8,128)(2,1)} %bitcast.6.held_ref, bf16[576,128]{1,0:T(8,128)(2,1)S(1)} %copy-done, bf16[576,128]{1,0:T(8,128)(2,1)S(1)} %collective-permute-done.refs_1_.refs_5_, bf16[576,128]{1,0:T(8,128)(2,1)S(1)} %collective-permute-done.1.refs_2_.refs_6_, ...), custom_call_target="tpu_custom_call" | custom-call | tf_op jit(solution)/shard_map/partial/pallas_call | solution.py:289
  69.6 5.2 %all-to-all-start.2 = ((bf16[4,96,384]{2,1,0:T(8,128)(2,1)}), bf16[4,96,384]{2,1,0:T(8,128)(2,1)S(1)}, u32[]{:S(2)}, u32[]{:S(2)}) async-start(bf16[4,96,384]{2,1,0:T(8,128)(2,1)} %bitcast.10), calls=%async_computation.2 | async-start | bytes 589824 | tf_op jit(solution)/shard_map/all_to_all | solution.py:249
  74.8 6.9 %collective-permute-start.5 = (bf16[384,128]{1,0:T(8,128)(2,1)S(1)}, bf16[384,128]{1,0:T(8,128)(2,1)S(1)}, u32[]{:S(2)}, u32[]{:S(2)}) collective-permute-start(bf16[384,128]{1,0:T(8,128)(2,1)S(1)} %copy-done.3), channel_id=1, source_target_pairs={{0,3},{1,2},{2,1},{3,0},{4,7},{5,6},{6,5},{7,4},{10,9},{11,8},{8,1... | collective-permute-start | bytes 294920 | tf_op jit(solution)/shard_map/ppermute | solution.py:282
  81.6 2.2 %collective-permute-start.4 = (bf16[384,128]{1,0:T(8,128)(2,1)S(1)}, bf16[384,128]{1,0:T(8,128)(2,1)S(1)}, u32[]{:S(2)}, u32[]{:S(2)}) collective-permute-start(bf16[384,128]{1,0:T(8,128)(2,1)S(1)} %copy-done.3), channel_id=1, source_target_pairs={{0,2},{1,3},{2,0},{3,1},{4,6},{5,7},{6,4},{7,5},{10,8},{11,9},{8,1... | collective-permute-start | bytes 294920 | tf_op jit(solution)/shard_map/ppermute | solution.py:282
  83.8 2.8 %collective-permute-start.3 = (bf16[384,128]{1,0:T(8,128)(2,1)S(1)}, bf16[384,128]{1,0:T(8,128)(2,1)S(1)}, u32[]{:S(2)}, u32[]{:S(2)}) collective-permute-start(bf16[384,128]{1,0:T(8,128)(2,1)S(1)} %copy-done.3), channel_id=1, source_target_pairs={{0,1},{1,0},{2,3},{3,2},{4,5},{5,4},{6,7},{7,6},{10,11},{11,10},{8... | collective-permute-start | bytes 294920 | tf_op jit(solution)/shard_map/ppermute | solution.py:282
  86.7 5.2 %collective-permute-done.5.refs_3_.refs_7_ = bf16[384,128]{1,0:T(8,128)(2,1)S(1)} collective-permute-done((bf16[384,128]{1,0:T(8,128)(2,1)S(1)}, bf16[384,128]{1,0:T(8,128)(2,1)S(1)}, u32[]{:S(2)}, u32[]{:S(2)}) %collective-permute-start.5) | collective-permute-done | bytes 98336 | tf_op jit(solution)/shard_map/ppermute | solution.py:282
  91.9 1.8 collective-permute-done.3.refs_1_.refs_5_
  94.0 7.9 %collective-permute-start.6 = (bf16[48,384]{1,0:T(8,128)(2,1)S(1)}, bf16[48,384]{1,0:T(8,128)(2,1)S(1)}, u32[]{:S(2)}, u32[]{:S(2)}) collective-permute-start(bf16[48,384]{1,0:T(8,128)(2,1)S(1)} %get-tuple-element.37), channel_id=1, source_target_pairs={{0,4},{4,0},{10,14},{14,10},{1,5},{5,1},{11,15},{15,11},{2,6},{6,2... | collective-permute-start | bytes 110600 | tf_op jit(solution)/shard_map/ppermute | solution.py:282
  101.9 1.9 collective-permute-start.7
  103.8 4.0 %collective-permute-start.8 = (bf16[48,384]{1,0:T(8,128)(2,1)S(1)}, bf16[48,384]{1,0:T(8,128)(2,1)S(1)}, u32[]{:S(2)}, u32[]{:S(2)}) collective-permute-start(bf16[48,384]{1,0:T(8,128)(2,1)S(1)} %get-tuple-element.39), channel_id=1, source_target_pairs={{0,14},{4,10},{10,4},{14,0},{1,15},{5,11},{11,5},{15,1},{2,12},{6,... | collective-permute-start | bytes 110600 | tf_op jit(solution)/shard_map/ppermute | solution.py:282
  107.8 4.5 %collective-permute-done.7.refs_2_ = bf16[48,384]{1,0:T(8,128)(2,1)S(1)} collective-permute-done((bf16[48,384]{1,0:T(8,128)(2,1)S(1)}, bf16[48,384]{1,0:T(8,128)(2,1)S(1)}, u32[]{:S(2)}, u32[]{:S(2)}) %collective-permute-start.7) | collective-permute-done | bytes 36896 | tf_op jit(solution)/shard_map/ppermute | solution.py:282
  112.4 28.1 %all_to_all.31 = bf16[4,104,384]{2,1,0:T(8,128)(2,1)S(1)} all-to-all(bf16[4,104,384]{2,1,0:T(8,128)(2,1)S(1)} %bitcast.29), channel_id=1, replica_groups={{0,4,10,14},{1,5,11,15},{2,6,8,12},{3,7,9,13},{18,22,28,16},{19,23,29,1..., dimensions={0} | all-to-all | bytes 638976 | tf_op jit(solution)/shard_map/all_to_all | solution.py:249
  141.1 14.3 %all_to_all.32 = bf16[4,392,128]{2,1,0:T(8,128)(2,1)S(1)} all-to-all(bf16[4,392,128]{2,1,0:T(8,128)(2,1)S(1)} %bitcast.24), channel_id=1, replica_groups={{0,1,2,3},{4,5,6,7},{10,11,8,9},{14,15,12,13},{18,19,20,21},{22,23,24,2..., dimensions={0} | all-to-all | bytes 802816 | tf_op jit(solution)/shard_map/all_to_all | solution.py:249
  156.6 6.2 %all-to-all-start.5 = ((bf16[64,8,128]{2,1,0:T(8,128)(2,1)}), bf16[64,8,128]{2,1,0:T(8,128)(2,1)S(1)}, u32[]{:S(2)}, u32[]{:S(2)}) async-start(bf16[64,8,128]{2,1,0:T(8,128)(2,1)} %bitcast.16), calls=%async_computation.5 | async-start | bytes 262144 | tf_op jit(solution)/shard_map/all_to_all | solution.py:249
  162.8 2.6 %collective-permute-start.11 = (bf16[48,384]{1,0:T(8,128)(2,1)S(1)}, bf16[48,384]{1,0:T(8,128)(2,1)S(1)}, u32[]{:S(2)}, u32[]{:S(2)}) collective-permute-start(bf16[48,384]{1,0:T(8,128)(2,1)S(1)} %get-tuple-element.43.refs_0_), channel_id=1, source_target_pairs={{0,14},{4,10},{10,4},{14,0},{1,15},{5,11},{11,5},{15,1},{2,12},{6,... | collective-permute-start | bytes 110600 | tf_op jit(solution)/shard_map/ppermute | solution.py:282
  165.4 7.3 %collective-permute-start.10 = (bf16[48,384]{1,0:T(8,128)(2,1)S(1)}, bf16[48,384]{1,0:T(8,128)(2,1)S(1)}, u32[]{:S(2)}, u32[]{:S(2)}) collective-permute-start(bf16[48,384]{1,0:T(8,128)(2,1)S(1)} %get-tuple-element.43.refs_0_), channel_id=1, source_target_pairs={{0,10},{4,14},{10,0},{14,4},{1,11},{5,15},{11,1},{15,5},{2,8},{6,1... | collective-permute-start | bytes 110600 | tf_op jit(solution)/shard_map/ppermute | solution.py:282
  172.8 3.2 %collective-permute-start.9 = (bf16[48,384]{1,0:T(8,128)(2,1)S(1)}, bf16[48,384]{1,0:T(8,128)(2,1)S(1)}, u32[]{:S(2)}, u32[]{:S(2)}) collective-permute-start(bf16[48,384]{1,0:T(8,128)(2,1)S(1)} %get-tuple-element.43.refs_0_), channel_id=1, source_target_pairs={{0,4},{4,0},{10,14},{14,10},{1,5},{5,1},{11,15},{15,11},{2,6},{6,2... | collective-permute-start | bytes 110600 | tf_op jit(solution)/shard_map/ppermute | solution.py:282
  176.2 6.3 %collective-permute-done.9.refs_1_ = bf16[48,384]{1,0:T(8,128)(2,1)S(1)} collective-permute-done((bf16[48,384]{1,0:T(8,128)(2,1)S(1)}, bf16[48,384]{1,0:T(8,128)(2,1)S(1)}, u32[]{:S(2)}, u32[]{:S(2)}) %collective-permute-start.9) | collective-permute-done | bytes 36896 | tf_op jit(solution)/shard_map/ppermute | solution.py:282
  184.2 2.8 %collective-permute-start.12 = (bf16[576,128]{1,0:T(8,128)(2,1)S(1)}, bf16[576,128]{1,0:T(8,128)(2,1)S(1)}, u32[]{:S(2)}, u32[]{:S(2)}) collective-permute-start(bf16[576,128]{1,0:T(8,128)(2,1)S(1)} %get-tuple-element.45), channel_id=1, source_target_pairs={{0,1},{1,0},{2,3},{3,2},{4,5},{5,4},{6,7},{7,6},{10,11},{11,10},{8... | collective-permute-start | bytes 442376 | tf_op jit(solution)/shard_map/ppermute | solution.py:282
  187.0 1.9 collective-permute-start.13
  188.9 4.9 %collective-permute-start.14 = (bf16[576,128]{1,0:T(8,128)(2,1)S(1)}, bf16[576,128]{1,0:T(8,128)(2,1)S(1)}, u32[]{:S(2)}, u32[]{:S(2)}) collective-permute-start(bf16[576,128]{1,0:T(8,128)(2,1)S(1)} %get-tuple-element.47), channel_id=1, source_target_pairs={{0,3},{1,2},{2,1},{3,0},{4,7},{5,6},{6,5},{7,4},{10,9},{11,8},{8,1... | collective-permute-start | bytes 442376 | tf_op jit(solution)/shard_map/ppermute | solution.py:282
  193.8 3.6 %collective-permute-done.13.refs_2_ = bf16[576,128]{1,0:T(8,128)(2,1)S(1)} collective-permute-done((bf16[576,128]{1,0:T(8,128)(2,1)S(1)}, bf16[576,128]{1,0:T(8,128)(2,1)S(1)}, u32[]{:S(2)}, u32[]{:S(2)}) %collective-permute-start.13) | collective-permute-done | bytes 147488 | tf_op jit(solution)/shard_map/ppermute | solution.py:282
  197.4 1.8 collective-permute-done.14.refs_3_
  (28 shorter events, 8.9 us)
Async XLA Ops:
  35.0 0.6 copy-start.2
  35.6 30.8 %all-to-all-start.1 = ((bf16[4,384,128]{2,1,0:T(8,128)(2,1)}), bf16[4,384,128]{2,1,0:T(8,128)(2,1)}, u32[]{:S(2)}, u32[]{:S(2)}) async-start(bf16[4,384,128]{2,1,0:T(8,128)(2,1)} %bitcast.5), calls=%async_computation.1 | async-start | bytes 786432 | tf_op jit(solution)/shard_map/all_to_all | solution.py:249
  48.5 9.8 %collective-permute-start = (bf16[576,128]{1,0:T(8,128)(2,1)}, bf16[576,128]{1,0:T(8,128)(2,1)S(1)}, u32[]{:S(2)}, u32[]{:S(2)}) collective-permute-start(bf16[576,128]{1,0:T(8,128)(2,1)} %get-tuple-element.32), channel_id=1, source_target_pairs={{0,1},{1,0},{2,3},{3,2},{4,5},{5,4},{6,7},{7,6},{10,11},{11,10},{8... | collective-permute-start | bytes 442376 | tf_op jit(solution)/shard_map/ppermute | solution.py:282
  51.8 11.5 %collective-permute-start.1 = (bf16[576,128]{1,0:T(8,128)(2,1)}, bf16[576,128]{1,0:T(8,128)(2,1)S(1)}, u32[]{:S(2)}, u32[]{:S(2)}) collective-permute-start(bf16[576,128]{1,0:T(8,128)(2,1)} %get-tuple-element.33), channel_id=1, source_target_pairs={{0,2},{1,3},{2,0},{3,1},{4,6},{5,7},{6,4},{7,5},{10,8},{11,9},{8,1... | collective-permute-start | bytes 442376 | tf_op jit(solution)/shard_map/ppermute | solution.py:282
  56.4 10.0 %collective-permute-start.2 = (bf16[576,128]{1,0:T(8,128)(2,1)}, bf16[576,128]{1,0:T(8,128)(2,1)S(1)}, u32[]{:S(2)}, u32[]{:S(2)}) collective-permute-start(bf16[576,128]{1,0:T(8,128)(2,1)} %get-tuple-element.34), channel_id=1, source_target_pairs={{0,3},{1,2},{2,1},{3,0},{4,7},{5,6},{6,5},{7,4},{10,9},{11,8},{8,1... | collective-permute-start | bytes 442376 | tf_op jit(solution)/shard_map/ppermute | solution.py:282
  66.4 0.9 copy-start
  69.6 5.2 %copy-start.3 = (bf16[384,128]{1,0:T(8,128)(2,1)S(1)}, bf16[384,128]{1,0:T(8,128)(2,1)}, u32[]{:S(2)}) copy-start(bf16[384,128]{1,0:T(8,128)(2,1)} %copy-done.2) | copy-start | bytes 294916
  69.6 24.1 %copy-start.1 = (bf16[576,128]{1,0:T(8,128)(2,1)S(1)}, bf16[576,128]{1,0:T(8,128)(2,1)}, u32[]{:S(2)}) copy-start(bf16[576,128]{1,0:T(8,128)(2,1)} %get-tuple-element.31.refs_0_.refs_4_) | copy-start | bytes 442372
  69.6 42.7 %all-to-all-start.2 = ((bf16[4,96,384]{2,1,0:T(8,128)(2,1)}), bf16[4,96,384]{2,1,0:T(8,128)(2,1)S(1)}, u32[]{:S(2)}, u32[]{:S(2)}) async-start(bf16[4,96,384]{2,1,0:T(8,128)(2,1)} %bitcast.10), calls=%async_computation.2 | async-start | bytes 589824 | tf_op jit(solution)/shard_map/all_to_all | solution.py:249
  74.8 17.1 %collective-permute-start.5 = (bf16[384,128]{1,0:T(8,128)(2,1)S(1)}, bf16[384,128]{1,0:T(8,128)(2,1)S(1)}, u32[]{:S(2)}, u32[]{:S(2)}) collective-permute-start(bf16[384,128]{1,0:T(8,128)(2,1)S(1)} %copy-done.3), channel_id=1, source_target_pairs={{0,3},{1,2},{2,1},{3,0},{4,7},{5,6},{6,5},{7,4},{10,9},{11,8},{8,1... | collective-permute-start | bytes 294920 | tf_op jit(solution)/shard_map/ppermute | solution.py:282
  81.6 10.3 %collective-permute-start.4 = (bf16[384,128]{1,0:T(8,128)(2,1)S(1)}, bf16[384,128]{1,0:T(8,128)(2,1)S(1)}, u32[]{:S(2)}, u32[]{:S(2)}) collective-permute-start(bf16[384,128]{1,0:T(8,128)(2,1)S(1)} %copy-done.3), channel_id=1, source_target_pairs={{0,2},{1,3},{2,0},{3,1},{4,6},{5,7},{6,4},{7,5},{10,8},{11,9},{8,1... | collective-permute-start | bytes 294920 | tf_op jit(solution)/shard_map/ppermute | solution.py:282
  83.8 9.8 %collective-permute-start.3 = (bf16[384,128]{1,0:T(8,128)(2,1)S(1)}, bf16[384,128]{1,0:T(8,128)(2,1)S(1)}, u32[]{:S(2)}, u32[]{:S(2)}) collective-permute-start(bf16[384,128]{1,0:T(8,128)(2,1)S(1)} %copy-done.3), channel_id=1, source_target_pairs={{0,1},{1,0},{2,3},{3,2},{4,5},{5,4},{6,7},{7,6},{10,11},{11,10},{8... | collective-permute-start | bytes 294920 | tf_op jit(solution)/shard_map/ppermute | solution.py:282
  94.0 13.8 %collective-permute-start.6 = (bf16[48,384]{1,0:T(8,128)(2,1)S(1)}, bf16[48,384]{1,0:T(8,128)(2,1)S(1)}, u32[]{:S(2)}, u32[]{:S(2)}) collective-permute-start(bf16[48,384]{1,0:T(8,128)(2,1)S(1)} %get-tuple-element.37), channel_id=1, source_target_pairs={{0,4},{4,0},{10,14},{14,10},{1,5},{5,1},{11,15},{15,11},{2,6},{6,2... | collective-permute-start | bytes 110600 | tf_op jit(solution)/shard_map/ppermute | solution.py:282
  101.9 10.4 %collective-permute-start.7 = (bf16[48,384]{1,0:T(8,128)(2,1)S(1)}, bf16[48,384]{1,0:T(8,128)(2,1)S(1)}, u32[]{:S(2)}, u32[]{:S(2)}) collective-permute-start(bf16[48,384]{1,0:T(8,128)(2,1)S(1)} %get-tuple-element.38), channel_id=1, source_target_pairs={{0,10},{4,14},{10,0},{14,4},{1,11},{5,15},{11,1},{15,5},{2,8},{6,1... | collective-permute-start | bytes 110600 | tf_op jit(solution)/shard_map/ppermute | solution.py:282
  103.8 8.5 %collective-permute-start.8 = (bf16[48,384]{1,0:T(8,128)(2,1)S(1)}, bf16[48,384]{1,0:T(8,128)(2,1)S(1)}, u32[]{:S(2)}, u32[]{:S(2)}) collective-permute-start(bf16[48,384]{1,0:T(8,128)(2,1)S(1)} %get-tuple-element.39), channel_id=1, source_target_pairs={{0,14},{4,10},{10,4},{14,0},{1,15},{5,11},{11,5},{15,1},{2,12},{6,... | collective-permute-start | bytes 110600 | tf_op jit(solution)/shard_map/ppermute | solution.py:282
  156.6 44.0 %all-to-all-start.5 = ((bf16[64,8,128]{2,1,0:T(8,128)(2,1)}), bf16[64,8,128]{2,1,0:T(8,128)(2,1)S(1)}, u32[]{:S(2)}, u32[]{:S(2)}) async-start(bf16[64,8,128]{2,1,0:T(8,128)(2,1)} %bitcast.16), calls=%async_computation.5 | async-start | bytes 262144 | tf_op jit(solution)/shard_map/all_to_all | solution.py:249
  162.8 13.2 %collective-permute-start.11 = (bf16[48,384]{1,0:T(8,128)(2,1)S(1)}, bf16[48,384]{1,0:T(8,128)(2,1)S(1)}, u32[]{:S(2)}, u32[]{:S(2)}) collective-permute-start(bf16[48,384]{1,0:T(8,128)(2,1)S(1)} %get-tuple-element.43.refs_0_), channel_id=1, source_target_pairs={{0,14},{4,10},{10,4},{14,0},{1,15},{5,11},{11,5},{15,1},{2,12},{6,... | collective-permute-start | bytes 110600 | tf_op jit(solution)/shard_map/ppermute | solution.py:282
  165.4 10.8 %collective-permute-start.10 = (bf16[48,384]{1,0:T(8,128)(2,1)S(1)}, bf16[48,384]{1,0:T(8,128)(2,1)S(1)}, u32[]{:S(2)}, u32[]{:S(2)}) collective-permute-start(bf16[48,384]{1,0:T(8,128)(2,1)S(1)} %get-tuple-element.43.refs_0_), channel_id=1, source_target_pairs={{0,10},{4,14},{10,0},{14,4},{1,11},{5,15},{11,1},{15,5},{2,8},{6,1... | collective-permute-start | bytes 110600 | tf_op jit(solution)/shard_map/ppermute | solution.py:282
  172.8 9.8 %collective-permute-start.9 = (bf16[48,384]{1,0:T(8,128)(2,1)S(1)}, bf16[48,384]{1,0:T(8,128)(2,1)S(1)}, u32[]{:S(2)}, u32[]{:S(2)}) collective-permute-start(bf16[48,384]{1,0:T(8,128)(2,1)S(1)} %get-tuple-element.43.refs_0_), channel_id=1, source_target_pairs={{0,4},{4,0},{10,14},{14,10},{1,5},{5,1},{11,15},{15,11},{2,6},{6,2... | collective-permute-start | bytes 110600 | tf_op jit(solution)/shard_map/ppermute | solution.py:282
  184.2 9.6 %collective-permute-start.12 = (bf16[576,128]{1,0:T(8,128)(2,1)S(1)}, bf16[576,128]{1,0:T(8,128)(2,1)S(1)}, u32[]{:S(2)}, u32[]{:S(2)}) collective-permute-start(bf16[576,128]{1,0:T(8,128)(2,1)S(1)} %get-tuple-element.45), channel_id=1, source_target_pairs={{0,1},{1,0},{2,3},{3,2},{4,5},{5,4},{6,7},{7,6},{10,11},{11,10},{8... | collective-permute-start | bytes 442376 | tf_op jit(solution)/shard_map/ppermute | solution.py:282
  187.0 10.4 %collective-permute-start.13 = (bf16[576,128]{1,0:T(8,128)(2,1)S(1)}, bf16[576,128]{1,0:T(8,128)(2,1)S(1)}, u32[]{:S(2)}, u32[]{:S(2)}) collective-permute-start(bf16[576,128]{1,0:T(8,128)(2,1)S(1)} %get-tuple-element.46), channel_id=1, source_target_pairs={{0,2},{1,3},{2,0},{3,1},{4,6},{5,7},{6,4},{7,5},{10,8},{11,9},{8,1... | collective-permute-start | bytes 442376 | tf_op jit(solution)/shard_map/ppermute | solution.py:282
  188.9 10.3 %collective-permute-start.14 = (bf16[576,128]{1,0:T(8,128)(2,1)S(1)}, bf16[576,128]{1,0:T(8,128)(2,1)S(1)}, u32[]{:S(2)}, u32[]{:S(2)}) collective-permute-start(bf16[576,128]{1,0:T(8,128)(2,1)S(1)} %get-tuple-element.47), channel_id=1, source_target_pairs={{0,3},{1,2},{2,1},{3,0},{4,7},{5,6},{6,5},{7,4},{10,9},{11,8},{8,1... | collective-permute-start | bytes 442376 | tf_op jit(solution)/shard_map/ppermute | solution.py:282
  199.3 1.3 copy-start.4

commit v7 on v6

--- a/solution.py
+++ b/solution.py
@@ -119,7 +119,7 @@
 
 
 def act_kernel(strided, part_ref, *refs):
-    *back_refs, out_ref, act_ref = refs
+    *back_refs, out_ref = refs
     n = part_ref.shape[0] // strided
     chunk = n // 2
     total = part_ref[0:n, :].astype(F32)
@@ -134,36 +134,36 @@
     grad_u = (back * silu).astype(BF16)
     score = jnp.sum(act.astype(F32) * back, axis=0, keepdims=True)
     score = jnp.where(iota((PAD, score.shape[1]), 0) == 0, score, 0.0).astype(BF16)
-    act_ref[...] = act
     m = out_ref.shape[0] // strided
     for q in range(strided):
         at = q * m
         out_ref[at : at + chunk, :] = grad_g
         out_ref[at + chunk : at + n, :] = grad_u
-        out_ref[at + n : at + m, :] = score
-
-
-def pair_of(pair_ref, strided):
-    m = pair_ref.shape[0] // strided
-    chunk = (m - PAD) // 2
+        out_ref[at + n : at + n + chunk, :] = act
+        out_ref[at + n + chunk : at + m, :] = score
+
+
+def three_of(acts_ref, strided):
+    m = acts_ref.shape[0] // strided
+    chunk = (m - PAD) // 3
     return [
         jnp.concatenate(
-            [pair_ref[q * m + k * chunk : q * m + (k + 1) * chunk, :] for q in range(strided)], axis=0
+            [acts_ref[q * m + k * chunk : q * m + (k + 1) * chunk, :] for q in range(strided)], axis=0
         )
-        for k in range(2)
+        for k in range(3)
     ]
 
 
-def term_kernel(strided, me_ref, pair_ref, *refs):
+def term_kernel(strided, me_ref, acts_ref, *refs):
     *weight_refs, out_ref = refs
-    slots = pair_ref.shape[1]
+    slots = acts_ref.shape[1]
     width = out_ref.shape[1]
     piece = weight_refs[0].shape[0] // 3
-    m = pair_ref.shape[0] // strided
-    grad_g, grad_u = pair_of(pair_ref, strided)
-    score = pair_ref[m - PAD : m, :].astype(F32)
+    m = acts_ref.shape[0] // strided
+    grad_g, grad_u, _ = three_of(acts_ref, strided)
+    score = acts_ref[m - PAD : m, :].astype(F32)
     for q in range(1, strided):
-        score = score + pair_ref[(q + 1) * m - PAD : (q + 1) * m, :].astype(F32)
+        score = score + acts_ref[(q + 1) * m - PAD : (q + 1) * m, :].astype(F32)
     lines = slots // width
     score = jnp.concatenate(
         [score[0:1, k * width : (k + 1) * width] for k in range(lines)]
@@ -177,20 +177,16 @@
         out_ref[pl.ds(to + slots, PAD), :] = score
 
 
-def grad_kernel(strided, local, me_ref, held_ref, pair_ref, *refs):
-    act_refs, scaled_refs = refs[:strided], refs[strided : strided + local]
-    out_refs, act_ref = refs[strided + local : -1], refs[-1]
-    slots = pair_ref.shape[1]
+def grad_kernel(strided, local, me_ref, held_ref, acts_ref, *refs):
+    scaled_refs, out_refs = refs[:local], refs[local:]
+    slots = acts_ref.shape[1]
     piece = out_refs[0].shape[0] // 3
-    chunk = piece // strided
-    grad_g, grad_u = pair_of(pair_ref, strided)
-    for k, ref in enumerate(act_refs):
-        act_ref[pl.ds(pl.multiple_of(((me_ref[0] >> 4) ^ k) * chunk, 16), chunk), :] = ref[...]
+    grad_g, grad_u, act = three_of(acts_ref, strided)
     for k, out_ref in enumerate(out_refs):
         feat = rows_of(held_ref, me_ref, k, slots)
         out_ref[0:piece, :] = mm(grad_g, feat, 1, 0).astype(BF16)
         out_ref[piece : 2 * piece, :] = mm(grad_u, feat, 1, 0).astype(BF16)
-        out_ref[2 * piece : 3 * piece, :] = mm(act_ref[...], scaled_refs[k][...], 1, 0).astype(BF16)
+        out_ref[2 * piece : 3 * piece, :] = mm(act, scaled_refs[k][...], 1, 0).astype(BF16)
 
 
 def back_kernel(cap, slots, local, got_ref, send_ref):
@@ -376,26 +372,24 @@
         name="upstream",
     )
     backs = swap(backs, far)
-    pair, act = call(
+    acts = call(
         functools.partial(act_kernel, strided),
         (part, *backs),
-        out_shape=(shape_of(2 * piece + strided * PAD, slots), shape_of(chunk, slots)),
+        out_shape=shape_of(3 * piece + strided * PAD, slots),
         name="acts",
     )
-    pair = exchange(pair, "attn", far)
-    act = swap([act] * strided, far)
+    acts = exchange(acts, "attn", far)
     terms = call(
         functools.partial(term_kernel, strided),
-        (me, pair, *chunks),
+        (me, acts, *chunks),
         out_shape=shape_of(local * (slots + PAD), width),
         name="terms",
     )
     terms = exchange(terms, "attn", near)
     got = call(
         functools.partial(grad_kernel, strided, local),
-        (me, held, pair, *act, *scaled),
+        (me, held, acts, *scaled),
         out_shape=(shape_of(3 * piece, width),) * local,
-        scratch_shapes=[pltpu.VMEM((piece, slots), BF16)],
         name="grads",
     )
     got = swap(got, near)

time: 205 us -> 188 us (0.917); the launches traced: 202 us -> 187 us
  starting transfers between devices: 80.2 us -> 66.4 us
  waiting for transfers between devices: 31.6 us -> 25.6 us
  blocking collectives: 73.8 us -> 79 us
    ppermute x15 -> x12, starting transfers between devices: 58.2 us -> 44.5 us  [swap(): out.append(lax.ppermute(chunks[k], ('exp', 'attn'), pairs))]
    ppermute x15 -> x12, waiting for transfers between devices: 31.6 us -> 25.6 us  [swap(): out.append(lax.ppermute(chunks[k], ('exp', 'attn'), pairs))]
    all_to_all x3, blocking collectives: 73.8 us -> 79 us  [exchange(): lax.all_to_all(blocks, axis, split_axis=0, concat_axis=0, tiled=True, axi...]
  transfers between devices with their start and end apart: 18 -> 15, of which waited for: 9 -> 7; matrix products, arithmetic and copies ran while one was open for 0% -> 0% of each run, Pallas kernels for 3% -> 3%
where the time goes in v7:
time: 188 us; the launch traced here: 187 us
  blocking collectives  79 us (42%)
  starting transfers between devices  66.4 us (35%)
  waiting for transfers between devices  25.6 us (14%)
  Pallas kernels  13.5 us (7%)
    all_to_all x3, blocking collectives, exchange(): lax.all_to_all(blocks, axis, split_axis=0, concat_axis=0, tiled=True, axi...  79 us
    ppermute x12, starting transfers between devices, swap(): out.append(lax.ppermute(chunks[k], ('exp', 'attn'), pairs))  44.5 us
    ppermute x12, waiting for transfers between devices, swap(): out.append(lax.ppermute(chunks[k], ('exp', 'attn'), pairs))  25.6 us
    all_to_all x3, starting transfers between devices, exchange(): lax.all_to_all(blocks, axis, split_axis=0, concat_axis=0, tiled=True, axi...  21.9 us
    pallas_call x9, Pallas kernels, call(): pl.pallas_call(kernel, in_specs=specs, compiler_params=params, **options)  9.34 us
    pallas_call x2, Pallas kernels, call_fetching(): pl.pallas_call(body, in_specs=[pl.BlockSpec(memory_space=x) for x in spac...  4.16 us
  transfers between devices with their start and end apart: 15, of which 7 were waited for; matrix products, arithmetic and copies ran while one was open for 0% of the time, Pallas kernels for 3%

profile of v7, /device:TPU:1, one launch (start us, length us, event | category | flops | bytes accessed | tf_op | source)
XLA Modules:
  0.0 187.0 jit_solution(15033999203291868339)
XLA Ops:
  0.6 1.9 %pack.1 = (bf16[512,256]{1,0:T(8,128)(2,1)}, f32[6,128]{1,0:T(8,128)}) custom-call(s32[2,128]{1,0:T(2,128)} %bitcast.34, bf16[2,128]{1,0:T(2,128)(2,1)} %bitcast.35, bf16[128,128]{1,0:T(8,128)(2,1)} %refs_2_.1, bf16[128,128]{1,0:T(8,128)(2,1)} %refs_3_.1), custom_call_target="tpu_custom_call" | custom-call | tf_op jit(solution)/shard_map/pack/pallas_call | solution.py:304
  2.6 31.4 %all_to_all.30 = bf16[64,8,256]{2,1,0:T(8,128)(2,1)S(1)} all-to-all(bf16[64,8,256]{2,1,0:T(8,128)(2,1)} %bitcast.30), channel_id=1, replica_groups=mesh['exp'=64,'attn'=16] {'exp'}, dimensions={0} | all-to-all | bytes 524288 | tf_op jit(solution)/shard_map/all_to_all | solution.py:245
  33.9 1.0 spread.1
  35.6 10.6 %all-to-all-start.1 = ((bf16[4,384,128]{2,1,0:T(8,128)(2,1)}), bf16[4,384,128]{2,1,0:T(8,128)(2,1)}, u32[]{:S(2)}, u32[]{:S(2)}) async-start(bf16[4,384,128]{2,1,0:T(8,128)(2,1)} %bitcast.5), calls=%async_computation.1 | async-start | bytes 786432 | tf_op jit(solution)/shard_map/all_to_all | solution.py:245
  46.2 2.2 %turn.1 = (bf16[576,128]{1,0:T(8,128)(2,1)}, bf16[576,128]{1,0:T(8,128)(2,1)}, bf16[576,128]{1,0:T(8,128)(2,1)}, bf16[576,128]{1,0:T(8,128)(2,1)}) custom-call(s32[1]{0:T(128)} %bitcast.2.refs_0_.me_ref.near_ref, bf16[128,768]{1,0:T(8,128)(2,1)} %bitcast.31, bf16[128,768]{1,0:T(8,128)(2,1)} %bitcast.32, bf16[768,128]{1,0:T(8,128)(2,1)} %bitcast.33), custom_call_target="tpu_custom_call" | custom-call | tf_op jit(solution)/shard_map/turn/pallas_call | solution.py:304
  48.5 3.4 %collective-permute-start = (bf16[576,128]{1,0:T(8,128)(2,1)}, bf16[576,128]{1,0:T(8,128)(2,1)S(1)}, u32[]{:S(2)}, u32[]{:S(2)}) collective-permute-start(bf16[576,128]{1,0:T(8,128)(2,1)} %get-tuple-element.30), channel_id=1, source_target_pairs={{0,1},{1,0},{2,3},{3,2},{4,5},{5,4},{6,7},{7,6},{10,11},{11,10},{8... | collective-permute-start | bytes 442376 | tf_op jit(solution)/shard_map/ppermute | solution.py:278
  51.8 4.5 %collective-permute-start.1 = (bf16[576,128]{1,0:T(8,128)(2,1)}, bf16[576,128]{1,0:T(8,128)(2,1)S(1)}, u32[]{:S(2)}, u32[]{:S(2)}) collective-permute-start(bf16[576,128]{1,0:T(8,128)(2,1)} %get-tuple-element.31), channel_id=1, source_target_pairs={{0,2},{1,3},{2,0},{3,1},{4,6},{5,7},{6,4},{7,5},{10,8},{11,9},{8,1... | collective-permute-start | bytes 442376 | tf_op jit(solution)/shard_map/ppermute | solution.py:278
  56.4 1.9 %collective-permute-start.2 = (bf16[576,128]{1,0:T(8,128)(2,1)}, bf16[576,128]{1,0:T(8,128)(2,1)S(1)}, u32[]{:S(2)}, u32[]{:S(2)}) collective-permute-start(bf16[576,128]{1,0:T(8,128)(2,1)} %get-tuple-element.32), channel_id=1, source_target_pairs={{0,3},{1,2},{2,1},{3,0},{4,7},{5,6},{6,5},{7,4},{10,9},{11,8},{8,1... | collective-permute-start | bytes 442376 | tf_op jit(solution)/shard_map/ppermute | solution.py:278
  58.3 5.1 %collective-permute-done.1.refs_2_.refs_6_ = bf16[576,128]{1,0:T(8,128)(2,1)S(1)} collective-permute-done((bf16[576,128]{1,0:T(8,128)(2,1)}, bf16[576,128]{1,0:T(8,128)(2,1)S(1)}, u32[]{:S(2)}, u32[]{:S(2)}) %collective-permute-start.1) | collective-permute-done | bytes 147488 | tf_op jit(solution)/shard_map/ppermute | solution.py:278
  63.4 3.1 %collective-permute-done.2.refs_3_.refs_7_ = bf16[576,128]{1,0:T(8,128)(2,1)S(1)} collective-permute-done((bf16[576,128]{1,0:T(8,128)(2,1)}, bf16[576,128]{1,0:T(8,128)(2,1)S(1)}, u32[]{:S(2)}, u32[]{:S(2)}) %collective-permute-start.2) | collective-permute-done | bytes 147488 | tf_op jit(solution)/shard_map/ppermute | solution.py:278
  67.3 2.2 %partial.1 = bf16[384,384]{1,0:T(8,128)(2,1)} custom-call(s32[1]{0:T(128)} %bitcast.2.refs_0_.me_ref.near_ref, bf16[1536,128]{1,0:T(8,128)(2,1)} %bitcast.6.held_ref, bf16[576,128]{1,0:T(8,128)(2,1)S(1)} %copy-done, bf16[576,128]{1,0:T(8,128)(2,1)S(1)} %collective-permute-done.refs_1_.refs_5_, bf16[576,128]{1,0:T(8,128)(2,1)S(1)} %collective-permute-done.1.refs_2_.refs_6_, ...), custom_call_target="tpu_custom_call" | custom-call | tf_op jit(solution)/shard_map/partial/pallas_call | solution.py:285
  69.6 5.2 %all-to-all-start.2 = ((bf16[4,96,384]{2,1,0:T(8,128)(2,1)}), bf16[4,96,384]{2,1,0:T(8,128)(2,1)S(1)}, u32[]{:S(2)}, u32[]{:S(2)}) async-start(bf16[4,96,384]{2,1,0:T(8,128)(2,1)} %bitcast.10), calls=%async_computation.2 | async-start | bytes 589824 | tf_op jit(solution)/shard_map/all_to_all | solution.py:245
  74.7 3.9 %collective-permute-start.3 = (bf16[384,128]{1,0:T(8,128)(2,1)S(1)}, bf16[384,128]{1,0:T(8,128)(2,1)S(1)}, u32[]{:S(2)}, u32[]{:S(2)}) collective-permute-start(bf16[384,128]{1,0:T(8,128)(2,1)S(1)} %copy-done.3), channel_id=1, source_target_pairs={{0,1},{1,0},{2,3},{3,2},{4,5},{5,4},{6,7},{7,6},{10,11},{11,10},{8... | collective-permute-start | bytes 294920 | tf_op jit(solution)/shard_map/ppermute | solution.py:278
  78.6 6.1 %collective-permute-start.4 = (bf16[384,128]{1,0:T(8,128)(2,1)S(1)}, bf16[384,128]{1,0:T(8,128)(2,1)S(1)}, u32[]{:S(2)}, u32[]{:S(2)}) collective-permute-start(bf16[384,128]{1,0:T(8,128)(2,1)S(1)} %copy-done.3), channel_id=1, source_target_pairs={{0,2},{1,3},{2,0},{3,1},{4,6},{5,7},{6,4},{7,5},{10,8},{11,9},{8,1... | collective-permute-start | bytes 294920 | tf_op jit(solution)/shard_map/ppermute | solution.py:278
  84.7 1.9 %collective-permute-start.5 = (bf16[384,128]{1,0:T(8,128)(2,1)S(1)}, bf16[384,128]{1,0:T(8,128)(2,1)S(1)}, u32[]{:S(2)}, u32[]{:S(2)}) collective-permute-start(bf16[384,128]{1,0:T(8,128)(2,1)S(1)} %copy-done.3), channel_id=1, source_target_pairs={{0,3},{1,2},{2,1},{3,0},{4,7},{5,6},{6,5},{7,4},{10,9},{11,8},{8,1... | collective-permute-start | bytes 294920 | tf_op jit(solution)/shard_map/ppermute | solution.py:278
  86.6 3.8 %collective-permute-done.3.refs_1_ = bf16[384,128]{1,0:T(8,128)(2,1)S(1)} collective-permute-done((bf16[384,128]{1,0:T(8,128)(2,1)S(1)}, bf16[384,128]{1,0:T(8,128)(2,1)S(1)}, u32[]{:S(2)}, u32[]{:S(2)}) %collective-permute-start.3) | collective-permute-done | bytes 98336 | tf_op jit(solution)/shard_map/ppermute | solution.py:278
  90.5 3.5 %collective-permute-done.4.refs_2_ = bf16[384,128]{1,0:T(8,128)(2,1)S(1)} collective-permute-done((bf16[384,128]{1,0:T(8,128)(2,1)S(1)}, bf16[384,128]{1,0:T(8,128)(2,1)S(1)}, u32[]{:S(2)}, u32[]{:S(2)}) %collective-permute-start.4) | collective-permute-done | bytes 98336 | tf_op jit(solution)/shard_map/ppermute | solution.py:278
  94.3 7.3 %collective-permute-start.6 = (bf16[48,384]{1,0:T(8,128)(2,1)S(1)}, bf16[48,384]{1,0:T(8,128)(2,1)S(1)}, u32[]{:S(2)}, u32[]{:S(2)}) collective-permute-start(bf16[48,384]{1,0:T(8,128)(2,1)S(1)} %get-tuple-element.35), channel_id=1, source_target_pairs={{0,4},{4,0},{10,14},{14,10},{1,5},{5,1},{11,15},{15,11},{2,6},{6,2... | collective-permute-start | bytes 110600 | tf_op jit(solution)/shard_map/ppermute | solution.py:278
  101.6 3.4 %collective-permute-start.7 = (bf16[48,384]{1,0:T(8,128)(2,1)S(1)}, bf16[48,384]{1,0:T(8,128)(2,1)S(1)}, u32[]{:S(2)}, u32[]{:S(2)}) collective-permute-start(bf16[48,384]{1,0:T(8,128)(2,1)S(1)} %get-tuple-element.36), channel_id=1, source_target_pairs={{0,10},{4,14},{10,0},{14,4},{1,11},{5,15},{11,1},{15,5},{2,8},{6,1... | collective-permute-start | bytes 110600 | tf_op jit(solution)/shard_map/ppermute | solution.py:278
  105.0 2.5 %collective-permute-start.8 = (bf16[48,384]{1,0:T(8,128)(2,1)S(1)}, bf16[48,384]{1,0:T(8,128)(2,1)S(1)}, u32[]{:S(2)}, u32[]{:S(2)}) collective-permute-start(bf16[48,384]{1,0:T(8,128)(2,1)S(1)} %get-tuple-element.37), channel_id=1, source_target_pairs={{0,14},{4,10},{10,4},{14,0},{1,15},{5,11},{11,5},{15,1},{2,12},{6,... | collective-permute-start | bytes 110600 | tf_op jit(solution)/shard_map/ppermute | solution.py:278
  107.5 4.9 %collective-permute-done.7.refs_2_ = bf16[48,384]{1,0:T(8,128)(2,1)S(1)} collective-permute-done((bf16[48,384]{1,0:T(8,128)(2,1)S(1)}, bf16[48,384]{1,0:T(8,128)(2,1)S(1)}, u32[]{:S(2)}, u32[]{:S(2)}) %collective-permute-start.7) | collective-permute-done | bytes 36896 | tf_op jit(solution)/shard_map/ppermute | solution.py:278
  112.5 35.2 %all_to_all.31 = bf16[4,152,384]{2,1,0:T(8,128)(2,1)S(1)} all-to-all(bf16[4,152,384]{2,1,0:T(8,128)(2,1)S(1)} %bitcast.24), channel_id=1, replica_groups={{0,4,10,14},{1,5,11,15},{2,6,8,12},{3,7,9,13},{18,22,28,16},{19,23,29,1..., dimensions={0} | all-to-all | bytes 933888 | tf_op jit(solution)/shard_map/all_to_all | solution.py:245
  148.3 12.5 %all_to_all.32 = bf16[4,392,128]{2,1,0:T(8,128)(2,1)S(1)} all-to-all(bf16[4,392,128]{2,1,0:T(8,128)(2,1)S(1)} %bitcast.25), channel_id=1, replica_groups={{0,1,2,3},{4,5,6,7},{10,11,8,9},{14,15,12,13},{18,19,20,21},{22,23,24,2..., dimensions={0} | all-to-all | bytes 802816 | tf_op jit(solution)/shard_map/all_to_all | solution.py:245
  160.8 1.2 back.1
  162.0 6.1 %all-to-all-start.5 = ((bf16[64,8,128]{2,1,0:T(8,128)(2,1)}), bf16[64,8,128]{2,1,0:T(8,128)(2,1)S(1)}, u32[]{:S(2)}, u32[]{:S(2)}) async-start(bf16[64,8,128]{2,1,0:T(8,128)(2,1)} %bitcast.16), calls=%async_computation.5 | async-start | bytes 262144 | tf_op jit(solution)/shard_map/all_to_all | solution.py:245
  168.2 1.6 grads.1
  169.8 2.2 %collective-permute-start.9 = (bf16[576,128]{1,0:T(8,128)(2,1)S(1)}, bf16[576,128]{1,0:T(8,128)(2,1)S(1)}, u32[]{:S(2)}, u32[]{:S(2)}) collective-permute-start(bf16[576,128]{1,0:T(8,128)(2,1)S(1)} %get-tuple-element.41), channel_id=1, source_target_pairs={{0,1},{1,0},{2,3},{3,2},{4,5},{5,4},{6,7},{7,6},{10,11},{11,10},{8... | collective-permute-start | bytes 442376 | tf_op jit(solution)/shard_map/ppermute | solution.py:278
  172.0 2.5 %collective-permute-start.10 = (bf16[576,128]{1,0:T(8,128)(2,1)S(1)}, bf16[576,128]{1,0:T(8,128)(2,1)S(1)}, u32[]{:S(2)}, u32[]{:S(2)}) collective-permute-start(bf16[576,128]{1,0:T(8,128)(2,1)S(1)} %get-tuple-element.42), channel_id=1, source_target_pairs={{0,2},{1,3},{2,0},{3,1},{4,6},{5,7},{6,4},{7,5},{10,8},{11,9},{8,1... | collective-permute-start | bytes 442376 | tf_op jit(solution)/shard_map/ppermute | solution.py:278
  174.5 4.9 %collective-permute-start.11 = (bf16[576,128]{1,0:T(8,128)(2,1)S(1)}, bf16[576,128]{1,0:T(8,128)(2,1)S(1)}, u32[]{:S(2)}, u32[]{:S(2)}) collective-permute-start(bf16[576,128]{1,0:T(8,128)(2,1)S(1)} %get-tuple-element.43), channel_id=1, source_target_pairs={{0,3},{1,2},{2,1},{3,0},{4,7},{5,6},{6,5},{7,4},{10,9},{11,8},{8,1... | collective-permute-start | bytes 442376 | tf_op jit(solution)/shard_map/ppermute | solution.py:278
  179.4 2.3 %collective-permute-done.10.refs_2_ = bf16[576,128]{1,0:T(8,128)(2,1)S(1)} collective-permute-done((bf16[576,128]{1,0:T(8,128)(2,1)S(1)}, bf16[576,128]{1,0:T(8,128)(2,1)S(1)}, u32[]{:S(2)}, u32[]{:S(2)}) %collective-permute-start.10) | collective-permute-done | bytes 147488 | tf_op jit(solution)/shard_map/ppermute | solution.py:278
  181.7 3.0 %collective-permute-done.11.refs_3_ = bf16[576,128]{1,0:T(8,128)(2,1)S(1)} collective-permute-done((bf16[576,128]{1,0:T(8,128)(2,1)S(1)}, bf16[576,128]{1,0:T(8,128)(2,1)S(1)}, u32[]{:S(2)}, u32[]{:S(2)}) %collective-permute-start.11) | collective-permute-done | bytes 147488 | tf_op jit(solution)/shard_map/ppermute | solution.py:278
  184.7 1.3 out.1
  (22 shorter events, 3.6 us)
Async XLA Ops:
  35.0 0.6 copy-start.2
  35.6 30.8 %all-to-all-start.1 = ((bf16[4,384,128]{2,1,0:T(8,128)(2,1)}), bf16[4,384,128]{2,1,0:T(8,128)(2,1)}, u32[]{:S(2)}, u32[]{:S(2)}) async-start(bf16[4,384,128]{2,1,0:T(8,128)(2,1)} %bitcast.5), calls=%async_computation.1 | async-start | bytes 786432 | tf_op jit(solution)/shard_map/all_to_all | solution.py:245
  48.5 9.8 %collective-permute-start = (bf16[576,128]{1,0:T(8,128)(2,1)}, bf16[576,128]{1,0:T(8,128)(2,1)S(1)}, u32[]{:S(2)}, u32[]{:S(2)}) collective-permute-start(bf16[576,128]{1,0:T(8,128)(2,1)} %get-tuple-element.30), channel_id=1, source_target_pairs={{0,1},{1,0},{2,3},{3,2},{4,5},{5,4},{6,7},{7,6},{10,11},{11,10},{8... | collective-permute-start | bytes 442376 | tf_op jit(solution)/shard_map/ppermute | solution.py:278
  51.8 11.5 %collective-permute-start.1 = (bf16[576,128]{1,0:T(8,128)(2,1)}, bf16[576,128]{1,0:T(8,128)(2,1)S(1)}, u32[]{:S(2)}, u32[]{:S(2)}) collective-permute-start(bf16[576,128]{1,0:T(8,128)(2,1)} %get-tuple-element.31), channel_id=1, source_target_pairs={{0,2},{1,3},{2,0},{3,1},{4,6},{5,7},{6,4},{7,5},{10,8},{11,9},{8,1... | collective-permute-start | bytes 442376 | tf_op jit(solution)/shard_map/ppermute | solution.py:278
  56.4 10.1 %collective-permute-start.2 = (bf16[576,128]{1,0:T(8,128)(2,1)}, bf16[576,128]{1,0:T(8,128)(2,1)S(1)}, u32[]{:S(2)}, u32[]{:S(2)}) collective-permute-start(bf16[576,128]{1,0:T(8,128)(2,1)} %get-tuple-element.32), channel_id=1, source_target_pairs={{0,3},{1,2},{2,1},{3,0},{4,7},{5,6},{6,5},{7,4},{10,9},{11,8},{8,1... | collective-permute-start | bytes 442376 | tf_op jit(solution)/shard_map/ppermute | solution.py:278
  66.4 0.9 copy-start
  69.6 5.2 %copy-start.3 = (bf16[384,128]{1,0:T(8,128)(2,1)S(1)}, bf16[384,128]{1,0:T(8,128)(2,1)}, u32[]{:S(2)}) copy-start(bf16[384,128]{1,0:T(8,128)(2,1)} %copy-done.2) | copy-start | bytes 294916
  69.6 24.4 %copy-start.1 = (bf16[576,128]{1,0:T(8,128)(2,1)S(1)}, bf16[576,128]{1,0:T(8,128)(2,1)}, u32[]{:S(2)}) copy-start(bf16[576,128]{1,0:T(8,128)(2,1)} %get-tuple-element.29.refs_0_.refs_4_) | copy-start | bytes 442372
  69.6 42.9 %all-to-all-start.2 = ((bf16[4,96,384]{2,1,0:T(8,128)(2,1)}), bf16[4,96,384]{2,1,0:T(8,128)(2,1)S(1)}, u32[]{:S(2)}, u32[]{:S(2)}) async-start(bf16[4,96,384]{2,1,0:T(8,128)(2,1)} %bitcast.10), calls=%async_computation.2 | async-start | bytes 589824 | tf_op jit(solution)/shard_map/all_to_all | solution.py:245
  74.7 15.7 %collective-permute-start.3 = (bf16[384,128]{1,0:T(8,128)(2,1)S(1)}, bf16[384,128]{1,0:T(8,128)(2,1)S(1)}, u32[]{:S(2)}, u32[]{:S(2)}) collective-permute-start(bf16[384,128]{1,0:T(8,128)(2,1)S(1)} %copy-done.3), channel_id=1, source_target_pairs={{0,1},{1,0},{2,3},{3,2},{4,5},{5,4},{6,7},{7,6},{10,11},{11,10},{8... | collective-permute-start | bytes 294920 | tf_op jit(solution)/shard_map/ppermute | solution.py:278
  78.6 15.3 %collective-permute-start.4 = (bf16[384,128]{1,0:T(8,128)(2,1)S(1)}, bf16[384,128]{1,0:T(8,128)(2,1)S(1)}, u32[]{:S(2)}, u32[]{:S(2)}) collective-permute-start(bf16[384,128]{1,0:T(8,128)(2,1)S(1)} %copy-done.3), channel_id=1, source_target_pairs={{0,2},{1,3},{2,0},{3,1},{4,6},{5,7},{6,4},{7,5},{10,8},{11,9},{8,1... | collective-permute-start | bytes 294920 | tf_op jit(solution)/shard_map/ppermute | solution.py:278
  84.7 9.2 %collective-permute-start.5 = (bf16[384,128]{1,0:T(8,128)(2,1)S(1)}, bf16[384,128]{1,0:T(8,128)(2,1)S(1)}, u32[]{:S(2)}, u32[]{:S(2)}) collective-permute-start(bf16[384,128]{1,0:T(8,128)(2,1)S(1)} %copy-done.3), channel_id=1, source_target_pairs={{0,3},{1,2},{2,1},{3,0},{4,7},{5,6},{6,5},{7,4},{10,9},{11,8},{8,1... | collective-permute-start | bytes 294920 | tf_op jit(solution)/shard_map/ppermute | solution.py:278
  94.3 13.2 %collective-permute-start.6 = (bf16[48,384]{1,0:T(8,128)(2,1)S(1)}, bf16[48,384]{1,0:T(8,128)(2,1)S(1)}, u32[]{:S(2)}, u32[]{:S(2)}) collective-permute-start(bf16[48,384]{1,0:T(8,128)(2,1)S(1)} %get-tuple-element.35), channel_id=1, source_target_pairs={{0,4},{4,0},{10,14},{14,10},{1,5},{5,1},{11,15},{15,11},{2,6},{6,2... | collective-permute-start | bytes 110600 | tf_op jit(solution)/shard_map/ppermute | solution.py:278
  101.6 10.8 %collective-permute-start.7 = (bf16[48,384]{1,0:T(8,128)(2,1)S(1)}, bf16[48,384]{1,0:T(8,128)(2,1)S(1)}, u32[]{:S(2)}, u32[]{:S(2)}) collective-permute-start(bf16[48,384]{1,0:T(8,128)(2,1)S(1)} %get-tuple-element.36), channel_id=1, source_target_pairs={{0,10},{4,14},{10,0},{14,4},{1,11},{5,15},{11,1},{15,5},{2,8},{6,1... | collective-permute-start | bytes 110600 | tf_op jit(solution)/shard_map/ppermute | solution.py:278
  105.0 7.4 %collective-permute-start.8 = (bf16[48,384]{1,0:T(8,128)(2,1)S(1)}, bf16[48,384]{1,0:T(8,128)(2,1)S(1)}, u32[]{:S(2)}, u32[]{:S(2)}) collective-permute-start(bf16[48,384]{1,0:T(8,128)(2,1)S(1)} %get-tuple-element.37), channel_id=1, source_target_pairs={{0,14},{4,10},{10,4},{14,0},{1,15},{5,11},{11,5},{15,1},{2,12},{6,... | collective-permute-start | bytes 110600 | tf_op jit(solution)/shard_map/ppermute | solution.py:278
  162.0 24.0 %all-to-all-start.5 = ((bf16[64,8,128]{2,1,0:T(8,128)(2,1)}), bf16[64,8,128]{2,1,0:T(8,128)(2,1)S(1)}, u32[]{:S(2)}, u32[]{:S(2)}) async-start(bf16[64,8,128]{2,1,0:T(8,128)(2,1)} %bitcast.16), calls=%async_computation.5 | async-start | bytes 262144 | tf_op jit(solution)/shard_map/all_to_all | solution.py:245
  169.8 9.6 %collective-permute-start.9 = (bf16[576,128]{1,0:T(8,128)(2,1)S(1)}, bf16[576,128]{1,0:T(8,128)(2,1)S(1)}, u32[]{:S(2)}, u32[]{:S(2)}) collective-permute-start(bf16[576,128]{1,0:T(8,128)(2,1)S(1)} %get-tuple-element.41), channel_id=1, source_target_pairs={{0,1},{1,0},{2,3},{3,2},{4,5},{5,4},{6,7},{7,6},{10,11},{11,10},{8... | collective-permute-start | bytes 442376 | tf_op jit(solution)/shard_map/ppermute | solution.py:278
  172.0 9.7 %collective-permute-start.10 = (bf16[576,128]{1,0:T(8,128)(2,1)S(1)}, bf16[576,128]{1,0:T(8,128)(2,1)S(1)}, u32[]{:S(2)}, u32[]{:S(2)}) collective-permute-start(bf16[576,128]{1,0:T(8,128)(2,1)S(1)} %get-tuple-element.42), channel_id=1, source_target_pairs={{0,2},{1,3},{2,0},{3,1},{4,6},{5,7},{6,4},{7,5},{10,8},{11,9},{8,1... | collective-permute-start | bytes 442376 | tf_op jit(solution)/shard_map/ppermute | solution.py:278
  174.5 10.2 %collective-permute-start.11 = (bf16[576,128]{1,0:T(8,128)(2,1)S(1)}, bf16[576,128]{1,0:T(8,128)(2,1)S(1)}, u32[]{:S(2)}, u32[]{:S(2)}) collective-permute-start(bf16[576,128]{1,0:T(8,128)(2,1)S(1)} %get-tuple-element.43), channel_id=1, source_target_pairs={{0,3},{1,2},{2,1},{3,0},{4,7},{5,6},{6,5},{7,4},{10,9},{11,8},{8,1... | collective-permute-start | bytes 442376 | tf_op jit(solution)/shard_map/ppermute | solution.py:278
  184.7 1.3 copy-start.4

commit v8 on v6

--- a/solution.py
+++ b/solution.py
@@ -73,60 +73,47 @@
             chunk_ref[m * piece : (m + 1) * piece, :] = held_ref[pl.ds(at, piece), :]
 
 
-def spread_kernel(cap, local, recv_ref, out_ref, scaled_ref):
+def spread_kernel(cap, local, recv_ref, out_ref):
     padded = recv_ref.shape[0]
-    slots, width = scaled_ref.shape
+    width = out_ref.shape[1]
+    slots = padded // PAD * cap
     s, r = iota((slots, padded), 0), iota((slots, padded), 1)
     keep = one_hot(((r >> 3) * cap + (r & 7) == s) & ((r & 7) < cap))
     rows = mm(keep, recv_ref[...], 1, 0).astype(BF16)
     for p in range(local):
-        out_ref[p * slots : (p + 1) * slots, :] = rows[:, :width]
-    scaled_ref[...] = rows[:, width:]
-
-
-def rows_of(held_ref, me_ref, k, slots):
-    return held_ref[pl.ds(pl.multiple_of(((me_ref[0] & 15) ^ k) * slots, 16), slots), :]
-
-
-def partial_kernel(slots, strided, me_ref, held_ref, *refs):
+        at = p * 2 * slots
+        out_ref[at : at + slots, :] = rows[:, :width]
+        out_ref[at + slots : at + 2 * slots, :] = rows[:, width:]
+
+
+def rows_of(held_ref, near_ref, k, slots, scaled):
+    at = pl.multiple_of(((near_ref[0] & 15) ^ k) * (2 * slots) + slots * scaled, 16)
+    return held_ref[pl.ds(at, slots), :]
+
+
+def partial_kernel(slots, strided, near_ref, held_ref, *refs):
     *weight_refs, part_ref = refs
     piece = weight_refs[0].shape[0] // 3
     chunk = piece // strided
-    for m in range(2):
+    for m in range(3):
         total = None
         for k, weight_ref in enumerate(weight_refs):
-            rows = rows_of(held_ref, me_ref, k, slots)
+            rows = rows_of(held_ref, near_ref, k, slots, m // 2)
             term = mm(weight_ref[m * piece : (m + 1) * piece, :], rows, 1, 1)
             total = term if total is None else total + term
         total = total.astype(BF16)
         for q in range(strided):
-            to = (q * 2 + m) * chunk
+            to = (q * 3 + m) * chunk
             part_ref[to : to + chunk, :] = total[q * chunk : (q + 1) * chunk, :]
 
 
-def upstream_kernel(n, me_ref, *refs):
-    scaled_refs, weight_refs, chunk_refs, held_ref = refs[:n], refs[n : 2 * n], refs[2 * n : -1], refs[-1]
-    piece = weight_refs[0].shape[0] // 3
-    chunk = chunk_refs[0].shape[0]
-    total = None
-    for scaled_ref, weight_ref in zip(scaled_refs, weight_refs):
-        term = mm(weight_ref[2 * piece :, :], scaled_ref[...], 1, 1)
-        total = term if total is None else total + term
-    held_ref[...] = total.astype(BF16)
-    for k, chunk_ref in enumerate(chunk_refs):
-        at = pl.multiple_of(((me_ref[0] >> 4) ^ k) * chunk, 16)
-        chunk_ref[...] = held_ref[pl.ds(at, chunk), :]
-
-
-def act_kernel(strided, part_ref, *refs):
-    *back_refs, out_ref, act_ref = refs
+def act_kernel(strided, part_ref, out_ref, act_ref):
     n = part_ref.shape[0] // strided
-    chunk = n // 2
+    chunk = n // 3
     total = part_ref[0:n, :].astype(F32)
     for q in range(1, strided):
         total = total + part_ref[q * n : (q + 1) * n, :].astype(F32)
-    gate, up = total[:chunk, :], total[chunk:, :]
-    back = functools.reduce(jnp.add, [ref[...].astype(F32) for ref in back_refs])
+    gate, up, back = (total[m * chunk : (m + 1) * chunk, :] for m in range(3))
     sig = jax.nn.sigmoid(gate)
     silu = gate * sig
     act = (silu * up).astype(BF16)
@@ -139,8 +126,8 @@
     for q in range(strided):
         at = q * m
         out_ref[at : at + chunk, :] = grad_g
-        out_ref[at + chunk : at + n, :] = grad_u
-        out_ref[at + n : at + m, :] = score
+        out_ref[at + chunk : at + 2 * chunk, :] = grad_u
+        out_ref[at + 2 * chunk : at + m, :] = score
 
 
 def pair_of(pair_ref, strided):
@@ -177,9 +164,8 @@
         out_ref[pl.ds(to + slots, PAD), :] = score
 
 
-def grad_kernel(strided, local, me_ref, held_ref, pair_ref, *refs):
-    act_refs, scaled_refs = refs[:strided], refs[strided : strided + local]
-    out_refs, act_ref = refs[strided + local : -1], refs[-1]
+def grad_kernel(strided, me_ref, held_ref, pair_ref, *refs):
+    act_refs, out_refs, act_ref = refs[:strided], refs[strided:-1], refs[-1]
     slots = pair_ref.shape[1]
     piece = out_refs[0].shape[0] // 3
     chunk = piece // strided
@@ -187,10 +173,11 @@
     for k, ref in enumerate(act_refs):
         act_ref[pl.ds(pl.multiple_of(((me_ref[0] >> 4) ^ k) * chunk, 16), chunk), :] = ref[...]
     for k, out_ref in enumerate(out_refs):
-        feat = rows_of(held_ref, me_ref, k, slots)
+        feat = rows_of(held_ref, me_ref, k, slots, 0)
+        scaled = rows_of(held_ref, me_ref, k, slots, 1)
         out_ref[0:piece, :] = mm(grad_g, feat, 1, 0).astype(BF16)
         out_ref[piece : 2 * piece, :] = mm(grad_u, feat, 1, 0).astype(BF16)
-        out_ref[2 * piece : 3 * piece, :] = mm(act_ref[...], scaled_refs[k][...], 1, 0).astype(BF16)
+        out_ref[2 * piece : 3 * piece, :] = mm(act_ref[...], scaled, 1, 0).astype(BF16)
 
 
 def back_kernel(cap, slots, local, got_ref, send_ref):
@@ -353,32 +340,23 @@
     )
     chunks = swap(chunks, near)
     chunk = piece // strided
-    held, scaled = call(
+    held = call(
         functools.partial(spread_kernel, cap, local),
         (recv,),
-        out_shape=(shape_of(local * slots, width), shape_of(slots, width)),
+        out_shape=shape_of(local * 2 * slots, width),
         name="spread",
     )
     held = exchange(held, "attn", near)
-    scaled = swap([scaled] * local, near)
     part = call(
         functools.partial(partial_kernel, slots, strided),
         (me, held, *chunks),
-        out_shape=shape_of(2 * piece, slots),
+        out_shape=shape_of(3 * piece, slots),
         name="partial",
     )
     part = exchange(part, "attn", far)
-    backs = call(
-        functools.partial(upstream_kernel, local),
-        (me, *scaled, *chunks),
-        out_shape=(shape_of(chunk, slots),) * strided,
-        scratch_shapes=[pltpu.VMEM((piece, slots), BF16)],
-        name="upstream",
-    )
-    backs = swap(backs, far)
     pair, act = call(
         functools.partial(act_kernel, strided),
-        (part, *backs),
+        (part,),
         out_shape=(shape_of(2 * piece + strided * PAD, slots), shape_of(chunk, slots)),
         name="acts",
     )
@@ -392,8 +370,8 @@
     )
     terms = exchange(terms, "attn", near)
     got = call(
-        functools.partial(grad_kernel, strided, local),
-        (me, held, pair, *act, *scaled),
+        functools.partial(grad_kernel, strided),
+        (me, held, pair, *act),
         out_shape=(shape_of(3 * piece, width),) * local,
         scratch_shapes=[pltpu.VMEM((piece, slots), BF16)],
         name="grads",

time: 205 us -> 186 us (0.907)
  starting transfers between devices: 80.2 us -> 48.9 us
  blocking collectives: 73.8 us -> 96.2 us
  waiting for transfers between devices: 31.6 us -> 22.9 us
    ppermute x15 -> x9, starting transfers between devices: 58.2 us -> 32.7 us  [swap(): out.append(lax.ppermute(chunks[k], ('exp', 'attn'), pairs))]
    all_to_all x3 -> x4, blocking collectives: 73.8 us -> 96.2 us  [exchange(): lax.all_to_all(blocks, axis, split_axis=0, concat_axis=0, tiled=True, axi...]
    ppermute x15 -> x9, waiting for transfers between devices: 31.6 us -> 22.9 us  [swap(): out.append(lax.ppermute(chunks[k], ('exp', 'attn'), pairs))]
    all_to_all x3 -> x2, starting transfers between devices: 22 us -> 16.2 us  [exchange(): lax.all_to_all(blocks, axis, split_axis=0, concat_axis=0, tiled=True, axi...]
    pallas_call x9 -> x8, Pallas kernels: 9.35 us -> 8.89 us  [call(): pl.pallas_call(kernel, in_specs=specs, compiler_params=params, **options)]
  transfers between devices with their start and end apart: 18 -> 11, of which waited for: 9 -> 6; matrix products, arithmetic and copies ran while one was open for 0% -> 0% of each run, Pallas kernels for 3% -> 3%
where the time goes in v8:
time: 186 us; the launch traced here: 183 us
  blocking collectives  96.2 us (52%)
  starting transfers between devices  48.9 us (26%)
  waiting for transfers between devices  22.9 us (12%)
  Pallas kernels  13.1 us (7%)
    all_to_all x4, blocking collectives, exchange(): lax.all_to_all(blocks, axis, split_axis=0, concat_axis=0, tiled=True, axi...  96.2 us
    ppermute x9, starting transfers between devices, swap(): out.append(lax.ppermute(chunks[k], ('exp', 'attn'), pairs))  32.7 us
    ppermute x9, waiting for transfers between devices, swap(): out.append(lax.ppermute(chunks[k], ('exp', 'attn'), pairs))  22.9 us
    all_to_all x2, starting transfers between devices, exchange(): lax.all_to_all(blocks, axis, split_axis=0, concat_axis=0, tiled=True, axi...  16.2 us
    pallas_call x8, Pallas kernels, call(): pl.pallas_call(kernel, in_specs=specs, compiler_params=params, **options)  8.89 us
    pallas_call x2, Pallas kernels, call_fetching(): pl.pallas_call(body, in_specs=[pl.BlockSpec(memory_space=x) for x in spac...  4.19 us
  transfers between devices with their start and end apart: 11, of which 6 were waited for; matrix products, arithmetic and copies ran while one was open for 0% of the time, Pallas kernels for 3%

profile of v8, /device:TPU:1, one launch (start us, length us, event | category | flops | bytes accessed | tf_op | source)
XLA Modules:
  0.0 182.8 jit_solution(12242507151290695453)
XLA Ops:
  0.6 1.9 %pack.1 = (bf16[512,256]{1,0:T(8,128)(2,1)}, f32[6,128]{1,0:T(8,128)}) custom-call(s32[2,128]{1,0:T(2,128)} %bitcast.35, bf16[2,128]{1,0:T(2,128)(2,1)} %bitcast.36, bf16[128,128]{1,0:T(8,128)(2,1)} %refs_2_.1, bf16[128,128]{1,0:T(8,128)(2,1)} %refs_3_.1), custom_call_target="tpu_custom_call" | custom-call | tf_op jit(solution)/shard_map/pack/pallas_call | solution.py:295
  2.6 31.4 %all_to_all.30 = bf16[64,8,256]{2,1,0:T(8,128)(2,1)S(1)} all-to-all(bf16[64,8,256]{2,1,0:T(8,128)(2,1)} %bitcast.31), channel_id=1, replica_groups=mesh['exp'=64,'attn'=16] {'exp'}, dimensions={0} | all-to-all | bytes 524288 | tf_op jit(solution)/shard_map/all_to_all | solution.py:236
  33.9 1.2 spread.1
  35.1 10.6 %all-to-all-start.1 = ((bf16[4,768,128]{2,1,0:T(8,128)(2,1)}), bf16[4,768,128]{2,1,0:T(8,128)(2,1)}, u32[]{:S(2)}, u32[]{:S(2)}) async-start(bf16[4,768,128]{2,1,0:T(8,128)(2,1)} %bitcast.5), calls=%async_computation.1 | async-start | bytes 1572864 | tf_op jit(solution)/shard_map/all_to_all | solution.py:236
  45.7 2.3 %turn.1 = (bf16[576,128]{1,0:T(8,128)(2,1)}, bf16[576,128]{1,0:T(8,128)(2,1)}, bf16[576,128]{1,0:T(8,128)(2,1)}, bf16[576,128]{1,0:T(8,128)(2,1)}) custom-call(s32[1]{0:T(128)} %bitcast.2.refs_0_.near_ref.me_ref, bf16[128,768]{1,0:T(8,128)(2,1)} %bitcast.32, bf16[128,768]{1,0:T(8,128)(2,1)} %bitcast.33, bf16[768,128]{1,0:T(8,128)(2,1)} %bitcast.34), custom_call_target="tpu_custom_call" | custom-call | tf_op jit(solution)/shard_map/turn/pallas_call | solution.py:295
  48.0 3.4 %collective-permute-start = (bf16[576,128]{1,0:T(8,128)(2,1)}, bf16[576,128]{1,0:T(8,128)(2,1)S(1)}, u32[]{:S(2)}, u32[]{:S(2)}) collective-permute-start(bf16[576,128]{1,0:T(8,128)(2,1)} %get-tuple-element.25), channel_id=1, source_target_pairs={{0,1},{1,0},{2,3},{3,2},{4,5},{5,4},{6,7},{7,6},{10,11},{11,10},{8... | collective-permute-start | bytes 442376 | tf_op jit(solution)/shard_map/ppermute | solution.py:269
  51.4 4.6 %collective-permute-start.1 = (bf16[576,128]{1,0:T(8,128)(2,1)}, bf16[576,128]{1,0:T(8,128)(2,1)S(1)}, u32[]{:S(2)}, u32[]{:S(2)}) collective-permute-start(bf16[576,128]{1,0:T(8,128)(2,1)} %get-tuple-element.26), channel_id=1, source_target_pairs={{0,2},{1,3},{2,0},{3,1},{4,6},{5,7},{6,4},{7,5},{10,8},{11,9},{8,1... | collective-permute-start | bytes 442376 | tf_op jit(solution)/shard_map/ppermute | solution.py:269
  56.0 1.9 %collective-permute-start.2 = (bf16[576,128]{1,0:T(8,128)(2,1)}, bf16[576,128]{1,0:T(8,128)(2,1)S(1)}, u32[]{:S(2)}, u32[]{:S(2)}) collective-permute-start(bf16[576,128]{1,0:T(8,128)(2,1)} %get-tuple-element.27), channel_id=1, source_target_pairs={{0,3},{1,2},{2,1},{3,0},{4,7},{5,6},{6,5},{7,4},{10,9},{11,8},{8,1... | collective-permute-start | bytes 442376 | tf_op jit(solution)/shard_map/ppermute | solution.py:269
  57.9 3.0 %collective-permute-done.refs_1_ = bf16[576,128]{1,0:T(8,128)(2,1)S(1)} collective-permute-done((bf16[576,128]{1,0:T(8,128)(2,1)}, bf16[576,128]{1,0:T(8,128)(2,1)S(1)}, u32[]{:S(2)}, u32[]{:S(2)}) %collective-permute-start) | collective-permute-done | bytes 147488 | tf_op jit(solution)/shard_map/ppermute | solution.py:269
  60.9 8.2 %collective-permute-done.1.refs_2_ = bf16[576,128]{1,0:T(8,128)(2,1)S(1)} collective-permute-done((bf16[576,128]{1,0:T(8,128)(2,1)}, bf16[576,128]{1,0:T(8,128)(2,1)S(1)}, u32[]{:S(2)}, u32[]{:S(2)}) %collective-permute-start.1) | collective-permute-done | bytes 147488 | tf_op jit(solution)/shard_map/ppermute | solution.py:269
  69.2 0.9 copy-done
  70.1 1.8 partial.1
  71.9 29.3 %all_to_all.31 = bf16[4,144,384]{2,1,0:T(8,128)(2,1)S(1)} all-to-all(bf16[4,144,384]{2,1,0:T(8,128)(2,1)S(1)} %bitcast.25), channel_id=1, replica_groups={{0,4,10,14},{1,5,11,15},{2,6,8,12},{3,7,9,13},{18,22,28,16},{19,23,29,1..., dimensions={0} | all-to-all | bytes 884736 | tf_op jit(solution)/shard_map/all_to_all | solution.py:236
  101.2 0.1 acts.1
  101.3 17.1 %all_to_all.32 = bf16[4,104,384]{2,1,0:T(8,128)(2,1)S(1)} all-to-all(bf16[4,104,384]{2,1,0:T(8,128)(2,1)S(1)} %bitcast.30), channel_id=1, replica_groups={{0,4,10,14},{1,5,11,15},{2,6,8,12},{3,7,9,13},{18,22,28,16},{19,23,29,1..., dimensions={0} | all-to-all | bytes 638976 | tf_op jit(solution)/shard_map/all_to_all | solution.py:236
  118.4 0.6 terms.1
  119.0 18.5 %all_to_all.33 = bf16[4,392,128]{2,1,0:T(8,128)(2,1)S(1)} all-to-all(bf16[4,392,128]{2,1,0:T(8,128)(2,1)S(1)} %bitcast.26), channel_id=1, replica_groups={{0,1,2,3},{4,5,6,7},{10,11,8,9},{14,15,12,13},{18,19,20,21},{22,23,24,2..., dimensions={0} | all-to-all | bytes 802816 | tf_op jit(solution)/shard_map/all_to_all | solution.py:236
  137.5 1.2 back.1
  138.7 5.6 %all-to-all-start.5 = ((bf16[64,8,128]{2,1,0:T(8,128)(2,1)}), bf16[64,8,128]{2,1,0:T(8,128)(2,1)S(1)}, u32[]{:S(2)}, u32[]{:S(2)}) async-start(bf16[64,8,128]{2,1,0:T(8,128)(2,1)} %bitcast.16), calls=%async_computation.5 | async-start | bytes 262144 | tf_op jit(solution)/shard_map/all_to_all | solution.py:236
  144.2 3.5 %collective-permute-start.5 = (bf16[48,384]{1,0:T(8,128)(2,1)S(1)}, bf16[48,384]{1,0:T(8,128)(2,1)S(1)}, u32[]{:S(2)}, u32[]{:S(2)}) collective-permute-start(bf16[48,384]{1,0:T(8,128)(2,1)S(1)} %get-tuple-element.31.refs_0_), channel_id=1, source_target_pairs={{0,14},{4,10},{10,4},{14,0},{1,15},{5,11},{11,5},{15,1},{2,12},{6,... | collective-permute-start | bytes 110600 | tf_op jit(solution)/shard_map/ppermute | solution.py:269
  147.8 7.3 %collective-permute-start.4 = (bf16[48,384]{1,0:T(8,128)(2,1)S(1)}, bf16[48,384]{1,0:T(8,128)(2,1)S(1)}, u32[]{:S(2)}, u32[]{:S(2)}) collective-permute-start(bf16[48,384]{1,0:T(8,128)(2,1)S(1)} %get-tuple-element.31.refs_0_), channel_id=1, source_target_pairs={{0,10},{4,14},{10,0},{14,4},{1,11},{5,15},{11,1},{15,5},{2,8},{6,1... | collective-permute-start | bytes 110600 | tf_op jit(solution)/shard_map/ppermute | solution.py:269
  155.1 2.4 %collective-permute-start.3 = (bf16[48,384]{1,0:T(8,128)(2,1)S(1)}, bf16[48,384]{1,0:T(8,128)(2,1)S(1)}, u32[]{:S(2)}, u32[]{:S(2)}) collective-permute-start(bf16[48,384]{1,0:T(8,128)(2,1)S(1)} %get-tuple-element.31.refs_0_), channel_id=1, source_target_pairs={{0,4},{4,0},{10,14},{14,10},{1,5},{5,1},{11,15},{15,11},{2,6},{6,2... | collective-permute-start | bytes 110600 | tf_op jit(solution)/shard_map/ppermute | solution.py:269
  157.5 1.3 collective-permute-done.4.refs_2_
  158.7 5.0 %collective-permute-done.3.refs_1_ = bf16[48,384]{1,0:T(8,128)(2,1)S(1)} collective-permute-done((bf16[48,384]{1,0:T(8,128)(2,1)S(1)}, bf16[48,384]{1,0:T(8,128)(2,1)S(1)}, u32[]{:S(2)}, u32[]{:S(2)}) %collective-permute-start.3) | collective-permute-done | bytes 36896 | tf_op jit(solution)/shard_map/ppermute | solution.py:269
  163.7 1.8 grads.1
  165.5 2.5 %collective-permute-start.6 = (bf16[576,128]{1,0:T(8,128)(2,1)S(1)}, bf16[576,128]{1,0:T(8,128)(2,1)S(1)}, u32[]{:S(2)}, u32[]{:S(2)}) collective-permute-start(bf16[576,128]{1,0:T(8,128)(2,1)S(1)} %get-tuple-element.33), channel_id=1, source_target_pairs={{0,1},{1,0},{2,3},{3,2},{4,5},{5,4},{6,7},{7,6},{10,11},{11,10},{8... | collective-permute-start | bytes 442376 | tf_op jit(solution)/shard_map/ppermute | solution.py:269
  168.0 2.0 %collective-permute-start.7 = (bf16[576,128]{1,0:T(8,128)(2,1)S(1)}, bf16[576,128]{1,0:T(8,128)(2,1)S(1)}, u32[]{:S(2)}, u32[]{:S(2)}) collective-permute-start(bf16[576,128]{1,0:T(8,128)(2,1)S(1)} %get-tuple-element.34), channel_id=1, source_target_pairs={{0,2},{1,3},{2,0},{3,1},{4,6},{5,7},{6,4},{7,5},{10,8},{11,9},{8,1... | collective-permute-start | bytes 442376 | tf_op jit(solution)/shard_map/ppermute | solution.py:269
  170.0 5.1 %collective-permute-start.8 = (bf16[576,128]{1,0:T(8,128)(2,1)S(1)}, bf16[576,128]{1,0:T(8,128)(2,1)S(1)}, u32[]{:S(2)}, u32[]{:S(2)}) collective-permute-start(bf16[576,128]{1,0:T(8,128)(2,1)S(1)} %get-tuple-element.35), channel_id=1, source_target_pairs={{0,3},{1,2},{2,1},{3,0},{4,7},{5,6},{6,5},{7,4},{10,9},{11,8},{8,1... | collective-permute-start | bytes 442376 | tf_op jit(solution)/shard_map/ppermute | solution.py:269
  175.1 2.1 %collective-permute-done.7.refs_2_ = bf16[576,128]{1,0:T(8,128)(2,1)S(1)} collective-permute-done((bf16[576,128]{1,0:T(8,128)(2,1)S(1)}, bf16[576,128]{1,0:T(8,128)(2,1)S(1)}, u32[]{:S(2)}, u32[]{:S(2)}) %collective-permute-start.7) | collective-permute-done | bytes 147488 | tf_op jit(solution)/shard_map/ppermute | solution.py:269
  177.2 3.3 %collective-permute-done.8.refs_3_ = bf16[576,128]{1,0:T(8,128)(2,1)S(1)} collective-permute-done((bf16[576,128]{1,0:T(8,128)(2,1)S(1)}, bf16[576,128]{1,0:T(8,128)(2,1)S(1)}, u32[]{:S(2)}, u32[]{:S(2)}) %collective-permute-start.8) | collective-permute-done | bytes 147488 | tf_op jit(solution)/shard_map/ppermute | solution.py:269
  180.5 1.3 out.1
  181.8 0.9 merge.1
  (10 shorter events, 0.0 us)
Async XLA Ops:
  35.1 34.1 %all-to-all-start.1 = ((bf16[4,768,128]{2,1,0:T(8,128)(2,1)}), bf16[4,768,128]{2,1,0:T(8,128)(2,1)}, u32[]{:S(2)}, u32[]{:S(2)}) async-start(bf16[4,768,128]{2,1,0:T(8,128)(2,1)} %bitcast.5), calls=%async_computation.1 | async-start | bytes 1572864 | tf_op jit(solution)/shard_map/all_to_all | solution.py:236
  48.0 12.9 %collective-permute-start = (bf16[576,128]{1,0:T(8,128)(2,1)}, bf16[576,128]{1,0:T(8,128)(2,1)S(1)}, u32[]{:S(2)}, u32[]{:S(2)}) collective-permute-start(bf16[576,128]{1,0:T(8,128)(2,1)} %get-tuple-element.25), channel_id=1, source_target_pairs={{0,1},{1,0},{2,3},{3,2},{4,5},{5,4},{6,7},{7,6},{10,11},{11,10},{8... | collective-permute-start | bytes 442376 | tf_op jit(solution)/shard_map/ppermute | solution.py:269
  51.4 17.8 %collective-permute-start.1 = (bf16[576,128]{1,0:T(8,128)(2,1)}, bf16[576,128]{1,0:T(8,128)(2,1)S(1)}, u32[]{:S(2)}, u32[]{:S(2)}) collective-permute-start(bf16[576,128]{1,0:T(8,128)(2,1)} %get-tuple-element.26), channel_id=1, source_target_pairs={{0,2},{1,3},{2,0},{3,1},{4,6},{5,7},{6,4},{7,5},{10,8},{11,9},{8,1... | collective-permute-start | bytes 442376 | tf_op jit(solution)/shard_map/ppermute | solution.py:269
  56.0 13.2 %collective-permute-start.2 = (bf16[576,128]{1,0:T(8,128)(2,1)}, bf16[576,128]{1,0:T(8,128)(2,1)S(1)}, u32[]{:S(2)}, u32[]{:S(2)}) collective-permute-start(bf16[576,128]{1,0:T(8,128)(2,1)} %get-tuple-element.27), channel_id=1, source_target_pairs={{0,3},{1,2},{2,1},{3,0},{4,7},{5,6},{6,5},{7,4},{10,9},{11,8},{8,1... | collective-permute-start | bytes 442376 | tf_op jit(solution)/shard_map/ppermute | solution.py:269
  69.2 0.9 copy-start
  101.3 17.1 %copy-start.1 = (bf16[576,128]{1,0:T(8,128)(2,1)S(1)}, bf16[576,128]{1,0:T(8,128)(2,1)}, u32[]{:S(2)}) copy-start(bf16[576,128]{1,0:T(8,128)(2,1)} %get-tuple-element.24.refs_0_) | copy-start | bytes 442372
  138.7 43.2 %all-to-all-start.5 = ((bf16[64,8,128]{2,1,0:T(8,128)(2,1)}), bf16[64,8,128]{2,1,0:T(8,128)(2,1)S(1)}, u32[]{:S(2)}, u32[]{:S(2)}) async-start(bf16[64,8,128]{2,1,0:T(8,128)(2,1)} %bitcast.16), calls=%async_computation.5 | async-start | bytes 262144 | tf_op jit(solution)/shard_map/all_to_all | solution.py:236
  144.2 13.2 %collective-permute-start.5 = (bf16[48,384]{1,0:T(8,128)(2,1)S(1)}, bf16[48,384]{1,0:T(8,128)(2,1)S(1)}, u32[]{:S(2)}, u32[]{:S(2)}) collective-permute-start(bf16[48,384]{1,0:T(8,128)(2,1)S(1)} %get-tuple-element.31.refs_0_), channel_id=1, source_target_pairs={{0,14},{4,10},{10,4},{14,0},{1,15},{5,11},{11,5},{15,1},{2,12},{6,... | collective-permute-start | bytes 110600 | tf_op jit(solution)/shard_map/ppermute | solution.py:269
  147.8 11.0 %collective-permute-start.4 = (bf16[48,384]{1,0:T(8,128)(2,1)S(1)}, bf16[48,384]{1,0:T(8,128)(2,1)S(1)}, u32[]{:S(2)}, u32[]{:S(2)}) collective-permute-start(bf16[48,384]{1,0:T(8,128)(2,1)S(1)} %get-tuple-element.31.refs_0_), channel_id=1, source_target_pairs={{0,10},{4,14},{10,0},{14,4},{1,11},{5,15},{11,1},{15,5},{2,8},{6,1... | collective-permute-start | bytes 110600 | tf_op jit(solution)/shard_map/ppermute | solution.py:269
  155.1 8.6 %collective-permute-start.3 = (bf16[48,384]{1,0:T(8,128)(2,1)S(1)}, bf16[48,384]{1,0:T(8,128)(2,1)S(1)}, u32[]{:S(2)}, u32[]{:S(2)}) collective-permute-start(bf16[48,384]{1,0:T(8,128)(2,1)S(1)} %get-tuple-element.31.refs_0_), channel_id=1, source_target_pairs={{0,4},{4,0},{10,14},{14,10},{1,5},{5,1},{11,15},{15,11},{2,6},{6,2... | collective-permute-start | bytes 110600 | tf_op jit(solution)/shard_map/ppermute | solution.py:269
  165.5 9.6 %collective-permute-start.6 = (bf16[576,128]{1,0:T(8,128)(2,1)S(1)}, bf16[576,128]{1,0:T(8,128)(2,1)S(1)}, u32[]{:S(2)}, u32[]{:S(2)}) collective-permute-start(bf16[576,128]{1,0:T(8,128)(2,1)S(1)} %get-tuple-element.33), channel_id=1, source_target_pairs={{0,1},{1,0},{2,3},{3,2},{4,5},{5,4},{6,7},{7,6},{10,11},{11,10},{8... | collective-permute-start | bytes 442376 | tf_op jit(solution)/shard_map/ppermute | solution.py:269
  168.0 9.2 %collective-permute-start.7 = (bf16[576,128]{1,0:T(8,128)(2,1)S(1)}, bf16[576,128]{1,0:T(8,128)(2,1)S(1)}, u32[]{:S(2)}, u32[]{:S(2)}) collective-permute-start(bf16[576,128]{1,0:T(8,128)(2,1)S(1)} %get-tuple-element.34), channel_id=1, source_target_pairs={{0,2},{1,3},{2,0},{3,1},{4,6},{5,7},{6,4},{7,5},{10,8},{11,9},{8,1... | collective-permute-start | bytes 442376 | tf_op jit(solution)/shard_map/ppermute | solution.py:269
  170.0 10.6 %collective-permute-start.8 = (bf16[576,128]{1,0:T(8,128)(2,1)S(1)}, bf16[576,128]{1,0:T(8,128)(2,1)S(1)}, u32[]{:S(2)}, u32[]{:S(2)}) collective-permute-start(bf16[576,128]{1,0:T(8,128)(2,1)S(1)} %get-tuple-element.35), channel_id=1, source_target_pairs={{0,3},{1,2},{2,1},{3,0},{4,7},{5,6},{6,5},{7,4},{10,9},{11,8},{8,1... | collective-permute-start | bytes 442376 | tf_op jit(solution)/shard_map/ppermute | solution.py:269
  180.5 1.3 copy-start.2
